TPU v7x, 32 devices: a whole 2x2x4 slice. The times are simulated.
32 devices in a mesh: dp: 4 (over z), ctx: 2 (over y), seq: 4 (over x, core).
Axes of the slice: x: 2, y: 2, z: 4, core: 2. Of those that a mesh axis runs over, the one named last changes fastest.
Arguments:
- tokens: bfloat16 [4096, 2048], P(('dp', 'ctx', 'seq')), may hold values from -6 to 6
- w_query: bfloat16 [2048, 2048], P(None, 'seq'), may hold values from -1 to 1, as said below
- w_key: bfloat16 [2048, 2048], P(None, 'seq'), may hold values from -1 to 1, as said below
- w_value: bfloat16 [2048, 2048], P(None, 'seq'), may hold values from -0.125 to 0.125
- gain_query: float32 [2048], P('seq'), may hold values from 1 to 2
- gain_key: float32 [2048], P('seq'), may hold values from 1 to 2
- w_out: bfloat16 [2048, 2048], P('seq'), may hold values from -0.125 to 0.125
- gain_attn: float32 [2048], replicated, may hold values from 0.5 to 1.5
- w_gate: bfloat16 [2048, 8192], P(None, 'seq'), may hold values from -0.125 to 0.125
- w_up: bfloat16 [2048, 8192], P(None, 'seq'), may hold values from -0.125 to 0.125
- w_down: bfloat16 [8192, 2048], P('seq'), may hold values from -0.0625 to 0.0625
- gain_ffn: float32 [2048], replicated, may hold values from 0.5 to 1.5
- cotangent: bfloat16 [4096, 2048], P(('dp', 'ctx', 'seq')), may hold values from -6 to 6
- source_ids: int32 [4], P('dp'), may hold values from 0 to 7
- group_weights: float32 [8], replicated, may hold values from 0.5 to 2
Outputs:
- out_tokens: bfloat16 [4096, 2048], P(('dp', 'ctx', 'seq'))
- grad_tokens: float32 [4096, 2048], P(('dp', 'ctx', 'seq'))
- grad_w_query: float32 [2048, 2048], P(None, 'seq')
- grad_w_key: float32 [2048, 2048], P(None, 'seq')
- grad_w_value: float32 [2048, 2048], P(None, 'seq')
- grad_gain_query: float32 [2048], P('seq')
- grad_gain_key: float32 [2048], P('seq')
- grad_w_out: float32 [2048, 2048], P('seq')
- grad_gain_attn: float32 [2048], replicated
- grad_w_gate: float32 [2048, 8192], P(None, 'seq')
- grad_w_up: float32 [2048, 8192], P(None, 'seq')
- grad_w_down: float32 [8192, 2048], P('seq')
- grad_gain_ffn: float32 [2048], replicated
Inputs may be any that keep to these rules, and one draw needn't show every extreme that they name: `w_query`: entries of order one over the square root of 2048. `w_key`: entries of order one over the square root of 2048.
All inputs are finite; a program needn't handle non-finite values.
Results may differ from a plain program's by a relative error of at most 0.025.
Values may be sent and summed in bfloat16 or wider, within the bound.
No kernel may reach another device: no remote copies, remote signals or barrier semaphores. Data moves between devices by JAX's collectives and lax.ppermute only.
A program may use at most 256 MiB of HBM per device.

v0:
```python
import jax
import jax.numpy as jnp
from jax import lax
from jax.sharding import PartitionSpec as P

D = 2048
HD = 128


EPS = 1e-06
ROPE_BASE = 500000.0
NEG_FILL = -1e30


def shifted(value, axis, steps):
    count = lax.axis_size(axis)
    first, last = (max(0, -steps), min(count, count - steps))
    return lax.ppermute(value, axis, [(source, source + steps) for source in range(first, last)])


def rope_turn(values_in, cosine, sine, direction):
    half_dim = values_in.shape[-1] // 2
    first = values_in[..., :half_dim]
    second = values_in[..., half_dim:]
    return jnp.concatenate(
        [first * cosine - direction * second * sine, second * cosine + direction * first * sine],
        axis=-1,
    )


def norm_back(unit_val, inverse, grad_unit):
    return inverse * (grad_unit - unit_val * jnp.mean(grad_unit * unit_val, axis=-1, keepdims=True))


def contract_rows(left, right):
    return lax.dot_general(
        left, right, (((0,), (0,)), ((), ())), preferred_element_type=jnp.float32
    )


def times_transpose(left, right):
    return lax.dot_general(
        left, right, (((1,), (1,)), ((), ())), preferred_element_type=jnp.float32
    )


def sum_ffn(grad_parts):
    return (
        lax.psum(grad_parts[0].astype(jnp.bfloat16), ("dp", "ctx")).astype(jnp.float32),
        lax.psum(grad_parts[1].astype(jnp.bfloat16), ("dp", "ctx")).astype(jnp.float32),
        lax.psum(grad_parts[2].astype(jnp.bfloat16), ("dp", "ctx")).astype(jnp.float32),
    )


def body(
    tokens,
    w_query,
    w_key,
    w_value,
    gain_query,
    gain_key,
    w_out,
    gain_attn,
    w_gate,
    w_up,
    w_down,
    gain_ffn,
    cotangent,
    source_ids,
    group_weights,
):
    seq_count = lax.axis_size("seq")
    ctx_place = lax.axis_index("ctx")
    tok_rows = tokens.shape[0]
    half_rows = tok_rows * seq_count
    heads_here = w_query.shape[1] // HD
    head_width = heads_here * HD
    block_rows = min(512, half_rows)
    block_count = half_rows // block_rows
    score_scale = HD ** (-0.5)
    half_dim = HD // 2
    positions = (ctx_place * half_rows).astype(jnp.float32) + jnp.arange(
        half_rows, dtype=jnp.float32
    )
    inverse = ROPE_BASE ** (-(jnp.arange(half_dim, dtype=jnp.float32) * 2.0 / HD))
    angles = positions[:, None] * inverse[None, :]
    cosine = jnp.cos(angles)[:, None, :]
    sine = jnp.sin(angles)[:, None, :]
    tokens_all = lax.all_gather(tokens, "seq", axis=0, tiled=True)
    query_proj = jnp.dot(tokens_all, w_query, preferred_element_type=jnp.float32)
    key_proj = jnp.dot(tokens_all, w_key, preferred_element_type=jnp.float32)
    value_proj = jnp.dot(tokens_all, w_value, preferred_element_type=jnp.float32)
    sq_query, sq_key = lax.psum(
        (jnp.sum(query_proj * query_proj, axis=1), jnp.sum(key_proj * key_proj, axis=1)), "seq"
    )
    inv_query = lax.rsqrt(sq_query / D + EPS)[:, None]
    inv_key = lax.rsqrt(sq_key / D + EPS)[:, None]
    query_unit = query_proj * inv_query
    key_unit = key_proj * inv_key
    query_low = rope_turn(
        (query_unit * gain_query).reshape(half_rows, heads_here, HD), cosine, sine, 1.0
    ).astype(jnp.bfloat16)
    key_low = rope_turn(
        (key_unit * gain_key).reshape(half_rows, heads_here, HD), cosine, sine, 1.0
    ).astype(jnp.bfloat16)
    value_low = value_proj.reshape(half_rows, heads_here, HD).astype(jnp.bfloat16)
    key_prev, value_prev = shifted((key_low, value_low), "ctx", 1)
    has_prev = ctx_place > 0
    local_idx = jnp.arange(half_rows, dtype=jnp.int32)

    def scores_of(query_block, row_start):
        own_scores = score_scale * jnp.einsum(
            "qhd,khd->hqk", query_block, key_low, preferred_element_type=jnp.float32
        )
        prev_scores = score_scale * jnp.einsum(
            "qhd,khd->hqk", query_block, key_prev, preferred_element_type=jnp.float32
        )
        query_idx = row_start + jnp.arange(block_rows, dtype=jnp.int32)
        own_mask = local_idx[None, None, :] <= query_idx[None, :, None]
        own_scores = jnp.where(own_mask, own_scores, NEG_FILL)
        prev_scores = jnp.where(has_prev, prev_scores, NEG_FILL)
        return (own_scores, prev_scores)

    def forward_block(row_start):
        query_block = lax.dynamic_slice_in_dim(query_low, row_start, block_rows, 0)
        own_scores, prev_scores = scores_of(query_block, row_start)
        peak = jnp.maximum(jnp.max(own_scores, axis=-1), jnp.max(prev_scores, axis=-1))
        own_exp = jnp.exp(own_scores - peak[..., None])
        prev_exp = jnp.exp(prev_scores - peak[..., None])
        total_exp = jnp.sum(own_exp, axis=-1) + jnp.sum(prev_exp, axis=-1)
        log_total = peak + jnp.log(total_exp)
        own_probs = (own_exp / total_exp[..., None]).astype(jnp.bfloat16)
        prev_probs = (prev_exp / total_exp[..., None]).astype(jnp.bfloat16)
        mixed = jnp.einsum("hqk,khd->qhd", own_probs, value_low, preferred_element_type=jnp.float32)
        mixed = mixed + jnp.einsum(
            "hqk,khd->qhd", prev_probs, value_prev, preferred_element_type=jnp.float32
        )
        return (mixed, log_total)

    row_starts = jnp.arange(block_count) * block_rows
    attn_blocks, lse_blocks = lax.map(forward_block, row_starts)
    attn_low = attn_blocks.reshape(half_rows, head_width).astype(jnp.bfloat16)
    attn_proj = lax.psum_scatter(
        jnp.dot(attn_low, w_out, preferred_element_type=jnp.float32).astype(jnp.bfloat16),
        "seq",
        scatter_dimension=0,
        tiled=True,
    ).astype(jnp.float32)
    inv_attn = lax.rsqrt(jnp.mean(attn_proj * attn_proj, axis=1, keepdims=True) + EPS)
    attn_unit = attn_proj * inv_attn
    hidden = tokens.astype(jnp.float32) + attn_unit * gain_attn
    hidden_all = lax.all_gather(hidden.astype(jnp.bfloat16), "seq", axis=0, tiled=True)
    gate_proj = jnp.dot(hidden_all, w_gate, preferred_element_type=jnp.float32)
    up_proj = jnp.dot(hidden_all, w_up, preferred_element_type=jnp.float32)
    gate_sig = jax.nn.sigmoid(gate_proj)
    swish = gate_proj * gate_sig
    inner_low = (swish * up_proj).astype(jnp.bfloat16)
    ffn = lax.psum_scatter(
        jnp.dot(inner_low, w_down, preferred_element_type=jnp.float32).astype(jnp.bfloat16),
        "seq",
        scatter_dimension=0,
        tiled=True,
    ).astype(jnp.float32)
    inv_ffn = lax.rsqrt(jnp.mean(ffn * ffn, axis=1, keepdims=True) + EPS)
    ffn_unit = ffn * inv_ffn
    out_tokens = (hidden + ffn_unit * gain_ffn).astype(jnp.bfloat16)
    picked = jnp.sum(
        jnp.where(
            jnp.arange(group_weights.shape[0], dtype=jnp.int32) == source_ids[0], group_weights, 0.0
        )
    )
    grad_out = cotangent.astype(jnp.float32) * picked
    gain_ffn_part = jnp.sum(grad_out * ffn_unit, axis=0)
    grad_ffn_low = norm_back(ffn_unit, inv_ffn, grad_out * gain_ffn).astype(jnp.bfloat16)
    grad_ffn_all = lax.all_gather(grad_ffn_low, "seq", axis=0, tiled=True)
    grad_w_down = contract_rows(inner_low, grad_ffn_all)
    grad_inner = times_transpose(grad_ffn_all, w_down)
    grad_gate = (grad_inner * up_proj * gate_sig * (1.0 + gate_proj * (1.0 - gate_sig))).astype(
        jnp.bfloat16
    )
    grad_up = (grad_inner * swish).astype(jnp.bfloat16)
    grad_w_gate = contract_rows(hidden_all, grad_gate)
    grad_w_up = contract_rows(hidden_all, grad_up)
    grad_hidden = grad_out + lax.psum_scatter(
        (times_transpose(grad_gate, w_gate) + times_transpose(grad_up, w_up)).astype(jnp.bfloat16),
        "seq",
        scatter_dimension=0,
        tiled=True,
    ).astype(jnp.float32)
    gain_attn_part = jnp.sum(grad_hidden * attn_unit, axis=0)
    grad_proj_low = norm_back(attn_unit, inv_attn, grad_hidden * gain_attn).astype(jnp.bfloat16)
    grad_proj_all = lax.all_gather(grad_proj_low, "seq", axis=0, tiled=True)
    grad_w_out = contract_rows(attn_low, grad_proj_all)
    grad_attn_low = (
        times_transpose(grad_proj_all, w_out)
        .astype(jnp.bfloat16)
        .reshape(half_rows, heads_here, HD)
    )

    def backward_block(grad_carry, block_item):
        own_dk, own_dv, prev_dk, prev_dv = grad_carry
        row_start, log_total = block_item
        query_block = lax.dynamic_slice_in_dim(query_low, row_start, block_rows, 0)
        grad_block = lax.dynamic_slice_in_dim(grad_attn_low, row_start, block_rows, 0)
        own_scores, prev_scores = scores_of(query_block, row_start)
        own_probs = jnp.exp(own_scores - log_total[..., None])
        prev_probs = jnp.exp(prev_scores - log_total[..., None])
        own_dprob = jnp.einsum(
            "qhd,khd->hqk", grad_block, value_low, preferred_element_type=jnp.float32
        )
        prev_dprob = jnp.einsum(
            "qhd,khd->hqk", grad_block, value_prev, preferred_element_type=jnp.float32
        )
        row_delta = jnp.sum(own_probs * own_dprob, axis=-1) + jnp.sum(
            prev_probs * prev_dprob, axis=-1
        )
        own_dscore = (own_probs * (own_dprob - row_delta[..., None])).astype(jnp.bfloat16)
        prev_dscore = (prev_probs * (prev_dprob - row_delta[..., None])).astype(jnp.bfloat16)
        query_grad = jnp.einsum(
            "hqk,khd->qhd", own_dscore, key_low, preferred_element_type=jnp.float32
        )
        query_grad = score_scale * (
            query_grad
            + jnp.einsum("hqk,khd->qhd", prev_dscore, key_prev, preferred_element_type=jnp.float32)
        )
        own_dk = own_dk + score_scale * jnp.einsum(
            "hqk,qhd->khd", own_dscore, query_block, preferred_element_type=jnp.float32
        )
        prev_dk = prev_dk + score_scale * jnp.einsum(
            "hqk,qhd->khd", prev_dscore, query_block, preferred_element_type=jnp.float32
        )
        own_dv = own_dv + jnp.einsum(
            "hqk,qhd->khd",
            own_probs.astype(jnp.bfloat16),
            grad_block,
            preferred_element_type=jnp.float32,
        )
        prev_dv = prev_dv + jnp.einsum(
            "hqk,qhd->khd",
            prev_probs.astype(jnp.bfloat16),
            grad_block,
            preferred_element_type=jnp.float32,
        )
        return ((own_dk, own_dv, prev_dk, prev_dv), query_grad)

    zero_grad = jnp.zeros((half_rows, heads_here, HD), jnp.float32)
    (own_dk, own_dv, prev_dk, prev_dv), query_grads = lax.scan(
        backward_block, (zero_grad, zero_grad, zero_grad, zero_grad), (row_starts, lse_blocks)
    )
    back_dk, back_dv = (
        shifted(prev_dk.astype(jnp.bfloat16), "ctx", -1).astype(prev_dk.dtype),
        shifted(prev_dv.astype(jnp.bfloat16), "ctx", -1).astype(prev_dv.dtype),
    )
    grad_key_rot = own_dk + back_dk
    grad_value_low = (own_dv + back_dv).reshape(half_rows, head_width).astype(jnp.bfloat16)
    grad_query_norm = rope_turn(
        query_grads.reshape(half_rows, heads_here, HD), cosine, sine, -1.0
    ).reshape(half_rows, head_width)
    grad_key_norm = rope_turn(grad_key_rot, cosine, sine, -1.0).reshape(half_rows, head_width)
    gain_query_part = jnp.sum(grad_query_norm * query_unit, axis=0)
    gain_key_part = jnp.sum(grad_key_norm * key_unit, axis=0)
    query_scaled = grad_query_norm * gain_query
    key_scaled = grad_key_norm * gain_key
    dots_query, dots_key, gain_attn_seq, gain_ffn_seq = (
        lax.psum(jnp.sum(query_scaled * query_unit, axis=1).astype(jnp.bfloat16), "seq").astype(
            jnp.float32
        ),
        lax.psum(jnp.sum(key_scaled * key_unit, axis=1).astype(jnp.bfloat16), "seq").astype(
            jnp.float32
        ),
        lax.psum(gain_attn_part.astype(jnp.bfloat16), "seq").astype(jnp.float32),
        lax.psum(gain_ffn_part.astype(jnp.bfloat16), "seq").astype(jnp.float32),
    )
    grad_query_low = (inv_query * (query_scaled - query_unit * (dots_query / D)[:, None])).astype(
        jnp.bfloat16
    )
    grad_key_low = (inv_key * (key_scaled - key_unit * (dots_key / D)[:, None])).astype(
        jnp.bfloat16
    )
    grad_w_query = contract_rows(tokens_all, grad_query_low)
    grad_w_key = contract_rows(tokens_all, grad_key_low)
    grad_w_value = contract_rows(tokens_all, grad_value_low)
    grad_tokens = grad_hidden + lax.psum_scatter(
        (
            times_transpose(grad_query_low, w_query)
            + times_transpose(grad_key_low, w_key)
            + times_transpose(grad_value_low, w_value)
        ).astype(jnp.bfloat16),
        "seq",
        scatter_dimension=0,
        tiled=True,
    ).astype(jnp.float32)
    attn_summed = (
        lax.psum(grad_w_query.astype(jnp.bfloat16), ("dp", "ctx")).astype(jnp.float32),
        lax.psum(grad_w_key.astype(jnp.bfloat16), ("dp", "ctx")).astype(jnp.float32),
        lax.psum(grad_w_value.astype(jnp.bfloat16), ("dp", "ctx")).astype(jnp.float32),
        lax.psum(gain_query_part.astype(jnp.bfloat16), ("dp", "ctx")).astype(jnp.float32),
        lax.psum(gain_key_part.astype(jnp.bfloat16), ("dp", "ctx")).astype(jnp.float32),
        lax.psum(grad_w_out.astype(jnp.bfloat16), ("dp", "ctx")).astype(jnp.float32),
        lax.psum(gain_attn_seq.astype(jnp.bfloat16), ("dp", "ctx")).astype(jnp.float32),
        lax.psum(gain_ffn_seq.astype(jnp.bfloat16), ("dp", "ctx")).astype(jnp.float32),
    )
    ffn_summed = sum_ffn((grad_w_gate, grad_w_up, grad_w_down))
    return (
        out_tokens,
        grad_tokens,
        attn_summed[0],
        attn_summed[1],
        attn_summed[2],
        attn_summed[3],
        attn_summed[4],
        attn_summed[5],
        attn_summed[6],
        ffn_summed[0],
        ffn_summed[1],
        ffn_summed[2],
        attn_summed[7],
    )


def solution(mesh):
    in_specs = (
        P(("dp", "ctx", "seq"), None),
        P(None, "seq"),
        P(None, "seq"),
        P(None, "seq"),
        P("seq"),
        P("seq"),
        P("seq", None),
        P(),
        P(None, "seq"),
        P(None, "seq"),
        P("seq", None),
        P(),
        P(("dp", "ctx", "seq"), None),
        P("dp"),
        P(),
    )
    out_specs = (
        P(("dp", "ctx", "seq"), None),
        P(("dp", "ctx", "seq"), None),
        P(None, "seq"),
        P(None, "seq"),
        P(None, "seq"),
        P("seq"),
        P("seq"),
        P("seq", None),
        P(),
        P(None, "seq"),
        P(None, "seq"),
        P("seq", None),
        P(),
    )
    return jax.shard_map(body, mesh=mesh, in_specs=in_specs, out_specs=out_specs, check_vma=False)
```

profile of v0, /device:TPU:0, one launch (start us, length us, event | category | flops | bytes accessed | tf_op | source)
XLA Modules:
  0.0 1465.8 jit_solution(15550866455530121957)
XLA Ops:
  10.6 24.3 %all-gather.5.cloned.1.call-done = bf16[512,2048]{1,0:T(8,128)(2,1)} async-done(((bf16[128,2048]{1,0:T(8,128)(2,1)}), bf16[512,2048]{1,0:T(8,128)(2,1)}) %all-gather.5.cloned.1.call-update) | async-done | bytes 2097168 | tf_op jit(solution)/shard_map/all_gather | solution.py:89
  69.6 8.1 collective-permute-done
  80.6 6.8 collective-permute-done.1
  91.9 32.3 %reduce-scatter.5.cloned.1.call-done = bf16[128,2048]{1,0:T(8,128)(2,1)} async-done(((bf16[512,2048]{1,0:T(8,128)(2,1)}), bf16[128,2048]{1,0:T(8,128)(2,1)}) %reduce-scatter.5.cloned.1.call-update) | async-done | bytes 524304 | tf_op jit(solution)/shard_map/reduce_scatter | solution.py:143
  127.6 22.7 %all-gather.7.cloned.1.call-done = bf16[512,2048]{1,0:T(8,128)(2,1)} async-done(((bf16[128,2048]{1,0:T(8,128)(2,1)}), bf16[512,2048]{1,0:T(8,128)(2,1)}) %all-gather.7.cloned.1.call-update) | async-done | bytes 2097168 | tf_op jit(solution)/shard_map/all_gather | solution.py:152
  150.3 8.5 fusion.64
  158.8 11.6 multiply_convert_fusion.4
  179.3 29.6 %reduce-scatter.7.cloned.1.call-done = bf16[128,2048]{1,0:T(8,128)(2,1)} async-done(((bf16[512,2048]{1,0:T(8,128)(2,1)}), bf16[128,2048]{1,0:T(8,128)(2,1)}) %reduce-scatter.7.cloned.1.call-update) | async-done | bytes 524304 | tf_op jit(solution)/shard_map/reduce_scatter | solution.py:158
  215.2 22.7 %all-gather.9.cloned.1.call-done = bf16[512,2048]{1,0:T(8,128)(2,1)} async-done(((bf16[128,2048]{1,0:T(8,128)(2,1)}), bf16[512,2048]{1,0:T(8,128)(2,1)}) %all-gather.9.cloned.1.call-update) | async-done | bytes 2097168 | tf_op jit(solution)/shard_map/all_gather | solution.py:175
  237.8 11.9 multiply_convert_fusion.2
  249.8 8.5 fusion.65
  258.3 9.2 add_convert_fusion.1
  267.6 31.3 %reduce-scatter.9.cloned.1.call-done = bf16[128,2048]{1,0:T(8,128)(2,1)} async-done(((bf16[512,2048]{1,0:T(8,128)(2,1)}), bf16[128,2048]{1,0:T(8,128)(2,1)}) %reduce-scatter.9.cloned.1.call-update) | async-done | bytes 524304 | tf_op jit(solution)/shard_map/reduce_scatter | solution.py:184
  304.9 22.5 %all-gather.11.cloned.1.call-done = bf16[512,2048]{1,0:T(8,128)(2,1)} async-done(((bf16[128,2048]{1,0:T(8,128)(2,1)}), bf16[512,2048]{1,0:T(8,128)(2,1)}) %all-gather.11.cloned.1.call-update) | async-done | bytes 2097168 | tf_op jit(solution)/shard_map/all_gather | solution.py:192
  344.4 12.3 collective-permute-done.2
  372.4 10.4 all-reduce.3
  394.8 10.3 convolution_convert_fusion.2
  405.1 7.1 convolution_convert_fusion.1
  412.2 6.8 convolution_convert_fusion
  429.4 37.6 %all-reduce.1 = (bf16[512]{0:T(512)(128)(2,1)S(1)}, bf16[512]{0:T(512)(128)(2,1)S(1)}, bf16[2048]{0:T(1024)(128)(2,1)S(1)}, bf16[2048]{0:T(1024)(128)(2,1)S(1)}) all-reduce(bf16[512]{0:T(512)(128)(2,1)S(1)} %get-tuple-element.103, bf16[512]{0:T(512)(128)(2,1)S(1)} %get-tuple-element.101, ...), channel_id=1, replica_groups=mesh['dp'=4,'ctx'=2,'seq'=4] {'dp','ctx'}, use_global_device_ids=true, to_apply=%region_27.28 | all-reduce | flops 5120 | bytes 20480 | tf_op jit(solution)/shard_map/psum | solution.py:297
  472.2 935.1 %all-reduce.6.cloned.1.call-done = (bf16[2048,512]{0,1:T(8,128)(2,1)}, bf16[2048,512]{0,1:T(8,128)(2,1)}, bf16[2048,512]{0,1:T(8,128)(2,1)}, bf16[512,2048]{1,0:...) async-done(((bf16[2048,512]{0,1:T(8,128)(2,1)}, bf16[2048,512]{0,1:T(8,128)(2,1)}, bf16[2048,512]{0,1:T(8,128)(2,1)}, ...) | async-done | bytes 33554448 | tf_op jit(solution)/shard_map/psum | solution.py:294
  1423.8 11.7 convert_element_type.281
  1435.5 11.7 convert_element_type.283
  1447.1 11.7 convert_element_type.285
  (220 shorter events, 145.6 us)
Async XLA Ops:
  7.2 31.4 %copy-start = (bf16[2048,512]{1,0:T(8,128)(2,1)S(1)}, bf16[2048,512]{1,0:T(8,128)(2,1)}, u32[]{:S(2)}) copy-start(bf16[2048,512]{1,0:T(8,128)(2,1)} %param.16) | copy-start | bytes 6291460
  7.2 27.7 %all-gather.5.cloned.1.call-start = ((), (), s32[]{:S(2)}) async-start(), calls=%async_computation.4 | async-start | bytes 2621440 | tf_op jit(solution)/shard_map/all_gather | solution.py:89
  7.9 116.2 %reduce-scatter.5.cloned.1.call-start = ((), (), s32[]{:S(2)}) async-start(), calls=%async_computation.5 | async-start | bytes 2621440 | tf_op jit(solution)/shard_map/reduce_scatter | solution.py:143
  61.7 16.0 %collective-permute-start = (bf16[512,4,128]{2,0,1:T(8,128)(2,1)S(1)}, bf16[512,4,128]{2,0,1:T(8,128)(2,1)S(1)}, u32[]{:S(2)}, u32[]{:S(2)}) collective-permute-start(bf16[512,4,128]{2,0,1:T(8,128)(2,1)S(1)} %pad_maximum_fusion.3), channel_id=1, source_target_pairs={{0,4},{1,5},{2,6},{3,7},{8,12},{9,13},{10,14},{11,15},{16,20},{17,... | collective-permute-start | bytes 1572872 | tf_op jit(solution)/shard_map/ppermute | solution.py:18
  66.7 13.0 copy-start.34
  66.7 20.7 %collective-permute-start.1 = (bf16[512,4,128]{0,2,1:T(8,128)(2,1)S(1)}, bf16[512,4,128]{0,2,1:T(8,128)(2,1)S(1)}, u32[]{:S(2)}, u32[]{:S(2)}) collective-permute-start(bf16[512,4,128]{0,2,1:T(8,128)(2,1)S(1)} %bitcast.116), channel_id=1, source_target_pairs={{0,4},{1,5},{2,6},{3,7},{8,12},{9,13},{10,14},{11,15},{16,20},{17,... | collective-permute-start | bytes 1572872 | tf_op jit(solution)/shard_map/ppermute | solution.py:18
  89.2 36.2 %copy-start.14 = (bf16[128,2048]{1,0:T(8,128)(2,1)S(1)}, bf16[128,2048]{1,0:T(8,128)(2,1)}, u32[]{:S(2)}) copy-start(bf16[128,2048]{1,0:T(8,128)(2,1)} %param.15) | copy-start | bytes 1572868
  89.2 36.2 %copy-start.35 = (f32[2048]{0:T(1024)S(1)}, f32[2048]{0:T(1024)}, u32[]{:S(2)}) copy-start(f32[2048]{0:T(1024)} %param.22) | copy-start | bytes 24580
  91.9 58.4 %all-gather.7.cloned.1.call-start = ((), (), s32[]{:S(2)}) async-start(), calls=%async_computation.6 | async-start | bytes 2621440 | tf_op jit(solution)/shard_map/all_gather | solution.py:152
  127.5 81.4 %reduce-scatter.7.cloned.1.call-start = ((), (), s32[]{:S(2)}) async-start(), calls=%async_computation.7 | async-start | bytes 2621440 | tf_op jit(solution)/shard_map/reduce_scatter | solution.py:158
  150.3 21.5 %slice-start = ((s8[8388608]{0:T(1024)(128)(4,1)}), s8[4194304]{0:T(1024)(128)(4,1)S(1)}, s32[]{:S(2)}) async-start(s8[8388608]{0:T(1024)(128)(4,1)} %bitcast.119), calls=%async_computation.13 | async-start | bytes 8388608
  158.8 13.0 slice-start.1
  171.8 38.3 %copy-start.6 = (bf16[128,2048]{1,0:T(8,128)(2,1)S(1)}, bf16[128,2048]{1,0:T(8,128)(2,1)}, u32[]{:S(2)}) copy-start(bf16[128,2048]{1,0:T(8,128)(2,1)} %param.27) | copy-start | bytes 1572868
  171.8 38.3 %copy-start.36 = (f32[2048]{0:T(1024)S(1)}, f32[2048]{0:T(1024)}, u32[]{:S(2)}) copy-start(f32[2048]{0:T(1024)} %param.26) | copy-start | bytes 24580
  177.6 60.3 %all-gather.9.cloned.1.call-start = ((), (), s32[]{:S(2)}) async-start(), calls=%async_computation.8 | async-start | bytes 2621440 | tf_op jit(solution)/shard_map/all_gather | solution.py:175
  215.1 83.8 %reduce-scatter.9.cloned.1.call-start = ((), (), s32[]{:S(2)}) async-start(), calls=%async_computation.9 | async-start | bytes 2621440 | tf_op jit(solution)/shard_map/reduce_scatter | solution.py:184
  258.3 40.6 %copy-start.11 = (bf16[128,2048]{1,0:T(8,128)(2,1)S(1)}, bf16[128,2048]{1,0:T(8,128)(2,1)}, u32[]{:S(2)}) copy-start(bf16[128,2048]{1,0:T(8,128)(2,1)} %reduce-scatter.5.cloned.1.call-done) | copy-start | bytes 1572868
  267.5 59.8 %all-gather.11.cloned.1.call-start = ((), (), s32[]{:S(2)}) async-start(), calls=%async_computation.10 | async-start | bytes 2621440 | tf_op jit(solution)/shard_map/all_gather | solution.py:192
  304.7 164.7 %reduce-scatter.11.cloned.1.call-start = ((), (), s32[]{:S(2)}) async-start(), calls=%async_computation.11 | async-start | bytes 2621440 | tf_op jit(solution)/shard_map/reduce_scatter | solution.py:283
  340.0 16.7 %collective-permute-start.2 = (bf16[512,4,128]{2,0,1:T(8,128)(2,1)S(1)}, bf16[512,4,128]{2,0,1:T(8,128)(2,1)S(1)}, u32[]{:S(2)}, u32[]{:S(2)}) collective-permute-start(bf16[512,4,128]{2,0,1:T(8,128)(2,1)S(1)} %fusion.36), channel_id=1, source_target_pairs={{4,0},{5,1},{6,2},{7,3},{12,8},{13,9},{14,10},{15,11},{20,16},{21,... | collective-permute-start | bytes 1572872 | tf_op jit(solution)/shard_map/ppermute | solution.py:18
  341.3 47.0 %collective-permute-start.3 = (bf16[512,4,128]{0,2,1:T(8,128)(2,1)}, bf16[512,4,128]{0,2,1:T(8,128)(2,1)}, u32[]{:S(2)}, u32[]{:S(2)}) collective-permute-start(bf16[512,4,128]{0,2,1:T(8,128)(2,1)} %fusion.37), channel_id=1, source_target_pairs={{4,0},{5,1},{6,2},{7,3},{12,8},{13,9},{14,10},{15,11},{20,16},{21,... | collective-permute-start | bytes 1572872 | tf_op jit(solution)/shard_map/ppermute | solution.py:18
  343.5 13.9 copy-start.30
  394.7 1012.6 %all-reduce.6.cloned.1.call-start = ((), (), s32[]{:S(2)}) async-start(), calls=%async_computation.12 | async-start | bytes 67108864 | tf_op jit(solution)/shard_map/psum | solution.py:294
  429.4 40.0 %copy-start.15 = (bf16[128,2048]{1,0:T(8,128)(2,1)S(1)}, bf16[128,2048]{1,0:T(8,128)(2,1)}, u32[]{:S(2)}) copy-start(bf16[128,2048]{1,0:T(8,128)(2,1)} %reduce-scatter.9.cloned.1.call-done) | copy-start | bytes 1572868
  (47 other events, 253.3 us)
Sparse Core Ops, SparseCore 0:
  9.6 25.2 all-gather.4
  92.0 32.1 reduce-scatter.4
  127.7 22.5 all-gather.6
  177.7 31.1 reduce-scatter.6
  215.2 22.5 all-gather.8
  267.7 31.1 reduce-scatter.8
  304.8 22.5 all-gather.10
  394.8 30.4 reduce-scatter.10
  432.4 974.8 all-reduce.5
where the time goes:
time: 1470 us
  waiting for transfers between devices  1150 us (78%)
  matrix products  123 us (8%)
  other arithmetic  81.9 us (6%)
  blocking collectives  54 us (4%)
  local copies, waits for them, and re-layouts  34.3 us (2%)
  between operations  15.8 us (1%)
    psum x1, waiting for transfers between devices, body(): lax.psum(grad_w_query.astype(jnp.bfloat16), ('dp', 'ctx'))  935 us
    dot_general x7, matrix products, times_transpose(): lax.dot_general(left, right, (((1,), (1,)), ((), ())), preferred_element_...  38.4 us
    psum x1, blocking collectives, body(): lax.psum(gain_query_part.astype(jnp.bfloat16), ('dp', 'ctx'))  37.6 us
    dot_general x7, matrix products, contract_rows(): lax.dot_general(left, right, (((0,), (0,)), ((), ())), preferred_element_...  34.6 us
    reduce_scatter x1, waiting for transfers between devices, body(): lax.psum_scatter(jnp.dot(attn_low, w_out, preferred_element_type=jnp.floa...  32.3 us
    reduce_scatter x1, waiting for transfers between devices, body(): lax.psum_scatter((times_transpose(grad_gate, w_gate) + times_transpose(gr...  31.3 us
    reduce_scatter x1, waiting for transfers between devices, body(): lax.psum_scatter(jnp.dot(inner_low, w_down, preferred_element_type=jnp.fl...  29.6 us
  transfers between devices with their start and end apart: 13, of which 11 were waited for; matrix products, arithmetic and copies ran while one was open for 5% of the time, Pallas kernels for 0%

commit v1 on v0

v1 whole, which is shorter than its diff:
```python
import functools

import jax
import jax.numpy as jnp
from jax import lax
from jax.experimental import pallas as pl
from jax.experimental.pallas import tpu as pltpu
from jax.sharding import PartitionSpec as P

D = 2048
HD = 128


EPS = 1e-06
ROPE_BASE = 500000.0
NEG_FILL = -1e30
CHUNKS = 4
STREAMS = 2


def flip(value, axis, distance):
    count = lax.axis_size(axis)
    return lax.ppermute(value, axis, [(place, place ^ distance) for place in range(count)])


def distances(axis):
    count = lax.axis_size(axis)
    found = []
    step = 1
    while step < count:
        found.append(step)
        step *= 2
    return found


def gather_rows(own, axis):
    parts = {0: own}
    for distance in reversed(distances(axis)):
        parts.update({o ^ distance: flip(block, axis, distance) for o, block in parts.items()})
    return [parts[o] for o in range(len(parts))]


def gather_both(own, axis):
    mine = gather_rows(own, axis)
    theirs = gather_rows(flip(own, "ctx", 1), axis)
    return jnp.concatenate(mine, axis=0), jnp.concatenate(theirs, axis=0)


def scatter_rows(blocks, axis):
    parts = dict(enumerate(blocks))
    for distance in distances(axis):
        kept = {o: block for o, block in parts.items() if not o & distance}
        for o in sorted(kept, reverse=True):
            sent = parts[o ^ distance].astype(jnp.bfloat16)
            kept[o] = kept[o] + flip(sent, axis, distance).astype(jnp.float32)
        parts = kept
    return parts[0]


def row_blocks(value, count):
    rows = value.shape[0] // count
    return [lax.slice_in_dim(value, o * rows, (o + 1) * rows, axis=0) for o in range(count)]


def norm_back(unit_val, inverse, grad_unit):
    return inverse * (grad_unit - unit_val * jnp.mean(grad_unit * unit_val, axis=-1, keepdims=True))


def contract_rows(left, right):
    return lax.dot_general(
        left, right, (((0,), (0,)), ((), ())), preferred_element_type=jnp.float32
    )


def times_transpose(left, right):
    return lax.dot_general(
        left, right, (((1,), (1,)), ((), ())), preferred_element_type=jnp.float32
    )


def half_columns(value, place):
    width = value.shape[1] // 2
    return lax.dynamic_slice_in_dim(value, place * width, width, axis=1)


def swap_halves(value):
    place = lax.axis_index("ctx")
    return half_columns(value, place), flip(half_columns(value, 1 - place), "ctx", 1)


def turned(values, cosine, sine):
    return values * cosine + pltpu.roll(values, HD // 2, 1) * sine


def attend_kernel(
    query_ref, key_ref, value_ref, inv_query_ref, inv_key_ref, gain_query_ref, gain_key_ref,
    cos_query_ref, sin_query_ref, cos_key_ref, sin_key_ref, at_query_ref, at_key_ref,
    query_low_ref, key_low_ref, mixed_ref, lse_ref,
):
    @pl.when(pl.program_id(1) == 0)
    def _():
        scaled = key_ref[...] * inv_key_ref[...] * gain_key_ref[...]
        key_low_ref[...] = turned(scaled, cos_key_ref[...], sin_key_ref[...]).astype(jnp.bfloat16)

    scaled = query_ref[...] * inv_query_ref[...] * gain_query_ref[...]
    query_low = turned(scaled, cos_query_ref[...], sin_query_ref[...]).astype(jnp.bfloat16)
    query_low_ref[...] = query_low
    scores = HD ** (-0.5) * times_transpose(query_low, key_low_ref[...])
    scores = jnp.where(at_key_ref[...] <= at_query_ref[...], scores, NEG_FILL)
    peak = jnp.max(scores, axis=1, keepdims=True)
    exps = jnp.exp(scores - peak)
    total = jnp.sum(exps, axis=1, keepdims=True)
    probs = (exps * (1.0 / total)).astype(jnp.bfloat16)
    mixed_ref[...] = jnp.dot(
        probs, value_ref[...], preferred_element_type=jnp.float32
    ).astype(jnp.bfloat16)
    lse_ref[0] = peak + jnp.log(total)


def attend_back_kernel(
    query_low_ref, key_low_ref, value_ref, grad_ref, lse_ref,
    cos_query_ref, sin_query_ref, cos_key_ref, sin_key_ref, at_query_ref, at_key_ref,
    grad_query_ref, grad_key_ref, grad_value_ref, prev_key_ref, prev_value_ref,
    key_sum, value_sum,
):
    scale = HD ** (-0.5)
    query_low = query_low_ref[...]
    key_low = key_low_ref[...]
    grad_low = grad_ref[...]
    scores = scale * times_transpose(query_low, key_low)
    allowed = at_key_ref[...] <= at_query_ref[...]
    probs = jnp.exp(jnp.where(allowed, scores, NEG_FILL) - lse_ref[0])
    grad_probs = times_transpose(grad_low, value_ref[...])
    delta = jnp.sum(probs * grad_probs, axis=1, keepdims=True)
    grad_scores = (probs * (grad_probs - delta)).astype(jnp.bfloat16)
    grad_query = scale * jnp.dot(grad_scores, key_low, preferred_element_type=jnp.float32)
    grad_query_ref[...] = turned(grad_query, cos_query_ref[...], -sin_query_ref[...])
    key_part = scale * contract_rows(grad_scores, query_low)
    value_part = contract_rows(probs.astype(jnp.bfloat16), grad_low)

    @pl.when(pl.program_id(1) == 0)
    def _():
        key_sum[...] = key_part
        value_sum[...] = value_part

    @pl.when(pl.program_id(1) > 0)
    def _():
        key_sum[...] += key_part
        value_sum[...] += value_part

    @pl.when(pl.program_id(1) == pl.num_programs(1) - 1)
    def _():
        half = key_sum.shape[0] // 2
        turned_back = turned(key_sum[...], cos_key_ref[...], -sin_key_ref[...])
        grad_key_ref[...] = turned_back[:half]
        prev_key_ref[...] = turned_back[half:].astype(jnp.bfloat16)
        grad_value_ref[...] = value_sum[:half]
        prev_value_ref[...] = value_sum[half:].astype(jnp.bfloat16)


def attention_specs(half_rows, key_rows, block_rows):
    spec = {
        "query": pl.BlockSpec((block_rows, HD), lambda h, i: (i, h)),
        "key": pl.BlockSpec((key_rows, HD), lambda h, i: (0, h)),
        "half": pl.BlockSpec((half_rows, HD), lambda h, i: (0, h)),
        "gain": pl.BlockSpec((1, HD), lambda h, i: (0, h)),
        "query_column": pl.BlockSpec((block_rows, 1), lambda h, i: (i, 0)),
        "key_column": pl.BlockSpec((key_rows, 1), lambda h, i: (0, 0)),
        "key_row": pl.BlockSpec((1, key_rows), lambda h, i: (0, 0)),
        "query_turn": pl.BlockSpec((block_rows, HD), lambda h, i: (i, 0)),
        "key_turn": pl.BlockSpec((key_rows, HD), lambda h, i: (0, 0)),
        "lse": pl.BlockSpec((1, block_rows, 1), lambda h, i: (h, i, 0)),
    }
    return spec


def attend(query, key, value, inv_query, inv_key, gain_query, gain_key, turns, block_rows):
    half_rows, width = query.shape
    key_rows = key.shape[0]
    heads = width // HD
    s = attention_specs(half_rows, key_rows, block_rows)
    return pl.pallas_call(
        attend_kernel,
        grid=(heads, half_rows // block_rows),
        in_specs=[
            s["query"], s["key"], s["key"], s["query_column"], s["key_column"], s["gain"], s["gain"],
            s["query_turn"], s["query_turn"], s["key_turn"], s["key_turn"],
            s["query_column"], s["key_row"],
        ],
        out_specs=[s["query"], s["key"], s["query"], s["lse"]],
        out_shape=[
            jax.ShapeDtypeStruct(query.shape, jnp.bfloat16),
            jax.ShapeDtypeStruct(key.shape, jnp.bfloat16),
            jax.ShapeDtypeStruct(query.shape, jnp.bfloat16),
            jax.ShapeDtypeStruct((heads, half_rows, 1), jnp.float32),
        ],
        name="attend",
    )(query, key, value, inv_query, inv_key, gain_query, gain_key, *turns)


def attend_back(query_low, key_low, value, grad, lse, turns, block_rows):
    half_rows, width = query_low.shape
    key_rows = key_low.shape[0]
    heads = width // HD
    s = attention_specs(half_rows, key_rows, block_rows)
    halves = (half_rows, width)
    return pl.pallas_call(
        attend_back_kernel,
        grid=(heads, half_rows // block_rows),
        in_specs=[
            s["query"], s["key"], s["key"], s["query"], s["lse"],
            s["query_turn"], s["query_turn"], s["key_turn"], s["key_turn"],
            s["query_column"], s["key_row"],
        ],
        out_specs=[s["query"], s["half"], s["half"], s["half"], s["half"]],
        out_shape=[
            jax.ShapeDtypeStruct(halves, jnp.float32),
            jax.ShapeDtypeStruct(halves, jnp.float32),
            jax.ShapeDtypeStruct(halves, jnp.float32),
            jax.ShapeDtypeStruct(halves, jnp.bfloat16),
            jax.ShapeDtypeStruct(halves, jnp.bfloat16),
        ],
        scratch_shapes=[
            pltpu.VMEM((key_rows, HD), jnp.float32),
            pltpu.VMEM((key_rows, HD), jnp.float32),
        ],
        name="attend_back",
    )(query_low, key_low, value, grad, lse, *turns)


def store_kernel(place_ref, mine_ref, theirs_ref, *refs):
    out_ref = refs[-1]

    @pl.when(pl.program_id(0) == 0)
    def _():
        out_ref[...] = mine_ref[...].astype(jnp.float32)

    @pl.when(pl.program_id(0) == 1)
    def _():
        out_ref[...] = theirs_ref[...].astype(jnp.float32)


def store_chunk(buffer, mine, theirs, shape, index, chunks, by_rows):
    place = lax.axis_index("ctx").astype(jnp.int32).reshape(1)
    rows, columns = mine.shape
    if by_rows:
        where_to = lambda i, place_ref: ((place_ref[0] ^ i) * chunks + index, 0)
    else:
        where_to = lambda i, place_ref: (index, place_ref[0] ^ i)
    whole = pl.BlockSpec((rows, columns), lambda i, place_ref: (0, 0))
    operands = [place, mine, theirs]
    in_specs = [whole, whole]
    aliases = {}
    if buffer is not None:
        operands.append(buffer)
        in_specs.append(pl.BlockSpec(memory_space=pl.ANY))
        aliases = {3: 0}
    return pl.pallas_call(
        store_kernel,
        grid_spec=pltpu.PrefetchScalarGridSpec(
            num_scalar_prefetch=1,
            grid=(2,),
            in_specs=in_specs,
            out_specs=pl.BlockSpec((rows, columns), where_to),
        ),
        out_shape=jax.ShapeDtypeStruct(shape, jnp.float32),
        input_output_aliases=aliases,
        name="store",
    )(*operands)


class Gradient:
    def __init__(self, name, shape, chunks, by_rows):
        self.name, self.shape, self.chunks, self.by_rows = name, shape, chunks, by_rows
        self.buffer = None
        self.kept = {}

    def part(self, sides, index):
        left_own, left_other, grad_own, grad_other = sides
        rows = left_own.shape[1] // self.chunks
        cut = functools.partial(
            lax.slice_in_dim, start_index=index * rows, limit_index=(index + 1) * rows, axis=1
        )
        part = contract_rows(cut(left_own), grad_own) + contract_rows(cut(left_other), grad_other)
        return part.astype(jnp.bfloat16)

    def store(self, index, mine, theirs):
        if not self.by_rows and mine.shape[1] % 128:
            self.kept[index] = (mine, theirs)
            return
        self.buffer = store_chunk(
            self.buffer, mine, theirs, self.shape, index, self.chunks, self.by_rows
        )

    def result(self):
        if self.buffer is not None:
            return self.buffer
        first = lax.axis_index("ctx") == 0
        pieces = [
            jnp.concatenate(
                [jnp.where(first, mine, theirs), jnp.where(first, theirs, mine)], axis=1
            )
            for _, (mine, theirs) in sorted(self.kept.items())
        ]
        return jnp.concatenate(pieces, axis=0).astype(jnp.float32)


def added(left, right):
    return (left.astype(jnp.float32) + right.astype(jnp.float32)).astype(left.dtype)


def body(
    tokens,
    w_query,
    w_key,
    w_value,
    gain_query,
    gain_key,
    w_out,
    gain_attn,
    w_gate,
    w_up,
    w_down,
    gain_ffn,
    cotangent,
    source_ids,
    group_weights,
):
    seq_count = lax.axis_size("seq")
    seq_place = lax.axis_index("seq")
    ctx_place = lax.axis_index("ctx")
    dp_place = lax.axis_index("dp")
    middle = jnp.logical_or(dp_place == 1, dp_place == 2)
    tok_rows = tokens.shape[0]
    half_rows = tok_rows * seq_count
    head_width = w_query.shape[1]
    hidden_width = w_gate.shape[1]
    block_rows = min(512, half_rows) if half_rows <= 512 else 256
    owners = jnp.bitwise_xor(jnp.arange(seq_count, dtype=jnp.int32), seq_place)
    row_ids = (owners[:, None] * tok_rows + jnp.arange(tok_rows, dtype=jnp.int32)[None, :]).reshape(
        half_rows
    )
    at_query = (ctx_place * half_rows + row_ids).astype(jnp.float32)
    at_key = jnp.concatenate([at_query, ((1 - ctx_place) * half_rows + row_ids).astype(jnp.float32)])
    lane = jnp.arange(HD, dtype=jnp.int32)
    inverse = ROPE_BASE ** (-((lane % (HD // 2)).astype(jnp.float32) * 2.0 / HD))
    angles = at_key[:, None] * inverse[None, :]
    cosine = jnp.cos(angles)
    sine = jnp.sin(angles) * jnp.where(lane < HD // 2, -1.0, 1.0)[None, :]
    turns = (cosine, sine, cosine, sine, at_query[:, None], at_key[None, :])

    tokens_own, tokens_other = gather_both(tokens, "seq")
    tokens_both = jnp.concatenate([tokens_own, tokens_other], axis=0)
    query_proj = jnp.dot(tokens_own, w_query, preferred_element_type=jnp.float32)
    key_proj = jnp.dot(tokens_both, w_key, preferred_element_type=jnp.float32)
    value_low = jnp.dot(tokens_both, w_value, preferred_element_type=jnp.float32).astype(
        jnp.bfloat16
    )

    def common_rows(parts):
        stacked = jnp.stack(parts).reshape(len(parts), seq_count, tok_rows)
        return jnp.take(stacked, owners, axis=1)

    def own_rows(sums):
        return jnp.take(sums, owners, axis=1).reshape(sums.shape[0], half_rows)

    sq_key = jnp.sum(key_proj * key_proj, axis=1)
    sums = own_rows(
        lax.psum(
            common_rows(
                (jnp.sum(query_proj * query_proj, axis=1), sq_key[:half_rows], sq_key[half_rows:])
            ),
            "seq",
        )
    )
    inv_query = lax.rsqrt(sums[0] / D + EPS)[:, None]
    inv_key_both = lax.rsqrt(sums[1:].reshape(2 * half_rows) / D + EPS)[:, None]
    inv_key = inv_key_both[:half_rows]
    query_low, key_low, attn_low, lse = attend(
        query_proj, key_proj, value_low, inv_query, inv_key_both, gain_query[None, :],
        gain_key[None, :], turns, block_rows,
    )

    def to_owners(partial):
        return scatter_rows(row_blocks(partial, seq_count), "seq")

    attn_proj = to_owners(jnp.dot(attn_low, w_out, preferred_element_type=jnp.float32))
    attn_halves = swap_halves(attn_low)
    inv_attn = lax.rsqrt(jnp.mean(attn_proj * attn_proj, axis=1, keepdims=True) + EPS)
    attn_unit = attn_proj * inv_attn
    hidden = tokens.astype(jnp.float32) + attn_unit * gain_attn
    hidden_own, hidden_other = gather_both(hidden.astype(jnp.bfloat16), "seq")
    gate_proj = jnp.dot(hidden_own, w_gate, preferred_element_type=jnp.float32)
    up_proj = jnp.dot(hidden_own, w_up, preferred_element_type=jnp.float32)
    gate_sig = jax.nn.sigmoid(gate_proj)
    swish = gate_proj * gate_sig
    inner_low = (swish * up_proj).astype(jnp.bfloat16)
    inner_halves = swap_halves(inner_low)
    ffn = to_owners(jnp.dot(inner_low, w_down, preferred_element_type=jnp.float32))
    inv_ffn = lax.rsqrt(jnp.mean(ffn * ffn, axis=1, keepdims=True) + EPS)
    ffn_unit = ffn * inv_ffn
    out_tokens = (hidden + ffn_unit * gain_ffn).astype(jnp.bfloat16)
    picked = jnp.sum(
        jnp.where(
            jnp.arange(group_weights.shape[0], dtype=jnp.int32) == source_ids[0], group_weights, 0.0
        )
    )
    grad_out = cotangent.astype(jnp.float32) * picked
    gain_ffn_part = jnp.sum(grad_out * ffn_unit, axis=0)
    grad_ffn_low = norm_back(ffn_unit, inv_ffn, grad_out * gain_ffn).astype(jnp.bfloat16)
    grad_ffn_own, grad_ffn_other = gather_both(grad_ffn_low, "seq")

    grads = {
        "down": Gradient("down", w_down.shape, CHUNKS, True),
        "gate": Gradient("gate", w_gate.shape, CHUNKS, False),
        "up": Gradient("up", w_up.shape, CHUNKS, False),
        "out": Gradient("out", w_out.shape, 1, True),
        "value": Gradient("value", w_value.shape, 1, False),
        "key": Gradient("key", w_key.shape, 1, False),
        "query": Gradient("query", w_query.shape, 1, False),
    }
    sides = {"down": (*inner_halves, grad_ffn_own, grad_ffn_other)}
    results = {}

    def stages():
        grad_inner = times_transpose(grad_ffn_own, w_down)
        grad_gate = (grad_inner * up_proj * gate_sig * (1.0 + gate_proj * (1.0 - gate_sig))).astype(
            jnp.bfloat16
        )
        grad_up = (grad_inner * swish).astype(jnp.bfloat16)
        grad_gate, grad_up = yield (grad_gate, grad_up)
        gate_halves = swap_halves(grad_gate)
        up_halves = swap_halves(grad_up)
        partial = times_transpose(grad_gate, w_gate) + times_transpose(grad_up, w_up)
        (partial,) = yield (partial,)
        grad_hidden = grad_out + to_owners(partial)
        (grad_hidden,) = yield (grad_hidden,)
        gain_attn_part = jnp.sum(grad_hidden * attn_unit, axis=0)
        grad_proj_low = norm_back(attn_unit, inv_attn, grad_hidden * gain_attn).astype(jnp.bfloat16)
        grad_proj_own, grad_proj_other = gather_both(grad_proj_low, "seq")
        grad_proj_own, grad_proj_other, *gate_halves = yield (
            grad_proj_own, grad_proj_other, *gate_halves
        )
        sides["gate"] = (hidden_own, hidden_other, *gate_halves)
        sides["out"] = (*attn_halves, grad_proj_own, grad_proj_other)
        grad_attn_low = times_transpose(grad_proj_own, w_out).astype(jnp.bfloat16)
        backs = attend_back(query_low, key_low, value_low, grad_attn_low, lse, turns, block_rows)
        *backs, up_own, up_other = yield (*backs, *up_halves)
        sides["up"] = (hidden_own, hidden_other, up_own, up_other)
        grad_query_norm, own_dk, own_dv, prev_dk, prev_dv = backs
        back_dk, back_dv = lax.ppermute((prev_dk, prev_dv), "ctx", [(1, 0)])
        grad_query_norm, own_dk, own_dv, back_dk, back_dv = yield (
            grad_query_norm, own_dk, own_dv, back_dk, back_dv
        )
        grad_value_low = (own_dv + back_dv.astype(jnp.float32)).astype(jnp.bfloat16)
        grad_key_norm = own_dk + back_dk.astype(jnp.float32)
        query_unit = query_proj * inv_query
        key_unit = key_proj[:half_rows] * inv_key
        gain_query_part = jnp.sum(grad_query_norm * query_unit, axis=0)
        gain_key_part = jnp.sum(grad_key_norm * key_unit, axis=0)
        query_scaled = grad_query_norm * gain_query
        key_scaled = grad_key_norm * gain_key
        dots, gain_sums = lax.psum(
            (
                common_rows(
                    (
                        jnp.sum(query_scaled * query_unit, axis=1),
                        jnp.sum(key_scaled * key_unit, axis=1),
                    )
                ),
                jnp.concatenate([gain_attn_part, gain_ffn_part]),
            ),
            "seq",
        )
        dots_query, dots_key = own_rows(dots)
        grad_query_low = (
            inv_query * (query_scaled - query_unit * (dots_query / D)[:, None])
        ).astype(jnp.bfloat16)
        grad_key_low = (inv_key * (key_scaled - key_unit * (dots_key / D)[:, None])).astype(
            jnp.bfloat16
        )
        gains = jnp.concatenate([gain_sums, gain_query_part, gain_key_part]).reshape(-1, 128)
        grad_value_low, grad_key_low, grad_query_low, gains = yield (
            grad_value_low, grad_key_low, grad_query_low, gains
        )
        value_halves = swap_halves(grad_value_low)
        key_halves = swap_halves(grad_key_low)
        query_halves = swap_halves(grad_query_low)
        gains = gains + flip(gains, "ctx", 1)
        partial = (
            times_transpose(grad_query_low, w_query)
            + times_transpose(grad_key_low, w_key)
            + times_transpose(grad_value_low, w_value)
        )
        partial, gains, *halves = yield (
            partial, gains, *value_halves, *key_halves, *query_halves
        )
        sides["value"] = (tokens_own, tokens_other, *halves[0:2])
        sides["key"] = (tokens_own, tokens_other, *halves[2:4])
        sides["query"] = (tokens_own, tokens_other, *halves[4:6])
        results["gains"] = gains
        grad_tokens = grad_hidden + to_owners(partial)
        (grad_tokens,) = yield (grad_tokens,)
        results["tokens"] = grad_tokens

    plan = [(name, index) for name in grads for index in range(grads[name].chunks)]
    count = len(plan)
    rider = count - 1
    pairs = [(0, 1), (1, 0), (2, 3), (3, 2)]
    step = STREAMS
    part, pair, total, final = {}, {}, {}, {}
    got_pair, got_across, got_half = {}, {}, {}
    main = stages()
    state = next(main)

    def rides(index):
        return (results["gains"],) if index == rider else ()

    for tick in range(count + 4 * step):
        before = tick - step
        if before in part:
            pair[before] = jax.tree.map(added, part[before], got_pair[before][1])
        if before - step in part:
            total[before - step] = jax.tree.map(added, pair[before - step], got_across[before])
        if before - 2 * step in part:
            final[before - 2 * step] = jax.tree.map(
                lambda kept, got: jnp.where(middle, kept, got),
                total[before - 2 * step],
                got_pair[before][0],
            )
        if before - 3 * step in part:
            name, index = plan[before - 3 * step]
            grads[name].store(index, final[before - 3 * step][0], got_half[before])
        if tick < count:
            name, index = plan[tick]
            part[tick] = (grads[name].part(sides[name], index),) + rides(tick)
        entering = part.get(tick)
        leaving = total.get(tick - 2 * step)
        crossing = pair.get(tick - step)
        swapping = final.get(tick - 3 * step)
        held = (entering, leaving, crossing, swapping, state)
        entering, leaving, crossing, swapping, state = lax.optimization_barrier(held)
        if entering is not None:
            part[tick] = entering
        if leaving is not None:
            total[tick - 2 * step] = leaving
        if crossing is not None:
            pair[tick - step] = crossing
        if swapping is not None:
            final[tick - 3 * step] = swapping
        arrived_out = arrived_in = None
        alike = entering is not None and leaving is not None
        if alike and [v.shape for v in entering] == [v.shape for v in leaving]:
            sent = jax.tree.map(lambda out, into: jnp.where(middle, out, into), leaving, entering)
            arrived_in = arrived_out = tuple(lax.ppermute(v, "dp", pairs) for v in sent)
        else:
            if entering is not None:
                arrived_in = tuple(lax.ppermute(v, "dp", [(0, 1), (3, 2)]) for v in entering)
            if leaving is not None:
                arrived_out = tuple(lax.ppermute(v, "dp", [(1, 0), (2, 3)]) for v in leaving)
        got_pair[tick] = (arrived_out, arrived_in)
        if crossing is not None:
            got_across[tick] = tuple(lax.ppermute(v, "dp", [(1, 2), (2, 1)]) for v in crossing)
        if swapping is not None:
            got_half[tick] = flip(swapping[0], "ctx", 1)
        try:
            state = main.send(state)
        except StopIteration:
            state = ()

    gains = final[rider][1].reshape(-1)
    grad_gain_attn = gains[:D]
    grad_gain_ffn = gains[D : 2 * D]
    grad_gain_query = gains[2 * D : 2 * D + head_width]
    grad_gain_key = gains[2 * D + head_width :]
    return (
        out_tokens,
        results["tokens"],
        grads["query"].result(),
        grads["key"].result(),
        grads["value"].result(),
        grad_gain_query,
        grad_gain_key,
        grads["out"].result(),
        grad_gain_attn,
        grads["gate"].result(),
        grads["up"].result(),
        grads["down"].result(),
        grad_gain_ffn,
    )


def solution(mesh):
    in_specs = (
        P(("dp", "ctx", "seq"), None),
        P(None, "seq"),
        P(None, "seq"),
        P(None, "seq"),
        P("seq"),
        P("seq"),
        P("seq", None),
        P(),
        P(None, "seq"),
        P(None, "seq"),
        P("seq", None),
        P(),
        P(("dp", "ctx", "seq"), None),
        P("dp"),
        P(),
    )
    out_specs = (
        P(("dp", "ctx", "seq"), None),
        P(("dp", "ctx", "seq"), None),
        P(None, "seq"),
        P(None, "seq"),
        P(None, "seq"),
        P("seq"),
        P("seq"),
        P("seq", None),
        P(),
        P(None, "seq"),
        P(None, "seq"),
        P("seq", None),
        P(),
    )
    return jax.shard_map(body, mesh=mesh, in_specs=in_specs, out_specs=out_specs, check_vma=False)
```

time: 1470 us -> 1070 us (0.73)
  waiting for transfers between devices: 1150 us -> 578 us
  starting transfers between devices: 8.77 us -> 158 us
  Pallas kernels: 0 us -> 81.8 us
  blocking collectives: 54 us -> 18.5 us
  other arithmetic: 81.9 us -> 48.1 us
    psum x1 -> x0, waiting for transfers between devices: 935 us -> none  [body(): lax.psum(grad_w_query.astype(jnp.bfloat16), ('dp', 'ctx'))]
    ppermute x4 -> x113, waiting for transfers between devices: 27.2 us -> 578 us  [the longest x64 351 us: flip(): lax.ppermute(value, axis, [(place, place ^ distance) for place in range(c...]
    ppermute x4 -> x113, starting transfers between devices: 7.82 us -> 158 us  [the longest x13 66 us: body(): lax.ppermute(v, 'dp', [(0, 1), (3, 2)])]
    reduce_scatter x4 -> x0, waiting for transfers between devices: 93.1 us -> none  [the longest x1 32.3 us: body(): lax.psum_scatter(jnp.dot(attn_low, w_out, preferred_element_type=jnp.floa...]
    all_gather x4 -> x0, waiting for transfers between devices: 92.1 us -> none  [the longest x1 24.3 us: body(): tokens_all = lax.all_gather(tokens, 'seq', axis=0, tiled=True)]
    pallas_call x0 -> x18, Pallas kernels: none -> 81.8 us  [the longest x16 59.2 us: store_chunk(): pl.pallas_call(store_kernel, grid_spec=pltpu.PrefetchScalarGridSpec(num_s...]
    psum x3 -> x2, blocking collectives: 54 us -> 18.5 us  [the longest x1 11 us: stages(): lax.psum((common_rows((jnp.sum(query_scaled * query_unit, axis=1), jnp.su...]
    convert_element_type x13 -> x42, other arithmetic: 51.6 us -> 25.6 us  [the longest x32 20.2 us: added(): (left.astype(jnp.float32) + right.astype(jnp.float32)).astype(left.dtype)]
  transfers between devices with their start and end apart: 13 -> 113, of which waited for: 11 -> 48; matrix products, arithmetic and copies ran while one was open for 5% -> 13% of each run, Pallas kernels for 0% -> 6%
where the time goes in v1:
time: 1070 us; the launch traced here: 1060 us
  waiting for transfers between devices  578 us (54%)
  starting transfers between devices  158 us (15%)
  matrix products  132 us (12%)
  Pallas kernels  81.8 us (8%)
  other arithmetic  48.1 us (4%)
  local copies, waits for them, and re-layouts  43.4 us (4%)
  blocking collectives  18.5 us (2%)
    ppermute x64, waiting for transfers between devices, flip(): lax.ppermute(value, axis, [(place, place ^ distance) for place in range(c...  351 us
    ppermute x13, waiting for transfers between devices, body(): lax.ppermute(v, 'dp', [(0, 1), (3, 2)])  87.1 us
    ppermute x13, waiting for transfers between devices, body(): lax.ppermute(v, 'dp', [(1, 0), (2, 3)])  74.2 us
    ppermute x4, waiting for transfers between devices, body(): lax.ppermute(v, 'dp', pairs)  66.5 us
    ppermute x13, starting transfers between devices, body(): lax.ppermute(v, 'dp', [(0, 1), (3, 2)])  66 us
    pallas_call x16, Pallas kernels, store_chunk(): pl.pallas_call(store_kernel, grid_spec=pltpu.PrefetchScalarGridSpec(num_s...  59.2 us
    dot_general x32, matrix products, contract_rows(): lax.dot_general(left, right, (((0,), (0,)), ((), ())), preferred_element_...  54 us
    ppermute x64, starting transfers between devices, flip(): lax.ppermute(value, axis, [(place, place ^ distance) for place in range(c...  47.8 us
  transfers between devices with their start and end apart: 113, of which 48 were waited for; matrix products, arithmetic and copies ran while one was open for 13% of the time, Pallas kernels for 6%

profile of v1, /device:TPU:0, one launch (start us, length us, event | category | flops | bytes accessed | tf_op | source)
XLA Modules:
  0.0 1064.4 jit_solution(2841378557730062772)
XLA Ops:
  89.1 13.3 %collective-permute-done.9 = bf16[128,2048]{1,0:T(8,128)(2,1)S(1)} collective-permute-done((bf16[128,2048]{1,0:T(8,128)(2,1)S(1)}, bf16[128,2048]{1,0:T(8,128)(2,1)S(1)}, u32[]{:S(2)}, u32[]{:S(2)}) %collective-permute-start.9) | collective-permute-done | bytes 524320 | tf_op jit(solution)/shard_map/ppermute | solution.py:23
  183.4 18.9 %collective-permute-done.20 = bf16[128,2048]{1,0:T(8,128)(2,1)S(1)} collective-permute-done((bf16[128,2048]{1,0:T(8,128)(2,1)S(1)}, bf16[128,2048]{1,0:T(8,128)(2,1)S(1)}, u32[]{:S(2)}, u32[]{:S(2)}) %collective-permute-start.20) | collective-permute-done | bytes 524320 | tf_op jit(solution)/shard_map/ppermute | solution.py:23
  205.3 14.0 %multiply_convert_fusion = (bf16[512,2048]{1,0:T(8,128)(2,1)}, bf16[512,2048]{1,0:T(8,128)(2,1)}) fusion(f32[512,2048]{1,0:T(8,128)} %copy-done.109, f32[512,2048]{1,0:T(8,128)} %get-tuple-element.305, bf16[2048,2048]{1,0:T(8,128)(2,1)} %param.29, bf16[128,2048]{1,0:T(8,128)(2,1)} %copy-done.106, bf16[128,2048]{1,0:T(8,128)(2,1)} %copy-done.102, ...), kind=kOutput, calls=%fused_computation.5 | convolution fusion | flops 4316987392 | bytes 23068672 | tf_op jit(solution)/shard_map/dot_general | solution.py:76
  269.1 14.4 %collective-permute-done.25 = bf16[256,2048]{1,0:T(8,128)(2,1)S(1)} collective-permute-done((bf16[256,2048]{1,0:T(8,128)(2,1)S(1)}, bf16[256,2048]{1,0:T(8,128)(2,1)S(1)}, u32[]{:S(2)}, u32[]{:S(2)}) %collective-permute-start.25) | collective-permute-done | bytes 1048608 | tf_op jit(solution)/shard_map/ppermute | solution.py:558
  292.2 13.7 %collective-permute-done.24 = bf16[256,2048]{1,0:T(8,128)(2,1)S(1)} collective-permute-done((bf16[256,2048]{1,0:T(8,128)(2,1)S(1)}, bf16[256,2048]{1,0:T(8,128)(2,1)S(1)}, u32[]{:S(2)}, u32[]{:S(2)}) %collective-permute-start.24) | collective-permute-done | bytes 1048608 | tf_op jit(solution)/shard_map/ppermute | solution.py:558
  308.3 19.4 %collective-permute-done.42 = bf16[256,2048]{1,0:T(8,128)(2,1)S(1)} collective-permute-done((bf16[256,2048]{1,0:T(8,128)(2,1)S(1)}, bf16[256,2048]{1,0:T(8,128)(2,1)S(1)}, u32[]{:S(2)}, u32[]{:S(2)}) %collective-permute-start.42) | collective-permute-done | bytes 1048608 | tf_op jit(solution)/shard_map/ppermute | solution.py:558
  507.8 16.3 %collective-permute-done.65 = bf16[512,1024]{1,0:T(8,128)(2,1)S(1)} collective-permute-done((bf16[512,1024]{1,0:T(8,128)(2,1)S(1)}, bf16[512,1024]{1,0:T(8,128)(2,1)S(1)}, u32[]{:S(2)}, u32[]{:S(2)}) %collective-permute-start.65) | collective-permute-done | bytes 1048608 | tf_op jit(solution)/shard_map/ppermute | solution.py:558
  532.7 19.8 %collective-permute-done.86 = bf16[512,1024]{1,0:T(8,128)(2,1)S(1)} collective-permute-done((bf16[512,1024]{1,0:T(8,128)(2,1)S(1)}, bf16[512,1024]{1,0:T(8,128)(2,1)S(1)}, u32[]{:S(2)}, u32[]{:S(2)}) %collective-permute-start.86) | collective-permute-done | bytes 1048608 | tf_op jit(solution)/shard_map/ppermute | solution.py:555
  558.0 16.9 %collective-permute-done.68 = bf16[512,1024]{1,0:T(8,128)(2,1)S(1)} collective-permute-done((bf16[512,1024]{1,0:T(8,128)(2,1)S(1)}, bf16[512,1024]{1,0:T(8,128)(2,1)S(1)}, u32[]{:S(2)}, u32[]{:S(2)}) %collective-permute-start.68) | collective-permute-done | bytes 1048608 | tf_op jit(solution)/shard_map/ppermute | solution.py:555
  580.5 16.9 %collective-permute-done.88 = bf16[512,1024]{1,0:T(8,128)(2,1)S(1)} collective-permute-done((bf16[512,1024]{1,0:T(8,128)(2,1)S(1)}, bf16[512,1024]{1,0:T(8,128)(2,1)S(1)}, u32[]{:S(2)}, u32[]{:S(2)}) %collective-permute-start.88) | collective-permute-done | bytes 1048608 | tf_op jit(solution)/shard_map/ppermute | solution.py:555
  607.1 12.8 %collective-permute-done.70 = bf16[512,1024]{1,0:T(8,128)(2,1)S(1)} collective-permute-done((bf16[512,1024]{1,0:T(8,128)(2,1)S(1)}, bf16[512,1024]{1,0:T(8,128)(2,1)S(1)}, u32[]{:S(2)}, u32[]{:S(2)}) %collective-permute-start.70) | collective-permute-done | bytes 1048608 | tf_op jit(solution)/shard_map/ppermute | solution.py:555
  627.9 14.5 %collective-permute-done.91 = bf16[512,1024]{1,0:T(8,128)(2,1)S(1)} collective-permute-done((bf16[512,1024]{1,0:T(8,128)(2,1)S(1)}, bf16[512,1024]{1,0:T(8,128)(2,1)S(1)}, u32[]{:S(2)}, u32[]{:S(2)}) %collective-permute-start.91) | collective-permute-done | bytes 1048608 | tf_op jit(solution)/shard_map/ppermute | solution.py:560
  702.6 15.6 %collective-permute-done.77 = bf16[512,1024]{1,0:T(8,128)(2,1)S(1)} collective-permute-done((bf16[512,1024]{1,0:T(8,128)(2,1)S(1)}, bf16[512,1024]{1,0:T(8,128)(2,1)S(1)}, u32[]{:S(2)}, u32[]{:S(2)}) %collective-permute-start.77) | collective-permute-done | bytes 1048608 | tf_op jit(solution)/shard_map/ppermute | solution.py:560
  748.1 20.9 %collective-permute-done.111.theirs_ref = bf16[256,2048]{1,0:T(8,128)(2,1)S(1)} collective-permute-done((bf16[256,2048]{1,0:T(8,128)(2,1)S(1)}, bf16[256,2048]{1,0:T(8,128)(2,1)S(1)}, u32[]{:S(2)}, u32[]{:S(2)}) %collective-permute-start.111) | collective-permute-done | bytes 1048608 | tf_op jit(solution)/shard_map/ppermute | solution.py:23
  771.3 20.3 %collective-permute-done.110.theirs_ref = bf16[256,2048]{1,0:T(8,128)(2,1)S(1)} collective-permute-done((bf16[256,2048]{1,0:T(8,128)(2,1)S(1)}, bf16[256,2048]{1,0:T(8,128)(2,1)S(1)}, u32[]{:S(2)}, u32[]{:S(2)}) %collective-permute-start.110) | collective-permute-done | bytes 1048608 | tf_op jit(solution)/shard_map/ppermute | solution.py:23
  794.7 19.3 %collective-permute-done.109.theirs_ref = bf16[256,2048]{1,0:T(8,128)(2,1)S(1)} collective-permute-done((bf16[256,2048]{1,0:T(8,128)(2,1)S(1)}, bf16[256,2048]{1,0:T(8,128)(2,1)S(1)}, u32[]{:S(2)}, u32[]{:S(2)}) %collective-permute-start.109) | collective-permute-done | bytes 1048608 | tf_op jit(solution)/shard_map/ppermute | solution.py:23
  815.3 21.2 %collective-permute-done.104.theirs_ref = bf16[512,1024]{1,0:T(8,128)(2,1)S(1)} collective-permute-done((bf16[512,1024]{1,0:T(8,128)(2,1)S(1)}, bf16[512,1024]{1,0:T(8,128)(2,1)S(1)}, u32[]{:S(2)}, u32[]{:S(2)}) %collective-permute-start.104) | collective-permute-done | bytes 1048608 | tf_op jit(solution)/shard_map/ppermute | solution.py:23
  838.0 20.9 %collective-permute-done.103.theirs_ref = bf16[512,1024]{1,0:T(8,128)(2,1)S(1)} collective-permute-done((bf16[512,1024]{1,0:T(8,128)(2,1)S(1)}, bf16[512,1024]{1,0:T(8,128)(2,1)S(1)}, u32[]{:S(2)}, u32[]{:S(2)}) %collective-permute-start.103) | collective-permute-done | bytes 1048608 | tf_op jit(solution)/shard_map/ppermute | solution.py:23
  861.8 19.6 %collective-permute-done.102.theirs_ref = bf16[512,1024]{1,0:T(8,128)(2,1)S(1)} collective-permute-done((bf16[512,1024]{1,0:T(8,128)(2,1)S(1)}, bf16[512,1024]{1,0:T(8,128)(2,1)S(1)}, u32[]{:S(2)}, u32[]{:S(2)}) %collective-permute-start.102) | collective-permute-done | bytes 1048608 | tf_op jit(solution)/shard_map/ppermute | solution.py:23
  883.6 20.3 %collective-permute-done.101.theirs_ref = bf16[512,1024]{1,0:T(8,128)(2,1)S(1)} collective-permute-done((bf16[512,1024]{1,0:T(8,128)(2,1)S(1)}, bf16[512,1024]{1,0:T(8,128)(2,1)S(1)}, u32[]{:S(2)}, u32[]{:S(2)}) %collective-permute-start.101) | collective-permute-done | bytes 1048608 | tf_op jit(solution)/shard_map/ppermute | solution.py:23
  905.4 20.9 %collective-permute-done.108.theirs_ref = bf16[512,1024]{1,0:T(8,128)(2,1)S(1)} collective-permute-done((bf16[512,1024]{1,0:T(8,128)(2,1)S(1)}, bf16[512,1024]{1,0:T(8,128)(2,1)S(1)}, u32[]{:S(2)}, u32[]{:S(2)}) %collective-permute-start.108) | collective-permute-done | bytes 1048608 | tf_op jit(solution)/shard_map/ppermute | solution.py:23
  929.6 19.3 %collective-permute-done.107.theirs_ref = bf16[512,1024]{1,0:T(8,128)(2,1)S(1)} collective-permute-done((bf16[512,1024]{1,0:T(8,128)(2,1)S(1)}, bf16[512,1024]{1,0:T(8,128)(2,1)S(1)}, u32[]{:S(2)}, u32[]{:S(2)}) %collective-permute-start.107) | collective-permute-done | bytes 1048608 | tf_op jit(solution)/shard_map/ppermute | solution.py:23
  950.4 20.9 %collective-permute-done.106.theirs_ref = bf16[512,1024]{1,0:T(8,128)(2,1)S(1)} collective-permute-done((bf16[512,1024]{1,0:T(8,128)(2,1)S(1)}, bf16[512,1024]{1,0:T(8,128)(2,1)S(1)}, u32[]{:S(2)}, u32[]{:S(2)}) %collective-permute-start.106) | collective-permute-done | bytes 1048608 | tf_op jit(solution)/shard_map/ppermute | solution.py:23
  1020.9 16.9 %collective-permute-done.99.theirs_ref = bf16[2048,256]{1,0:T(8,128)(2,1)} collective-permute-done((bf16[2048,256]{1,0:T(8,128)(2,1)S(1)}, bf16[2048,256]{1,0:T(8,128)(2,1)}, u32[]{:S(2)}, u32[]{:S(2)}) %collective-permute-start.99) | collective-permute-done | bytes 1048608 | tf_op jit(solution)/shard_map/ppermute | solution.py:23
  (643 shorter events, 633.0 us)
Async XLA Ops:
  166.6 64.5 %collective-permute-start.19 = (bf16[512,1024]{1,0:T(8,128)(2,1)}, bf16[512,1024]{1,0:T(8,128)(2,1)}, u32[]{:S(2)}, u32[]{:S(2)}) collective-permute-start(bf16[512,1024]{1,0:T(8,128)(2,1)} %constant_dynamic-slice_fusion.11), channel_id=1, source_target_pairs={{0,4},{4,0},{1,5},{5,1},{2,6},{6,2},{3,7},{7,3},{8,12},{12,8},{9,1... | collective-permute-start | bytes 3145736 | tf_op jit(solution)/shard_map/ppermute | solution.py:23
  260.0 45.9 %collective-permute-start.24 = (bf16[256,2048]{1,0:T(8,128)(2,1)S(1)}, bf16[256,2048]{1,0:T(8,128)(2,1)S(1)}, u32[]{:S(2)}, u32[]{:S(2)}) collective-permute-start(bf16[256,2048]{1,0:T(8,128)(2,1)S(1)} %fusion.2), channel_id=1, source_target_pairs={{0,8},{24,16},{1,9},{25,17},{2,10},{26,18},{3,11},{27,19},{4,12},{... | collective-permute-start | bytes 3145736 | tf_op jit(solution)/shard_map/ppermute | solution.py:558
  261.3 84.9 %collective-permute-start.36 = (bf16[512,1024]{1,0:T(8,128)(2,1)}, bf16[512,1024]{1,0:T(8,128)(2,1)S(1)}, u32[]{:S(2)}, u32[]{:S(2)}) collective-permute-start(bf16[512,1024]{1,0:T(8,128)(2,1)} %get-tuple-element.253), channel_id=1, source_target_pairs={{0,4},{4,0},{1,5},{5,1},{2,6},{6,2},{3,7},{7,3},{8,12},{12,8},{9,1... | collective-permute-start | bytes 3145736 | tf_op jit(solution)/shard_map/ppermute | solution.py:23
  342.4 60.3 %collective-permute-start.84 = (bf16[512,256]{1,0:T(8,128)(2,1)}, bf16[512,256]{1,0:T(8,128)(2,1)S(1)}, u32[]{:S(2)}, u32[]{:S(2)}) collective-permute-start(bf16[512,256]{1,0:T(8,128)(2,1)} %constant_dynamic-slice_fusion), channel_id=1, source_target_pairs={{0,4},{4,0},{1,5},{5,1},{2,6},{6,2},{3,7},{7,3},{8,12},{12,8},{9,1... | collective-permute-start | bytes 786440 | tf_op jit(solution)/shard_map/ppermute | solution.py:23
  530.3 44.6 %collective-permute-start.68 = (bf16[512,1024]{1,0:T(8,128)(2,1)S(1)}, bf16[512,1024]{1,0:T(8,128)(2,1)S(1)}, u32[]{:S(2)}, u32[]{:S(2)}) collective-permute-start(bf16[512,1024]{1,0:T(8,128)(2,1)S(1)} %broadcast_select_fusion.11), channel_id=1, source_target_pairs={{0,8},{8,0},{16,24},{24,16},{1,9},{9,1},{17,25},{25,17},{2,10},{10... | collective-permute-start | bytes 3145736 | tf_op jit(solution)/shard_map/ppermute | solution.py:555
  722.1 47.0 %collective-permute-start.111 = (bf16[256,2048]{1,0:T(8,128)(2,1)S(1)}, bf16[256,2048]{1,0:T(8,128)(2,1)S(1)}, u32[]{:S(2)}, u32[]{:S(2)}) collective-permute-start(bf16[256,2048]{1,0:T(8,128)(2,1)S(1)} %broadcast_select_fusion.17.mine_ref), channel_id=1, source_target_pairs={{0,4},{4,0},{1,5},{5,1},{2,6},{6,2},{3,7},{7,3},{8,12},{12,8},{9,1... | collective-permute-start | bytes 3145736 | tf_op jit(solution)/shard_map/ppermute | solution.py:23
  722.6 68.9 %collective-permute-start.110 = (bf16[256,2048]{1,0:T(8,128)(2,1)S(1)}, bf16[256,2048]{1,0:T(8,128)(2,1)S(1)}, u32[]{:S(2)}, u32[]{:S(2)}) collective-permute-start(bf16[256,2048]{1,0:T(8,128)(2,1)S(1)} %broadcast_select_fusion.18.mine_ref), channel_id=1, source_target_pairs={{0,4},{4,0},{1,5},{5,1},{2,6},{6,2},{3,7},{7,3},{8,12},{12,8},{9,1... | collective-permute-start | bytes 3145736 | tf_op jit(solution)/shard_map/ppermute | solution.py:23
  734.5 58.6 %collective-permute-start.78 = (bf16[2048,256]{1,0:T(8,128)(2,1)S(1)}, bf16[2048,256]{1,0:T(8,128)(2,1)S(1)}, u32[]{:S(2)}, u32[]{:S(2)}) collective-permute-start(bf16[2048,256]{1,0:T(8,128)(2,1)S(1)} %add_convert_fusion.11), channel_id=1, source_target_pairs={{8,16},{16,8},{9,17},{17,9},{10,18},{18,10},{11,19},{19,11},{12,20... | collective-permute-start | bytes 3145736 | tf_op jit(solution)/shard_map/ppermute | solution.py:563
  746.6 67.4 %collective-permute-start.109 = (bf16[256,2048]{1,0:T(8,128)(2,1)S(1)}, bf16[256,2048]{1,0:T(8,128)(2,1)S(1)}, u32[]{:S(2)}, u32[]{:S(2)}) collective-permute-start(bf16[256,2048]{1,0:T(8,128)(2,1)S(1)} %broadcast_select_fusion.16.mine_ref), channel_id=1, source_target_pairs={{0,4},{4,0},{1,5},{5,1},{2,6},{6,2},{3,7},{7,3},{8,12},{12,8},{9,1... | collective-permute-start | bytes 3145736 | tf_op jit(solution)/shard_map/ppermute | solution.py:23
  769.1 67.4 %collective-permute-start.104 = (bf16[512,1024]{1,0:T(8,128)(2,1)S(1)}, bf16[512,1024]{1,0:T(8,128)(2,1)S(1)}, u32[]{:S(2)}, u32[]{:S(2)}) collective-permute-start(bf16[512,1024]{1,0:T(8,128)(2,1)S(1)} %broadcast_select_fusion.4.mine_ref), channel_id=1, source_target_pairs={{0,4},{4,0},{1,5},{5,1},{2,6},{6,2},{3,7},{7,3},{8,12},{12,8},{9,1... | collective-permute-start | bytes 3145736 | tf_op jit(solution)/shard_map/ppermute | solution.py:23
  770.6 88.3 %collective-permute-start.103 = (bf16[512,1024]{1,0:T(8,128)(2,1)S(1)}, bf16[512,1024]{1,0:T(8,128)(2,1)S(1)}, u32[]{:S(2)}, u32[]{:S(2)}) collective-permute-start(bf16[512,1024]{1,0:T(8,128)(2,1)S(1)} %broadcast_select_fusion.10.mine_ref), channel_id=1, source_target_pairs={{0,4},{4,0},{1,5},{5,1},{2,6},{6,2},{3,7},{7,3},{8,12},{12,8},{9,1... | collective-permute-start | bytes 3145736 | tf_op jit(solution)/shard_map/ppermute | solution.py:23
  791.6 89.9 %collective-permute-start.102 = (bf16[512,1024]{1,0:T(8,128)(2,1)S(1)}, bf16[512,1024]{1,0:T(8,128)(2,1)S(1)}, u32[]{:S(2)}, u32[]{:S(2)}) collective-permute-start(bf16[512,1024]{1,0:T(8,128)(2,1)S(1)} %broadcast_select_fusion.2.mine_ref), channel_id=1, source_target_pairs={{0,4},{4,0},{1,5},{5,1},{2,6},{6,2},{3,7},{7,3},{8,12},{12,8},{9,1... | collective-permute-start | bytes 3145736 | tf_op jit(solution)/shard_map/ppermute | solution.py:23
  793.1 89.9 %collective-permute-start.97 = (bf16[2048,256]{1,0:T(8,128)(2,1)S(1)}, bf16[2048,256]{1,0:T(8,128)(2,1)S(1)}, u32[]{:S(2)}, u32[]{:S(2)}) collective-permute-start(bf16[2048,256]{1,0:T(8,128)(2,1)S(1)} %add_convert_fusion), channel_id=1, source_target_pairs={{8,0},{16,24},{9,1},{17,25},{10,2},{18,26},{11,3},{19,27},{12,4},{... | collective-permute-start | bytes 3145736 | tf_op jit(solution)/shard_map/ppermute | solution.py:560
  814.0 46.5 %collective-permute-start.82 = (f32[40,128]{1,0:T(8,128)S(1)}, f32[40,128]{1,0:T(8,128)S(1)}, u32[]{:S(2)}, u32[]{:S(2)}) collective-permute-start(f32[40,128]{1,0:T(8,128)S(1)} %add.437), channel_id=1, source_target_pairs={{8,0},{16,24},{9,1},{17,25},{10,2},{18,26},{11,3},{19,27},{12,4},{... | collective-permute-start | bytes 61448 | tf_op jit(solution)/shard_map/ppermute | solution.py:560
  836.5 67.4 %collective-permute-start.101 = (bf16[512,1024]{1,0:T(8,128)(2,1)S(1)}, bf16[512,1024]{1,0:T(8,128)(2,1)S(1)}, u32[]{:S(2)}, u32[]{:S(2)}) collective-permute-start(bf16[512,1024]{1,0:T(8,128)(2,1)S(1)} %broadcast_select_fusion.8.mine_ref), channel_id=1, source_target_pairs={{0,4},{4,0},{1,5},{5,1},{2,6},{6,2},{3,7},{7,3},{8,12},{12,8},{9,1... | collective-permute-start | bytes 3145736 | tf_op jit(solution)/shard_map/ppermute | solution.py:23
  859.0 67.4 %collective-permute-start.108 = (bf16[512,1024]{1,0:T(8,128)(2,1)S(1)}, bf16[512,1024]{1,0:T(8,128)(2,1)S(1)}, u32[]{:S(2)}, u32[]{:S(2)}) collective-permute-start(bf16[512,1024]{1,0:T(8,128)(2,1)S(1)} %broadcast_select_fusion.1.mine_ref), channel_id=1, source_target_pairs={{0,4},{4,0},{1,5},{5,1},{2,6},{6,2},{3,7},{7,3},{8,12},{12,8},{9,1... | collective-permute-start | bytes 3145736 | tf_op jit(solution)/shard_map/ppermute | solution.py:23
  860.5 67.4 %collective-permute-start.81 = (bf16[2048,256]{1,0:T(8,128)(2,1)S(1)}, bf16[2048,256]{1,0:T(8,128)(2,1)S(1)}, u32[]{:S(2)}, u32[]{:S(2)}) collective-permute-start(bf16[2048,256]{1,0:T(8,128)(2,1)S(1)} %add_convert_fusion.10), channel_id=1, source_target_pairs={{8,0},{16,24},{9,1},{17,25},{10,2},{18,26},{11,3},{19,27},{12,4},{... | collective-permute-start | bytes 3145736 | tf_op jit(solution)/shard_map/ppermute | solution.py:560
  881.4 67.4 %collective-permute-start.107 = (bf16[512,1024]{1,0:T(8,128)(2,1)S(1)}, bf16[512,1024]{1,0:T(8,128)(2,1)S(1)}, u32[]{:S(2)}, u32[]{:S(2)}) collective-permute-start(bf16[512,1024]{1,0:T(8,128)(2,1)S(1)} %broadcast_select_fusion.7.mine_ref), channel_id=1, source_target_pairs={{0,4},{4,0},{1,5},{5,1},{2,6},{6,2},{3,7},{7,3},{8,12},{12,8},{9,1... | collective-permute-start | bytes 3145736 | tf_op jit(solution)/shard_map/ppermute | solution.py:23
  883.0 88.3 %collective-permute-start.106 = (bf16[512,1024]{1,0:T(8,128)(2,1)S(1)}, bf16[512,1024]{1,0:T(8,128)(2,1)S(1)}, u32[]{:S(2)}, u32[]{:S(2)}) collective-permute-start(bf16[512,1024]{1,0:T(8,128)(2,1)S(1)} %broadcast_select_fusion.mine_ref), channel_id=1, source_target_pairs={{0,4},{4,0},{1,5},{5,1},{2,6},{6,2},{3,7},{7,3},{8,12},{12,8},{9,1... | collective-permute-start | bytes 3145736 | tf_op jit(solution)/shard_map/ppermute | solution.py:23
  903.9 109.6 %collective-permute-start.105 = (bf16[512,1024]{1,0:T(8,128)(2,1)}, bf16[512,1024]{1,0:T(8,128)(2,1)}, u32[]{:S(2)}, u32[]{:S(2)}) collective-permute-start(bf16[512,1024]{1,0:T(8,128)(2,1)} %broadcast_select_fusion.6.mine_ref), channel_id=1, source_target_pairs={{0,4},{4,0},{1,5},{5,1},{2,6},{6,2},{3,7},{7,3},{8,12},{12,8},{9,1... | collective-permute-start | bytes 3145736 | tf_op jit(solution)/shard_map/ppermute | solution.py:23
  926.4 90.8 %collective-permute-start.100 = (bf16[256,2048]{1,0:T(8,128)(2,1)}, bf16[256,2048]{1,0:T(8,128)(2,1)}, u32[]{:S(2)}, u32[]{:S(2)}) collective-permute-start(bf16[256,2048]{1,0:T(8,128)(2,1)} %broadcast_select_fusion.15.mine_ref), channel_id=1, source_target_pairs={{0,4},{4,0},{1,5},{5,1},{2,6},{6,2},{3,7},{7,3},{8,12},{12,8},{9,1... | collective-permute-start | bytes 3145736 | tf_op jit(solution)/shard_map/ppermute | solution.py:23
  927.9 109.9 %collective-permute-start.99 = (bf16[2048,256]{1,0:T(8,128)(2,1)S(1)}, bf16[2048,256]{1,0:T(8,128)(2,1)}, u32[]{:S(2)}, u32[]{:S(2)}) collective-permute-start(bf16[2048,256]{1,0:T(8,128)(2,1)S(1)} %broadcast_select_fusion.14.mine_ref), channel_id=1, source_target_pairs={{0,4},{4,0},{1,5},{5,1},{2,6},{6,2},{3,7},{7,3},{8,12},{12,8},{9,1... | collective-permute-start | bytes 3145736 | tf_op jit(solution)/shard_map/ppermute | solution.py:23
  948.8 100.2 %collective-permute-start.98 = (bf16[2048,256]{1,0:T(8,128)(2,1)S(1)}, bf16[2048,256]{1,0:T(8,128)(2,1)}, u32[]{:S(2)}, u32[]{:S(2)}) collective-permute-start(bf16[2048,256]{1,0:T(8,128)(2,1)S(1)} %broadcast_select_fusion.12.mine_ref), channel_id=1, source_target_pairs={{0,4},{4,0},{1,5},{5,1},{2,6},{6,2},{3,7},{7,3},{8,12},{12,8},{9,1... | collective-permute-start | bytes 3145736 | tf_op jit(solution)/shard_map/ppermute | solution.py:23
  971.3 89.0 %collective-permute-start.83 = (bf16[2048,256]{1,0:T(8,128)(2,1)}, bf16[2048,256]{1,0:T(8,128)(2,1)}, u32[]{:S(2)}, u32[]{:S(2)}) collective-permute-start(bf16[2048,256]{1,0:T(8,128)(2,1)} %broadcast_select_fusion.13.mine_ref), channel_id=1, source_target_pairs={{0,4},{4,0},{1,5},{5,1},{2,6},{6,2},{3,7},{7,3},{8,12},{12,8},{9,1... | collective-permute-start | bytes 3145736 | tf_op jit(solution)/shard_map/ppermute | solution.py:23
  (203 other events, 6292.0 us)

commit v2 on v1

--- a/solution.py
+++ b/solution.py
@@ -40,10 +40,28 @@
     return [parts[o] for o in range(len(parts))]
 
 
-def gather_both(own, axis):
-    mine = gather_rows(own, axis)
-    theirs = gather_rows(flip(own, "ctx", 1), axis)
-    return jnp.concatenate(mine, axis=0), jnp.concatenate(theirs, axis=0)
+def gather_both(own, axis, early=None):
+    swapped = flip(own, "ctx", 1)
+    mine, theirs = {0: own}, {0: swapped}
+    for far, distance in enumerate(reversed(distances(axis))):
+        for o in list(mine):
+            mine[o ^ distance] = flip(mine[o], axis, distance)
+            if far == 0 and distance > 1:
+                rows = own.shape[0] // 2
+                theirs[o ^ distance] = jnp.concatenate(
+                    [
+                        flip(theirs[o][:rows], axis, distance),
+                        flip(mine[o ^ distance][rows:], "ctx", 1),
+                    ],
+                    axis=0,
+                )
+            else:
+                theirs[o ^ distance] = flip(theirs[o], axis, distance)
+    return [mine[o] for o in range(len(mine))], [theirs[o] for o in range(len(theirs))]
+
+
+def stacked(blocks):
+    return jnp.concatenate(blocks, axis=0)
 
 
 def scatter_rows(blocks, axis):
@@ -92,15 +110,65 @@
     return values * cosine + pltpu.roll(values, HD // 2, 1) * sine
 
 
+def project_kernel(*refs, blocks, square, plain):
+    rows_ref = refs[blocks + square + plain]
+    outs = refs[blocks + square + plain + 1 :]
+    weights = refs[blocks : blocks + square + plain]
+
+    @pl.when(pl.program_id(0) == 0)
+    def _():
+        rows = refs[0].shape[0]
+        for o in range(blocks):
+            rows_ref[o * rows : (o + 1) * rows, :] = refs[o][...]
+        for sum_ref in outs[square + plain :]:
+            sum_ref[...] = jnp.zeros_like(sum_ref)
+
+    for k in range(square + plain):
+        product = jnp.dot(rows_ref[...], weights[k][...], preferred_element_type=jnp.float32)
+        outs[k][...] = product.astype(outs[k].dtype)
+        if k < square:
+            outs[square + plain + k][...] += jnp.sum(product * product, axis=1, keepdims=True)
+
+
+def project(blocks, square, plain):
+    rows, depth = blocks[0].shape
+    count = len(blocks)
+    width = square[0].shape[1]
+    wide = min(256, width)
+    whole = pl.BlockSpec((count * rows, depth), lambda i: (0, 0))
+    column = pl.BlockSpec((depth, wide), lambda i: (0, i))
+    product = pl.BlockSpec((count * rows, wide), lambda i: (0, i))
+    sums = pl.BlockSpec((count * rows, 1), lambda i: (0, 0))
+    return pl.pallas_call(
+        functools.partial(project_kernel, blocks=count, square=len(square), plain=len(plain)),
+        grid=(width // wide,),
+        in_specs=[pl.BlockSpec((rows, depth), lambda i: (0, 0))] * count
+        + [column] * (len(square) + len(plain)),
+        out_specs=[whole] + [product] * (len(square) + len(plain)) + [sums] * len(square),
+        out_shape=[jax.ShapeDtypeStruct((count * rows, depth), jnp.bfloat16)]
+        + [jax.ShapeDtypeStruct((count * rows, width), jnp.float32)] * len(square)
+        + [jax.ShapeDtypeStruct((count * rows, width), jnp.bfloat16)] * len(plain)
+        + [jax.ShapeDtypeStruct((count * rows, 1), jnp.float32)] * len(square),
+        name="project",
+    )(*blocks, *square, *plain)
+
+
 def attend_kernel(
-    query_ref, key_ref, value_ref, inv_query_ref, inv_key_ref, gain_query_ref, gain_key_ref,
+    query_ref, key_ref, key_other_ref, value_own_ref, value_other_ref,
+    inv_query_ref, inv_key_ref, gain_query_ref, gain_key_ref,
     cos_query_ref, sin_query_ref, cos_key_ref, sin_key_ref, at_query_ref, at_key_ref,
-    query_low_ref, key_low_ref, mixed_ref, lse_ref,
+    query_low_ref, key_low_ref, value_ref, mixed_ref, lse_ref,
 ):
     @pl.when(pl.program_id(1) == 0)
     def _():
-        scaled = key_ref[...] * inv_key_ref[...] * gain_key_ref[...]
-        key_low_ref[...] = turned(scaled, cos_key_ref[...], sin_key_ref[...]).astype(jnp.bfloat16)
+        half = key_ref.shape[0]
+        value_ref[:half] = value_own_ref[...]
+        value_ref[half:] = value_other_ref[...]
+        for side, ref in ((slice(0, half), key_ref), (slice(half, 2 * half), key_other_ref)):
+            scaled = ref[...] * inv_key_ref[side] * gain_key_ref[...]
+            key_low_ref[side] = turned(scaled, cos_key_ref[side], sin_key_ref[side]).astype(
+                jnp.bfloat16
+            )
 
     scaled = query_ref[...] * inv_query_ref[...] * gain_query_ref[...]
     query_low = turned(scaled, cos_query_ref[...], sin_query_ref[...]).astype(jnp.bfloat16)
@@ -174,28 +242,30 @@
     return spec
 
 
-def attend(query, key, value, inv_query, inv_key, gain_query, gain_key, turns, block_rows):
+def attend(query, keys, values, inv_query, inv_key, gain_query, gain_key, turns, block_rows):
     half_rows, width = query.shape
-    key_rows = key.shape[0]
+    key_rows = 2 * half_rows
     heads = width // HD
     s = attention_specs(half_rows, key_rows, block_rows)
     return pl.pallas_call(
         attend_kernel,
         grid=(heads, half_rows // block_rows),
         in_specs=[
-            s["query"], s["key"], s["key"], s["query_column"], s["key_column"], s["gain"], s["gain"],
+            s["query"], s["half"], s["half"], s["half"], s["half"],
+            s["query_column"], s["key_column"], s["gain"], s["gain"],
             s["query_turn"], s["query_turn"], s["key_turn"], s["key_turn"],
             s["query_column"], s["key_row"],
         ],
-        out_specs=[s["query"], s["key"], s["query"], s["lse"]],
+        out_specs=[s["query"], s["key"], s["key"], s["query"], s["lse"]],
         out_shape=[
             jax.ShapeDtypeStruct(query.shape, jnp.bfloat16),
-            jax.ShapeDtypeStruct(key.shape, jnp.bfloat16),
+            jax.ShapeDtypeStruct((key_rows, width), jnp.bfloat16),
+            jax.ShapeDtypeStruct((key_rows, width), jnp.bfloat16),
             jax.ShapeDtypeStruct(query.shape, jnp.bfloat16),
             jax.ShapeDtypeStruct((heads, half_rows, 1), jnp.float32),
         ],
         name="attend",
-    )(query, key, value, inv_query, inv_key, gain_query, gain_key, *turns)
+    )(query, *keys, *values, inv_query, inv_key, gain_query, gain_key, *turns)
 
 
 def attend_back(query_low, key_low, value, grad, lse, turns, block_rows):
@@ -349,12 +419,12 @@
     sine = jnp.sin(angles) * jnp.where(lane < HD // 2, -1.0, 1.0)[None, :]
     turns = (cosine, sine, cosine, sine, at_query[:, None], at_key[None, :])
 
-    tokens_own, tokens_other = gather_both(tokens, "seq")
-    tokens_both = jnp.concatenate([tokens_own, tokens_other], axis=0)
-    query_proj = jnp.dot(tokens_own, w_query, preferred_element_type=jnp.float32)
-    key_proj = jnp.dot(tokens_both, w_key, preferred_element_type=jnp.float32)
-    value_low = jnp.dot(tokens_both, w_value, preferred_element_type=jnp.float32).astype(
-        jnp.bfloat16
+    own_blocks, other_blocks = gather_both(tokens, "seq")
+    tokens_own, query_proj, key_proj, value_own, sq_query, sq_key = project(
+        own_blocks, (w_query, w_key), (w_value,)
+    )
+    tokens_other, key_other, value_other, sq_key_other = project(
+        other_blocks, (w_key,), (w_value,)
     )
 
     def common_rows(parts):
@@ -364,37 +434,35 @@
     def own_rows(sums):
         return jnp.take(sums, owners, axis=1).reshape(sums.shape[0], half_rows)
 
-    sq_key = jnp.sum(key_proj * key_proj, axis=1)
-    sums = own_rows(
-        lax.psum(
-            common_rows(
-                (jnp.sum(query_proj * query_proj, axis=1), sq_key[:half_rows], sq_key[half_rows:])
-            ),
-            "seq",
-        )
-    )
+    sums = own_rows(lax.psum(common_rows((sq_query, sq_key, sq_key_other)), "seq"))
     inv_query = lax.rsqrt(sums[0] / D + EPS)[:, None]
     inv_key_both = lax.rsqrt(sums[1:].reshape(2 * half_rows) / D + EPS)[:, None]
     inv_key = inv_key_both[:half_rows]
-    query_low, key_low, attn_low, lse = attend(
-        query_proj, key_proj, value_low, inv_query, inv_key_both, gain_query[None, :],
+    query_low, key_low, value_low, attn_low, lse = attend(
+        query_proj, (key_proj, key_other), (value_own, value_other), inv_query, inv_key_both, gain_query[None, :],
         gain_key[None, :], turns, block_rows,
     )
 
     def to_owners(partial):
         return scatter_rows(row_blocks(partial, seq_count), "seq")
 
+    attn_halves = swap_halves(attn_low)
     attn_proj = to_owners(jnp.dot(attn_low, w_out, preferred_element_type=jnp.float32))
-    attn_halves = swap_halves(attn_low)
+    attn_proj, attn_halves = lax.optimization_barrier((attn_proj, attn_halves))
     inv_attn = lax.rsqrt(jnp.mean(attn_proj * attn_proj, axis=1, keepdims=True) + EPS)
     attn_unit = attn_proj * inv_attn
     hidden = tokens.astype(jnp.float32) + attn_unit * gain_attn
-    hidden_own, hidden_other = gather_both(hidden.astype(jnp.bfloat16), "seq")
+    hidden_low = hidden.astype(jnp.bfloat16)
+    hidden_own = stacked(gather_rows(hidden_low, "seq"))
+    hidden_flip = flip(hidden_low, "ctx", 1)
+    hidden_own, hidden_flip = lax.optimization_barrier((hidden_own, hidden_flip))
+    hidden_rest = gather_rows(hidden_flip, "seq")
     gate_proj = jnp.dot(hidden_own, w_gate, preferred_element_type=jnp.float32)
     up_proj = jnp.dot(hidden_own, w_up, preferred_element_type=jnp.float32)
     gate_sig = jax.nn.sigmoid(gate_proj)
     swish = gate_proj * gate_sig
     inner_low = (swish * up_proj).astype(jnp.bfloat16)
+    inner_low, hidden_rest = lax.optimization_barrier((inner_low, hidden_rest))
     inner_halves = swap_halves(inner_low)
     ffn = to_owners(jnp.dot(inner_low, w_down, preferred_element_type=jnp.float32))
     inv_ffn = lax.rsqrt(jnp.mean(ffn * ffn, axis=1, keepdims=True) + EPS)
@@ -408,7 +476,9 @@
     grad_out = cotangent.astype(jnp.float32) * picked
     gain_ffn_part = jnp.sum(grad_out * ffn_unit, axis=0)
     grad_ffn_low = norm_back(ffn_unit, inv_ffn, grad_out * gain_ffn).astype(jnp.bfloat16)
-    grad_ffn_own, grad_ffn_other = gather_both(grad_ffn_low, "seq")
+    grad_ffn_low, inner_halves = lax.optimization_barrier((grad_ffn_low, inner_halves))
+    grad_ffn_own, grad_ffn_other = map(stacked, gather_both(grad_ffn_low, "seq"))
+    hidden_other = stacked(hidden_rest)
 
     grads = {
         "down": Gradient("down", w_down.shape, CHUNKS, True),
@@ -430,23 +500,25 @@
         grad_up = (grad_inner * swish).astype(jnp.bfloat16)
         grad_gate, grad_up = yield (grad_gate, grad_up)
         gate_halves = swap_halves(grad_gate)
+        sides["gate"] = (hidden_own, hidden_other, *gate_halves)
+        gate_share = times_transpose(grad_gate, w_gate)
+        gate_share, grad_up = yield (gate_share, grad_up)
         up_halves = swap_halves(grad_up)
-        partial = times_transpose(grad_gate, w_gate) + times_transpose(grad_up, w_up)
+        sides["up"] = (hidden_own, hidden_other, *up_halves)
+        partial = gate_share + times_transpose(grad_up, w_up)
         (partial,) = yield (partial,)
         grad_hidden = grad_out + to_owners(partial)
         (grad_hidden,) = yield (grad_hidden,)
         gain_attn_part = jnp.sum(grad_hidden * attn_unit, axis=0)
         grad_proj_low = norm_back(attn_unit, inv_attn, grad_hidden * gain_attn).astype(jnp.bfloat16)
-        grad_proj_own, grad_proj_other = gather_both(grad_proj_low, "seq")
-        grad_proj_own, grad_proj_other, *gate_halves = yield (
-            grad_proj_own, grad_proj_other, *gate_halves
-        )
-        sides["gate"] = (hidden_own, hidden_other, *gate_halves)
-        sides["out"] = (*attn_halves, grad_proj_own, grad_proj_other)
+        grad_proj_flip = flip(grad_proj_low, "ctx", 1)
+        grad_proj_own = stacked(gather_rows(grad_proj_low, "seq"))
+        grad_proj_own, grad_proj_flip = yield (grad_proj_own, grad_proj_flip)
+        grad_proj_rest = gather_rows(grad_proj_flip, "seq")
         grad_attn_low = times_transpose(grad_proj_own, w_out).astype(jnp.bfloat16)
         backs = attend_back(query_low, key_low, value_low, grad_attn_low, lse, turns, block_rows)
-        *backs, up_own, up_other = yield (*backs, *up_halves)
-        sides["up"] = (hidden_own, hidden_other, up_own, up_other)
+        backs, grad_proj_rest = yield (backs, grad_proj_rest)
+        sides["out"] = (*attn_halves, grad_proj_own, stacked(grad_proj_rest))
         grad_query_norm, own_dk, own_dv, prev_dk, prev_dv = backs
         back_dk, back_dv = lax.ppermute((prev_dk, prev_dv), "ctx", [(1, 0)])
         grad_query_norm, own_dk, own_dv, back_dk, back_dv = yield (
@@ -455,7 +527,7 @@
         grad_value_low = (own_dv + back_dv.astype(jnp.float32)).astype(jnp.bfloat16)
         grad_key_norm = own_dk + back_dk.astype(jnp.float32)
         query_unit = query_proj * inv_query
-        key_unit = key_proj[:half_rows] * inv_key
+        key_unit = key_proj * inv_key
         gain_query_part = jnp.sum(grad_query_norm * query_unit, axis=0)
         gain_key_part = jnp.sum(grad_key_norm * key_unit, axis=0)
         query_scaled = grad_query_norm * gain_query
@@ -486,18 +558,16 @@
         value_halves = swap_halves(grad_value_low)
         key_halves = swap_halves(grad_key_low)
         query_halves = swap_halves(grad_query_low)
+        sides["value"] = (tokens_own, tokens_other, *value_halves)
+        sides["key"] = (tokens_own, tokens_other, *key_halves)
+        sides["query"] = (tokens_own, tokens_other, *query_halves)
         gains = gains + flip(gains, "ctx", 1)
         partial = (
             times_transpose(grad_query_low, w_query)
             + times_transpose(grad_key_low, w_key)
             + times_transpose(grad_value_low, w_value)
         )
-        partial, gains, *halves = yield (
-            partial, gains, *value_halves, *key_halves, *query_halves
-        )
-        sides["value"] = (tokens_own, tokens_other, *halves[0:2])
-        sides["key"] = (tokens_own, tokens_other, *halves[2:4])
-        sides["query"] = (tokens_own, tokens_other, *halves[4:6])
+        partial, gains = yield (partial, gains)
         results["gains"] = gains
         grad_tokens = grad_hidden + to_owners(partial)
         (grad_tokens,) = yield (grad_tokens,)
@@ -512,6 +582,7 @@
     got_pair, got_across, got_half = {}, {}, {}
     main = stages()
     state = next(main)
+    last_name, last_buffer = None, None
 
     def rides(index):
         return (results["gains"],) if index == rider else ()
@@ -528,18 +599,25 @@
                 total[before - 2 * step],
                 got_pair[before][0],
             )
-        if before - 3 * step in part:
-            name, index = plan[before - 3 * step]
-            grads[name].store(index, final[before - 3 * step][0], got_half[before])
-        if tick < count:
-            name, index = plan[tick]
-            part[tick] = (grads[name].part(sides[name], index),) + rides(tick)
+        stored = before - 3 * step
+        arrived = got_half.get(before)
+        if tick == 0:
+            part[0] = (grads[plan[0][0]].part(sides[plan[0][0]], 0),)
         entering = part.get(tick)
         leaving = total.get(tick - 2 * step)
         crossing = pair.get(tick - step)
         swapping = final.get(tick - 3 * step)
-        held = (entering, leaving, crossing, swapping, state)
-        entering, leaving, crossing, swapping, state = lax.optimization_barrier(held)
+        coming = sides.get(plan[tick + 1][0]) if tick + 1 < count else None
+        held = (entering, leaving, crossing, swapping, state, arrived, coming, last_buffer)
+        entering, leaving, crossing, swapping, state, arrived, coming, last_buffer = (
+            lax.optimization_barrier(held)
+        )
+        if last_name:
+            grads[last_name].buffer = last_buffer
+        if stored in part:
+            last_name, index = plan[stored]
+            grads[last_name].store(index, final[stored][0], arrived)
+            last_buffer = grads[last_name].buffer
         if entering is not None:
             part[tick] = entering
         if leaving is not None:
@@ -567,6 +645,10 @@
             state = main.send(state)
         except StopIteration:
             state = ()
+        if tick + 1 < count:
+            name, index = plan[tick + 1]
+            coming = sides[name] if coming is None else coming
+            part[tick + 1] = (grads[name].part(coming, index),) + rides(tick + 1)
 
     gains = final[rider][1].reshape(-1)
     grad_gain_attn = gains[:D]

time: 1070 us -> 875 us (0.82)
  waiting for transfers between devices: 578 us -> 326 us
  other arithmetic: 48.1 us -> 121 us
  matrix products: 132 us -> 108 us
  local copies, waits for them, and re-layouts: 43.4 us -> 28.1 us
  Pallas kernels: 81.8 us -> 96.9 us
    ppermute x64 -> x66, waiting for transfers between devices: 351 us -> 227 us  [flip(): lax.ppermute(value, axis, [(place, place ^ distance) for place in range(c...]
    ppermute x13, waiting for transfers between devices: 74.2 us -> 17 us  [body(): lax.ppermute(v, 'dp', [(1, 0), (2, 3)])]
    ppermute x4, waiting for transfers between devices: 66.5 us -> 18.8 us  [body(): lax.ppermute(v, 'dp', pairs)]
    convert_element_type x32, other arithmetic: 20.2 us -> 60.2 us  [added(): (left.astype(jnp.float32) + right.astype(jnp.float32)).astype(left.dtype)]
    ppermute x13, waiting for transfers between devices: 87.1 us -> 54.3 us  [body(): lax.ppermute(v, 'dp', [(0, 1), (3, 2)])]
    select_n x17, other arithmetic: 6.37 us -> 27.3 us  [body(): jnp.where(middle, kept, got)]
    unnamed x241 -> x231, local copies, waits for them, and re-layouts: 25 us -> 9.51 us
    dot_general x3 -> x0, matrix products: 15 us -> none  [the longest x1 6.19 us: body(): jnp.dot(tokens_both, w_value, preferred_element_type=jnp.float32)]
  transfers between devices with their start and end apart: 113 -> 115, of which waited for: 48 -> 39; matrix products, arithmetic and copies ran while one was open for 13% -> 26% of each run, Pallas kernels for 6% -> 9%
where the time goes in v2:
time: 875 us; the launch traced here: 868 us
  waiting for transfers between devices  326 us (37%)
  starting transfers between devices  166 us (19%)
  other arithmetic  121 us (14%)
  matrix products  108 us (12%)
  Pallas kernels  96.9 us (11%)
  local copies, waits for them, and re-layouts  28.1 us (3%)
  blocking collectives  17.9 us (2%)
    ppermute x66, waiting for transfers between devices, flip(): lax.ppermute(value, axis, [(place, place ^ distance) for place in range(c...  227 us
    ppermute x13, starting transfers between devices, body(): lax.ppermute(v, 'dp', [(0, 1), (3, 2)])  71.5 us
    convert_element_type x32, other arithmetic, added(): (left.astype(jnp.float32) + right.astype(jnp.float32)).astype(left.dtype)  60.2 us
    pallas_call x16, Pallas kernels, store_chunk(): pl.pallas_call(store_kernel, grid_spec=pltpu.PrefetchScalarGridSpec(num_s...  59.8 us
    ppermute x13, waiting for transfers between devices, body(): lax.ppermute(v, 'dp', [(0, 1), (3, 2)])  54.3 us
    dot_general x32, matrix products, contract_rows(): lax.dot_general(left, right, (((0,), (0,)), ((), ())), preferred_element_...  53.7 us
    ppermute x66, starting transfers between devices, flip(): lax.ppermute(value, axis, [(place, place ^ distance) for place in range(c...  47.3 us
    dot_general x7, matrix products, times_transpose(): lax.dot_general(left, right, (((1,), (1,)), ((), ())), preferred_element_...  31.9 us
  transfers between devices with their start and end apart: 115, of which 39 were waited for; matrix products, arithmetic and copies ran while one was open for 26% of the time, Pallas kernels for 9%

profile of v2, /device:TPU:0, one launch (start us, length us, event | category | flops | bytes accessed | tf_op | source)
XLA Modules:
  0.0 868.0 jit_solution(14143249164513448002)
XLA Ops:
  5.3 10.6 %collective-permute-done.3.refs_0_ = bf16[128,2048]{1,0:T(8,128)(2,1)S(1)} collective-permute-done((bf16[128,2048]{1,0:T(8,128)(2,1)}, bf16[128,2048]{1,0:T(8,128)(2,1)S(1)}, u32[]{:S(2)}, u32[]{:S(2)}) %collective-permute-start.3) | collective-permute-done | bytes 524320 | tf_op jit(solution)/shard_map/ppermute | solution.py:23
  57.5 11.8 %attend.1 = (bf16[512,512]{1,0:T(8,128)(2,1)}, bf16[1024,512]{1,0:T(8,128)(2,1)}, bf16[1024,512]{1,0:T(8,128)(2,1)}, bf16[512,512]{1,0:T(8,128)(2,1)}, f32[4,512,1]{2,1,0:T(8,128)}) custom-call(f32[512,512]{1,0:T(8,128)} %get-tuple-element.236.query_ref, f32[512,512]{1,0:T(8,128)} %get-tuple-element.237.key_ref, ...), custom_call_target="tpu_custom_call" | custom-call | tf_op jit(solution)/shard_map/attend/pallas_call | solution.py:250
  77.8 11.1 %collective-permute-done.10 = bf16[128,2048]{1,0:T(8,128)(2,1)} collective-permute-done((bf16[128,2048]{1,0:T(8,128)(2,1)}, bf16[128,2048]{1,0:T(8,128)(2,1)}, u32[]{:S(2)}, u32[]{:S(2)}) %collective-permute-start.10) | collective-permute-done | bytes 524320 | tf_op jit(solution)/shard_map/ppermute | solution.py:23
  92.0 12.2 %collective-permute-done.13 = bf16[128,2048]{1,0:T(8,128)(2,1)S(1)} collective-permute-done((bf16[128,2048]{1,0:T(8,128)(2,1)S(1)}, bf16[128,2048]{1,0:T(8,128)(2,1)S(1)}, u32[]{:S(2)}, u32[]{:S(2)}) %collective-permute-start.13) | collective-permute-done | bytes 524320 | tf_op jit(solution)/shard_map/ppermute | solution.py:23
  106.4 12.2 %collective-permute-done.15 = bf16[128,2048]{1,0:T(8,128)(2,1)S(1)} collective-permute-done((bf16[128,2048]{1,0:T(8,128)(2,1)S(1)}, bf16[128,2048]{1,0:T(8,128)(2,1)S(1)}, u32[]{:S(2)}, u32[]{:S(2)}) %collective-permute-start.15) | collective-permute-done | bytes 524320 | tf_op jit(solution)/shard_map/ppermute | solution.py:23
  154.4 9.8 %collective-permute-done.21 = bf16[128,2048]{1,0:T(8,128)(2,1)S(1)} collective-permute-done((bf16[128,2048]{1,0:T(8,128)(2,1)S(1)}, bf16[128,2048]{1,0:T(8,128)(2,1)S(1)}, u32[]{:S(2)}, u32[]{:S(2)}) %collective-permute-start.21) | collective-permute-done | bytes 524320 | tf_op jit(solution)/shard_map/ppermute | solution.py:23
  180.5 9.8 %collective-permute-done.26 = bf16[128,2048]{1,0:T(8,128)(2,1)S(1)} collective-permute-done((bf16[128,2048]{1,0:T(8,128)(2,1)S(1)}, bf16[128,2048]{1,0:T(8,128)(2,1)S(1)}, u32[]{:S(2)}, u32[]{:S(2)}) %collective-permute-start.26) | collective-permute-done | bytes 524320 | tf_op jit(solution)/shard_map/ppermute | solution.py:23
  198.7 11.8 %multiply_convert_fusion = (bf16[512,2048]{1,0:T(8,128)(2,1)}, bf16[512,2048]{1,0:T(8,128)(2,1)}) fusion(f32[512,2048]{1,0:T(8,128)} %copy-done.105, f32[512,2048]{1,0:T(8,128)} %get-tuple-element.509, bf16[512,2048]{1,0:T(8,128)(2,1)S(1)} %constant_dynamic-update-slice_fusion.2, bf16[2048,2048]{1,0:T(8,128)(2,1)} %param.29), kind=kOutput, calls=%fused_computation.5 | convolution fusion | flops 4308598784 | bytes 23068672 | tf_op jit(solution)/shard_map/dot_general | solution.py:94
  258.0 15.5 %collective-permute-done.32 = bf16[256,2048]{1,0:T(8,128)(2,1)S(1)} collective-permute-done((bf16[256,2048]{1,0:T(8,128)(2,1)S(1)}, bf16[256,2048]{1,0:T(8,128)(2,1)S(1)}, u32[]{:S(2)}, u32[]{:S(2)}) %collective-permute-start.32) | collective-permute-done | bytes 1048608 | tf_op jit(solution)/shard_map/ppermute | solution.py:636
  277.3 18.2 %collective-permute-done.38 = bf16[256,2048]{1,0:T(8,128)(2,1)S(1)} collective-permute-done((bf16[256,2048]{1,0:T(8,128)(2,1)S(1)}, bf16[256,2048]{1,0:T(8,128)(2,1)S(1)}, u32[]{:S(2)}, u32[]{:S(2)}) %collective-permute-start.38) | collective-permute-done | bytes 1048608 | tf_op jit(solution)/shard_map/ppermute | solution.py:636
  299.4 9.6 %collective-permute-done.35 = bf16[128,2048]{1,0:T(8,128)(2,1)S(1)} collective-permute-done((bf16[128,2048]{1,0:T(8,128)(2,1)S(1)}, bf16[128,2048]{1,0:T(8,128)(2,1)S(1)}, u32[]{:S(2)}, u32[]{:S(2)}) %collective-permute-start.35) | collective-permute-done | bytes 524320 | tf_op jit(solution)/shard_map/ppermute | solution.py:23
  341.3 9.4 %collective-permute-start.49 = (bf16[512,1024]{1,0:T(8,128)(2,1)S(1)}, bf16[512,1024]{1,0:T(8,128)(2,1)}, u32[]{:S(2)}, u32[]{:S(2)}) collective-permute-start(bf16[512,1024]{1,0:T(8,128)(2,1)S(1)} %add_convert_fusion.37), channel_id=1, source_target_pairs={{0,8},{24,16},{1,9},{25,17},{2,10},{26,18},{3,11},{27,19},{4,12},{... | collective-permute-start | bytes 3145736 | tf_op jit(solution)/shard_map/ppermute | solution.py:636
  355.4 11.0 %attend_back.1 = (f32[512,512]{1,0:T(8,128)}, f32[512,512]{1,0:T(8,128)}, f32[512,512]{1,0:T(8,128)}, bf16[512,512]{1,0:T(8,128)(2,1)}, bf16[512,512]{1,0:T(8,128)(2,1)}) custom-call(bf16[512,512]{1,0:T(8,128)(2,1)} %get-tuple-element.288.query_low_ref, bf16[1024,512]{1,0:T(8,128)(2,1)} %get-tuple-element.289.key_low_ref, ...), custom_call_target="tpu_custom_call" | custom-call | tf_op jit(solution)/shard_map/attend_back/pallas_call | solution.py:277
  408.8 10.6 %all-reduce = (f32[2,4,128]{2,0,1:T(2,128)S(1)}, f32[4096]{0:T(1024)S(1)}) all-reduce(f32[2,4,128]{2,0,1:T(2,128)S(1)} %select_bitcast_fusion.3, f32[4096]{0:T(1024)S(1)} %pad_maximum_fusion.4), channel_id=1, replica_groups=mesh['dp'=4,'ctx'=2,'seq'=4] {'seq'}, use_global_device_ids=true, to_apply=%region_8.11 | all-reduce | flops 5120 | bytes 40960 | tf_op jit(solution)/shard_map/psum | solution.py:535
  454.5 9.4 %collective-permute-done.60 = f32[40,128]{1,0:T(8,128)S(1)} collective-permute-done((f32[40,128]{1,0:T(8,128)S(1)}, f32[40,128]{1,0:T(8,128)S(1)}, u32[]{:S(2)}, u32[]{:S(2)}) %collective-permute-start.60) | collective-permute-done | bytes 20512 | tf_op jit(solution)/shard_map/ppermute | solution.py:23
  512.3 10.4 %collective-permute-done.70 = bf16[512,1024]{1,0:T(8,128)(2,1)S(1)} collective-permute-done((bf16[512,1024]{1,0:T(8,128)(2,1)S(1)}, bf16[512,1024]{1,0:T(8,128)(2,1)S(1)}, u32[]{:S(2)}, u32[]{:S(2)}) %collective-permute-start.70) | collective-permute-done | bytes 1048608 | tf_op jit(solution)/shard_map/ppermute | solution.py:633
  588.4 9.3 %collective-permute-start.84 = (bf16[256,2048]{1,0:T(8,128)(2,1)}, bf16[256,2048]{1,0:T(8,128)(2,1)}, u32[]{:S(2)}, u32[]{:S(2)}) collective-permute-start(bf16[256,2048]{1,0:T(8,128)(2,1)} %fusion.5), channel_id=1, source_target_pairs={{0,8},{24,16},{1,9},{25,17},{2,10},{26,18},{3,11},{27,19},{4,12},{... | collective-permute-start | bytes 3145736 | tf_op jit(solution)/shard_map/ppermute | solution.py:636
  624.1 17.0 %collective-permute-done.85 = bf16[512,1024]{1,0:T(8,128)(2,1)S(1)} collective-permute-done((bf16[512,1024]{1,0:T(8,128)(2,1)S(1)}, bf16[512,1024]{1,0:T(8,128)(2,1)S(1)}, u32[]{:S(2)}, u32[]{:S(2)}) %collective-permute-start.85) | collective-permute-done | bytes 1048608 | tf_op jit(solution)/shard_map/ppermute | solution.py:638
  721.3 15.5 %collective-permute-done.96.theirs_ref = bf16[512,1024]{1,0:T(8,128)(2,1)S(1)} collective-permute-done((bf16[512,1024]{1,0:T(8,128)(2,1)}, bf16[512,1024]{1,0:T(8,128)(2,1)S(1)}, u32[]{:S(2)}, u32[]{:S(2)}) %collective-permute-start.96) | collective-permute-done | bytes 1048608 | tf_op jit(solution)/shard_map/ppermute | solution.py:23
  745.7 10.9 %collective-permute-done.107.theirs_ref = bf16[512,1024]{1,0:T(8,128)(2,1)} collective-permute-done((bf16[512,1024]{1,0:T(8,128)(2,1)}, bf16[512,1024]{1,0:T(8,128)(2,1)}, u32[]{:S(2)}, u32[]{:S(2)}) %collective-permute-start.107) | collective-permute-done | bytes 1048608 | tf_op jit(solution)/shard_map/ppermute | solution.py:23
  768.5 14.2 %collective-permute-done.104.theirs_ref = bf16[512,1024]{1,0:T(8,128)(2,1)} collective-permute-done((bf16[512,1024]{1,0:T(8,128)(2,1)S(1)}, bf16[512,1024]{1,0:T(8,128)(2,1)}, u32[]{:S(2)}, u32[]{:S(2)}) %collective-permute-start.104) | collective-permute-done | bytes 1048608 | tf_op jit(solution)/shard_map/ppermute | solution.py:23
  791.1 14.1 %collective-permute-done.112.theirs_ref = bf16[256,2048]{1,0:T(8,128)(2,1)} collective-permute-done((bf16[256,2048]{1,0:T(8,128)(2,1)S(1)}, bf16[256,2048]{1,0:T(8,128)(2,1)}, u32[]{:S(2)}, u32[]{:S(2)}) %collective-permute-start.112) | collective-permute-done | bytes 1048608 | tf_op jit(solution)/shard_map/ppermute | solution.py:23
  810.5 17.1 %collective-permute-done.110.theirs_ref = bf16[2048,256]{1,0:T(8,128)(2,1)} collective-permute-done((bf16[2048,256]{1,0:T(8,128)(2,1)}, bf16[2048,256]{1,0:T(8,128)(2,1)}, u32[]{:S(2)}, u32[]{:S(2)}) %collective-permute-start.110) | collective-permute-done | bytes 1048608 | tf_op jit(solution)/shard_map/ppermute | solution.py:23
  831.6 18.4 %collective-permute-done.114.theirs_ref = bf16[2048,256]{1,0:T(8,128)(2,1)S(1)} collective-permute-done((bf16[2048,256]{1,0:T(8,128)(2,1)S(1)}, bf16[2048,256]{1,0:T(8,128)(2,1)S(1)}, u32[]{:S(2)}, u32[]{:S(2)}) %collective-permute-start.114) | collective-permute-done | bytes 1048608 | tf_op jit(solution)/shard_map/ppermute | solution.py:23
  (644 shorter events, 564.6 us)
Async XLA Ops:
  235.4 38.1 %collective-permute-start.32 = (bf16[256,2048]{1,0:T(8,128)(2,1)S(1)}, bf16[256,2048]{1,0:T(8,128)(2,1)S(1)}, u32[]{:S(2)}, u32[]{:S(2)}) collective-permute-start(bf16[256,2048]{1,0:T(8,128)(2,1)S(1)} %fusion.2), channel_id=1, source_target_pairs={{0,8},{24,16},{1,9},{25,17},{2,10},{26,18},{3,11},{27,19},{4,12},{... | collective-permute-start | bytes 3145736 | tf_op jit(solution)/shard_map/ppermute | solution.py:636
  238.5 71.5 %collective-permute-start.36 = (bf16[512,1024]{1,0:T(8,128)(2,1)S(1)}, bf16[512,1024]{1,0:T(8,128)(2,1)S(1)}, u32[]{:S(2)}, u32[]{:S(2)}) collective-permute-start(bf16[512,1024]{1,0:T(8,128)(2,1)S(1)} %get-tuple-element.475), channel_id=1, source_target_pairs={{0,4},{4,0},{1,5},{5,1},{2,6},{6,2},{3,7},{7,3},{8,12},{12,8},{9,1... | collective-permute-start | bytes 3145736 | tf_op jit(solution)/shard_map/ppermute | solution.py:23
  241.7 200.8 %collective-permute-start.56 = (bf16[512,1024]{1,0:T(8,128)(2,1)}, bf16[512,1024]{1,0:T(8,128)(2,1)}, u32[]{:S(2)}, u32[]{:S(2)}) collective-permute-start(bf16[512,1024]{1,0:T(8,128)(2,1)} %get-tuple-element.473), channel_id=1, source_target_pairs={{0,4},{4,0},{1,5},{5,1},{2,6},{6,2},{3,7},{7,3},{8,12},{12,8},{9,1... | collective-permute-start | bytes 3145736 | tf_op jit(solution)/shard_map/ppermute | solution.py:23
  253.6 41.9 %collective-permute-start.38 = (bf16[256,2048]{1,0:T(8,128)(2,1)S(1)}, bf16[256,2048]{1,0:T(8,128)(2,1)S(1)}, u32[]{:S(2)}, u32[]{:S(2)}) collective-permute-start(bf16[256,2048]{1,0:T(8,128)(2,1)S(1)} %fusion.3), channel_id=1, source_target_pairs={{0,8},{24,16},{1,9},{25,17},{2,10},{26,18},{3,11},{27,19},{4,12},{... | collective-permute-start | bytes 3145736 | tf_op jit(solution)/shard_map/ppermute | solution.py:636
  340.0 37.4 %collective-permute-start.50 = (bf16[256,2048]{1,0:T(8,128)(2,1)}, bf16[256,2048]{1,0:T(8,128)(2,1)}, u32[]{:S(2)}, u32[]{:S(2)}) collective-permute-start(bf16[256,2048]{1,0:T(8,128)(2,1)} %add_convert_fusion.36), channel_id=1, source_target_pairs={{8,0},{16,24},{9,1},{17,25},{10,2},{18,26},{11,3},{19,27},{12,4},{... | collective-permute-start | bytes 3145736 | tf_op jit(solution)/shard_map/ppermute | solution.py:638
  382.5 54.3 %collective-permute-start.55 = (bf16[256,2048]{1,0:T(8,128)(2,1)}, bf16[256,2048]{1,0:T(8,128)(2,1)}, u32[]{:S(2)}, u32[]{:S(2)}) collective-permute-start(bf16[256,2048]{1,0:T(8,128)(2,1)} %add_convert_fusion.33), channel_id=1, source_target_pairs={{8,0},{16,24},{9,1},{17,25},{10,2},{18,26},{11,3},{19,27},{12,4},{... | collective-permute-start | bytes 3145736 | tf_op jit(solution)/shard_map/ppermute | solution.py:638
  383.8 43.9 %collective-permute-start.54 = (bf16[512,1024]{1,0:T(8,128)(2,1)}, bf16[512,1024]{1,0:T(8,128)(2,1)}, u32[]{:S(2)}, u32[]{:S(2)}) collective-permute-start(bf16[512,1024]{1,0:T(8,128)(2,1)} %add_convert_fusion.34), channel_id=1, source_target_pairs={{0,8},{24,16},{1,9},{25,17},{2,10},{26,18},{3,11},{27,19},{4,12},{... | collective-permute-start | bytes 3145736 | tf_op jit(solution)/shard_map/ppermute | solution.py:636
  396.7 42.4 %collective-permute-start.53 = (bf16[256,2048]{1,0:T(8,128)(2,1)}, bf16[256,2048]{1,0:T(8,128)(2,1)}, u32[]{:S(2)}, u32[]{:S(2)}) collective-permute-start(bf16[256,2048]{1,0:T(8,128)(2,1)} %add_convert_fusion.32), channel_id=1, source_target_pairs={{8,16},{16,8},{9,17},{17,9},{10,18},{18,10},{11,19},{19,11},{12,20... | collective-permute-start | bytes 3145736 | tf_op jit(solution)/shard_map/ppermute | solution.py:641
  420.2 55.3 %collective-permute-start.59 = (bf16[256,2048]{1,0:T(8,128)(2,1)}, bf16[256,2048]{1,0:T(8,128)(2,1)S(1)}, u32[]{:S(2)}, u32[]{:S(2)}) collective-permute-start(bf16[256,2048]{1,0:T(8,128)(2,1)} %add_convert_fusion.30), channel_id=1, source_target_pairs={{8,0},{16,24},{9,1},{17,25},{10,2},{18,26},{11,3},{19,27},{12,4},{... | collective-permute-start | bytes 3145736 | tf_op jit(solution)/shard_map/ppermute | solution.py:638
  428.8 36.4 %collective-permute-start.58 = (bf16[512,1024]{1,0:T(8,128)(2,1)S(1)}, bf16[512,1024]{1,0:T(8,128)(2,1)S(1)}, u32[]{:S(2)}, u32[]{:S(2)}) collective-permute-start(bf16[512,1024]{1,0:T(8,128)(2,1)S(1)} %copy-done.53), channel_id=1, source_target_pairs={{0,8},{24,16},{1,9},{25,17},{2,10},{26,18},{3,11},{27,19},{4,12},{... | collective-permute-start | bytes 3145736 | tf_op jit(solution)/shard_map/ppermute | solution.py:636
  436.8 36.3 %collective-permute-start.57 = (bf16[512,1024]{1,0:T(8,128)(2,1)S(1)}, bf16[512,1024]{1,0:T(8,128)(2,1)S(1)}, u32[]{:S(2)}, u32[]{:S(2)}) collective-permute-start(bf16[512,1024]{1,0:T(8,128)(2,1)S(1)} %copy-done.40), channel_id=1, source_target_pairs={{8,16},{16,8},{9,17},{17,9},{10,18},{18,10},{11,19},{19,11},{12,20... | collective-permute-start | bytes 3145736 | tf_op jit(solution)/shard_map/ppermute | solution.py:641
  439.1 37.9 %collective-permute-start.61 = (bf16[256,2048]{1,0:T(8,128)(2,1)S(1)}, bf16[256,2048]{1,0:T(8,128)(2,1)S(1)}, u32[]{:S(2)}, u32[]{:S(2)}) collective-permute-start(bf16[256,2048]{1,0:T(8,128)(2,1)S(1)} %copy-done.62), channel_id=1, source_target_pairs={{0,4},{4,0},{1,5},{5,1},{2,6},{6,2},{3,7},{7,3},{8,12},{12,8},{9,1... | collective-permute-start | bytes 3145736 | tf_op jit(solution)/shard_map/ppermute | solution.py:23
  475.5 35.4 %collective-permute-start.68 = (bf16[256,2048]{1,0:T(8,128)(2,1)S(1)}, bf16[256,2048]{1,0:T(8,128)(2,1)}, u32[]{:S(2)}, u32[]{:S(2)}) collective-permute-start(bf16[256,2048]{1,0:T(8,128)(2,1)S(1)} %broadcast_select_fusion.18.mine_ref), channel_id=1, source_target_pairs={{0,4},{4,0},{1,5},{5,1},{2,6},{6,2},{3,7},{7,3},{8,12},{12,8},{9,1... | collective-permute-start | bytes 3145736 | tf_op jit(solution)/shard_map/ppermute | solution.py:23
  487.8 97.1 %collective-permute-start.78 = (bf16[512,256]{1,0:T(8,128)(2,1)}, bf16[512,256]{1,0:T(8,128)(2,1)}, u32[]{:S(2)}, u32[]{:S(2)}) collective-permute-start(bf16[512,256]{1,0:T(8,128)(2,1)} %get-tuple-element.491), channel_id=1, source_target_pairs={{0,4},{4,0},{1,5},{5,1},{2,6},{6,2},{3,7},{7,3},{8,12},{12,8},{9,1... | collective-permute-start | bytes 786440 | tf_op jit(solution)/shard_map/ppermute | solution.py:23
  500.1 116.1 %collective-permute-start.82 = (bf16[512,256]{1,0:T(8,128)(2,1)}, bf16[512,256]{1,0:T(8,128)(2,1)}, u32[]{:S(2)}, u32[]{:S(2)}) collective-permute-start(bf16[512,256]{1,0:T(8,128)(2,1)} %get-tuple-element.489), channel_id=1, source_target_pairs={{0,4},{4,0},{1,5},{5,1},{2,6},{6,2},{3,7},{7,3},{8,12},{12,8},{9,1... | collective-permute-start | bytes 786440 | tf_op jit(solution)/shard_map/ppermute | solution.py:23
  604.9 44.0 %collective-permute-start.87 = (bf16[512,256]{1,0:T(8,128)(2,1)}, bf16[512,256]{1,0:T(8,128)(2,1)}, u32[]{:S(2)}, u32[]{:S(2)}) collective-permute-start(bf16[512,256]{1,0:T(8,128)(2,1)} %get-tuple-element.487), channel_id=1, source_target_pairs={{0,4},{4,0},{1,5},{5,1},{2,6},{6,2},{3,7},{7,3},{8,12},{12,8},{9,1... | collective-permute-start | bytes 786440 | tf_op jit(solution)/shard_map/ppermute | solution.py:23
  617.3 50.4 %collective-permute-start.90 = (bf16[512,1024]{1,0:T(8,128)(2,1)}, bf16[512,1024]{1,0:T(8,128)(2,1)}, u32[]{:S(2)}, u32[]{:S(2)}) collective-permute-start(bf16[512,1024]{1,0:T(8,128)(2,1)} %add_convert_fusion.11), channel_id=1, source_target_pairs={{8,0},{16,24},{9,1},{17,25},{10,2},{18,26},{11,3},{19,27},{12,4},{... | collective-permute-start | bytes 3145736 | tf_op jit(solution)/shard_map/ppermute | solution.py:638
  641.1 34.8 %collective-permute-start.88 = (bf16[512,1024]{1,0:T(8,128)(2,1)}, bf16[512,1024]{1,0:T(8,128)(2,1)}, u32[]{:S(2)}, u32[]{:S(2)}) collective-permute-start(bf16[512,1024]{1,0:T(8,128)(2,1)} %add_convert_fusion.10), channel_id=1, source_target_pairs={{8,16},{16,8},{9,17},{17,9},{10,18},{18,10},{11,19},{19,11},{12,20... | collective-permute-start | bytes 3145736 | tf_op jit(solution)/shard_map/ppermute | solution.py:641
  656.1 42.9 %collective-permute-start.99 = (bf16[512,1024]{1,0:T(8,128)(2,1)}, bf16[512,1024]{1,0:T(8,128)(2,1)}, u32[]{:S(2)}, u32[]{:S(2)}) collective-permute-start(bf16[512,1024]{1,0:T(8,128)(2,1)} %add_convert_fusion.9), channel_id=1, source_target_pairs={{8,0},{16,24},{9,1},{17,25},{10,2},{18,26},{11,3},{19,27},{12,4},{... | collective-permute-start | bytes 3145736 | tf_op jit(solution)/shard_map/ppermute | solution.py:638
  717.0 39.6 %collective-permute-start.107 = (bf16[512,1024]{1,0:T(8,128)(2,1)}, bf16[512,1024]{1,0:T(8,128)(2,1)}, u32[]{:S(2)}, u32[]{:S(2)}) collective-permute-start(bf16[512,1024]{1,0:T(8,128)(2,1)} %broadcast_select_fusion.mine_ref), channel_id=1, source_target_pairs={{0,4},{4,0},{1,5},{5,1},{2,6},{6,2},{3,7},{7,3},{8,12},{12,8},{9,1... | collective-permute-start | bytes 3145736 | tf_op jit(solution)/shard_map/ppermute | solution.py:23
  761.9 43.3 %collective-permute-start.112 = (bf16[256,2048]{1,0:T(8,128)(2,1)S(1)}, bf16[256,2048]{1,0:T(8,128)(2,1)}, u32[]{:S(2)}, u32[]{:S(2)}) collective-permute-start(bf16[256,2048]{1,0:T(8,128)(2,1)S(1)} %broadcast_select_fusion.15.mine_ref), channel_id=1, source_target_pairs={{0,4},{4,0},{1,5},{5,1},{2,6},{6,2},{3,7},{7,3},{8,12},{12,8},{9,1... | collective-permute-start | bytes 3145736 | tf_op jit(solution)/shard_map/ppermute | solution.py:23
  785.3 42.4 %collective-permute-start.110 = (bf16[2048,256]{1,0:T(8,128)(2,1)}, bf16[2048,256]{1,0:T(8,128)(2,1)}, u32[]{:S(2)}, u32[]{:S(2)}) collective-permute-start(bf16[2048,256]{1,0:T(8,128)(2,1)} %broadcast_select_fusion.14.mine_ref), channel_id=1, source_target_pairs={{0,4},{4,0},{1,5},{5,1},{2,6},{6,2},{3,7},{7,3},{8,12},{12,8},{9,1... | collective-permute-start | bytes 3145736 | tf_op jit(solution)/shard_map/ppermute | solution.py:23
  808.9 41.1 %collective-permute-start.114 = (bf16[2048,256]{1,0:T(8,128)(2,1)S(1)}, bf16[2048,256]{1,0:T(8,128)(2,1)S(1)}, u32[]{:S(2)}, u32[]{:S(2)}) collective-permute-start(bf16[2048,256]{1,0:T(8,128)(2,1)S(1)} %broadcast_select_fusion.12.mine_ref), channel_id=1, source_target_pairs={{0,4},{4,0},{1,5},{5,1},{2,6},{6,2},{3,7},{7,3},{8,12},{12,8},{9,1... | collective-permute-start | bytes 3145736 | tf_op jit(solution)/shard_map/ppermute | solution.py:23
  827.6 36.4 %collective-permute-start.113 = (bf16[2048,256]{1,0:T(8,128)(2,1)S(1)}, bf16[2048,256]{1,0:T(8,128)(2,1)}, u32[]{:S(2)}, u32[]{:S(2)}) collective-permute-start(bf16[2048,256]{1,0:T(8,128)(2,1)S(1)} %broadcast_select_fusion.13.mine_ref), channel_id=1, source_target_pairs={{0,4},{4,0},{1,5},{5,1},{2,6},{6,2},{3,7},{7,3},{8,12},{12,8},{9,1... | collective-permute-start | bytes 3145736 | tf_op jit(solution)/shard_map/ppermute | solution.py:23
  (201 other events, 2931.3 us)

commit v3 on v2

--- a/solution.py
+++ b/solution.py
@@ -15,7 +15,6 @@
 ROPE_BASE = 500000.0
 NEG_FILL = -1e30
 CHUNKS = 4
-STREAMS = 2
 
 
 def flip(value, axis, distance):
@@ -40,24 +39,35 @@
     return [parts[o] for o in range(len(parts))]
 
 
-def gather_both(own, axis, early=None):
-    swapped = flip(own, "ctx", 1)
-    mine, theirs = {0: own}, {0: swapped}
+def gather_both(own, axis, beside=None):
+    mine, theirs = {0: own}, {0: flip(own, "ctx", 1)}
     for far, distance in enumerate(reversed(distances(axis))):
         for o in list(mine):
             mine[o ^ distance] = flip(mine[o], axis, distance)
             if far == 0 and distance > 1:
                 rows = own.shape[0] // 2
-                theirs[o ^ distance] = jnp.concatenate(
+                theirs[o ^ distance] = stacked(
                     [
                         flip(theirs[o][:rows], axis, distance),
                         flip(mine[o ^ distance][rows:], "ctx", 1),
-                    ],
-                    axis=0,
+                    ]
                 )
+                held = (mine[o ^ distance], beside)
+                mine[o ^ distance], beside = lax.optimization_barrier(held)
             else:
                 theirs[o ^ distance] = flip(theirs[o], axis, distance)
-    return [mine[o] for o in range(len(mine))], [theirs[o] for o in range(len(theirs))]
+    blocks = range(len(mine))
+    return [mine[o] for o in blocks], [theirs[o] for o in blocks], beside
+
+
+def gather_beside(own, axis, beside):
+    parts = {0: own}
+    for distance in reversed(distances(axis)):
+        parts.update({o ^ distance: flip(block, axis, distance) for o, block in parts.items()})
+        if len(parts) == 2:
+            held = (parts[distance], beside)
+            parts[distance], beside = lax.optimization_barrier(held)
+    return [parts[o] for o in range(len(parts))], beside
 
 
 def stacked(blocks):
@@ -419,7 +429,7 @@
     sine = jnp.sin(angles) * jnp.where(lane < HD // 2, -1.0, 1.0)[None, :]
     turns = (cosine, sine, cosine, sine, at_query[:, None], at_key[None, :])
 
-    own_blocks, other_blocks = gather_both(tokens, "seq")
+    own_blocks, other_blocks, turns = gather_both(tokens, "seq", turns)
     tokens_own, query_proj, key_proj, value_own, sq_query, sq_key = project(
         own_blocks, (w_query, w_key), (w_value,)
     )
@@ -453,9 +463,9 @@
     attn_unit = attn_proj * inv_attn
     hidden = tokens.astype(jnp.float32) + attn_unit * gain_attn
     hidden_low = hidden.astype(jnp.bfloat16)
-    hidden_own = stacked(gather_rows(hidden_low, "seq"))
     hidden_flip = flip(hidden_low, "ctx", 1)
-    hidden_own, hidden_flip = lax.optimization_barrier((hidden_own, hidden_flip))
+    hidden_blocks, hidden_flip = gather_beside(hidden_low, "seq", hidden_flip)
+    hidden_own = stacked(hidden_blocks)
     hidden_rest = gather_rows(hidden_flip, "seq")
     gate_proj = jnp.dot(hidden_own, w_gate, preferred_element_type=jnp.float32)
     up_proj = jnp.dot(hidden_own, w_up, preferred_element_type=jnp.float32)
@@ -465,6 +475,7 @@
     inner_low, hidden_rest = lax.optimization_barrier((inner_low, hidden_rest))
     inner_halves = swap_halves(inner_low)
     ffn = to_owners(jnp.dot(inner_low, w_down, preferred_element_type=jnp.float32))
+    ffn, inner_halves = lax.optimization_barrier((ffn, inner_halves))
     inv_ffn = lax.rsqrt(jnp.mean(ffn * ffn, axis=1, keepdims=True) + EPS)
     ffn_unit = ffn * inv_ffn
     out_tokens = (hidden + ffn_unit * gain_ffn).astype(jnp.bfloat16)
@@ -476,8 +487,8 @@
     grad_out = cotangent.astype(jnp.float32) * picked
     gain_ffn_part = jnp.sum(grad_out * ffn_unit, axis=0)
     grad_ffn_low = norm_back(ffn_unit, inv_ffn, grad_out * gain_ffn).astype(jnp.bfloat16)
-    grad_ffn_low, inner_halves = lax.optimization_barrier((grad_ffn_low, inner_halves))
-    grad_ffn_own, grad_ffn_other = map(stacked, gather_both(grad_ffn_low, "seq"))
+    grad_ffn_own, grad_ffn_other, _ = gather_both(grad_ffn_low, "seq")
+    grad_ffn_own, grad_ffn_other = stacked(grad_ffn_own), stacked(grad_ffn_other)
     hidden_other = stacked(hidden_rest)
 
     grads = {
@@ -493,7 +504,8 @@
     results = {}
 
     def stages():
-        grad_inner = times_transpose(grad_ffn_own, w_down)
+        (grad_ffn,) = yield (grad_ffn_own,)
+        grad_inner = times_transpose(grad_ffn, w_down)
         grad_gate = (grad_inner * up_proj * gate_sig * (1.0 + gate_proj * (1.0 - gate_sig))).astype(
             jnp.bfloat16
         )
@@ -576,71 +588,56 @@
     plan = [(name, index) for name in grads for index in range(grads[name].chunks)]
     count = len(plan)
     rider = count - 1
-    pairs = [(0, 1), (1, 0), (2, 3), (3, 2)]
-    step = STREAMS
+    across_at = {chunk + (2 if chunk else 1): chunk for chunk in range(count)}
+    out_at = {tick + 1: chunk for tick, chunk in across_at.items()}
+    half_at = {tick + 1: chunk for tick, chunk in out_at.items()}
+    store_at = {tick + 1: chunk for tick, chunk in half_at.items()}
     part, pair, total, final = {}, {}, {}, {}
-    got_pair, got_across, got_half = {}, {}, {}
+    got_in, got_across, got_out, got_half = {}, {}, {}, {}
     main = stages()
     state = next(main)
     last_name, last_buffer = None, None
-
-    def rides(index):
-        return (results["gains"],) if index == rider else ()
-
-    for tick in range(count + 4 * step):
-        before = tick - step
-        if before in part:
-            pair[before] = jax.tree.map(added, part[before], got_pair[before][1])
-        if before - step in part:
-            total[before - step] = jax.tree.map(added, pair[before - step], got_across[before])
-        if before - 2 * step in part:
-            final[before - 2 * step] = jax.tree.map(
-                lambda kept, got: jnp.where(middle, kept, got),
-                total[before - 2 * step],
-                got_pair[before][0],
-            )
-        stored = before - 3 * step
-        arrived = got_half.get(before)
-        if tick == 0:
-            part[0] = (grads[plan[0][0]].part(sides[plan[0][0]], 0),)
+    token = picked
+    part[0] = (grads[plan[0][0]].part(sides[plan[0][0]], 0),)
+
+    def send(values, axis, pairs):
+        return tuple(lax.ppermute(value, axis, pairs) for value in values)
+
+    for tick in range(max(store_at) + 1):
         entering = part.get(tick)
-        leaving = total.get(tick - 2 * step)
-        crossing = pair.get(tick - step)
-        swapping = final.get(tick - 3 * step)
+        chunk = across_at.get(tick)
+        crossing = None
+        if chunk is not None:
+            crossing = jax.tree.map(added, part[chunk], got_in[chunk])
         coming = sides.get(plan[tick + 1][0]) if tick + 1 < count else None
-        held = (entering, leaving, crossing, swapping, state, arrived, coming, last_buffer)
-        entering, leaving, crossing, swapping, state, arrived, coming, last_buffer = (
-            lax.optimization_barrier(held)
-        )
+        held = (entering, crossing, state, coming, last_buffer, token)
+        entering, crossing, state, coming, last_buffer, token = lax.optimization_barrier(held)
         if last_name:
             grads[last_name].buffer = last_buffer
-        if stored in part:
-            last_name, index = plan[stored]
-            grads[last_name].store(index, final[stored][0], arrived)
-            last_buffer = grads[last_name].buffer
+        if crossing is not None:
+            pair[chunk] = crossing
+            got_across[chunk] = send(crossing, "dp", [(1, 2), (2, 1)])
         if entering is not None:
             part[tick] = entering
-        if leaving is not None:
-            total[tick - 2 * step] = leaving
-        if crossing is not None:
-            pair[tick - step] = crossing
-        if swapping is not None:
-            final[tick - 3 * step] = swapping
-        arrived_out = arrived_in = None
-        alike = entering is not None and leaving is not None
-        if alike and [v.shape for v in entering] == [v.shape for v in leaving]:
-            sent = jax.tree.map(lambda out, into: jnp.where(middle, out, into), leaving, entering)
-            arrived_in = arrived_out = tuple(lax.ppermute(v, "dp", pairs) for v in sent)
-        else:
-            if entering is not None:
-                arrived_in = tuple(lax.ppermute(v, "dp", [(0, 1), (3, 2)]) for v in entering)
-            if leaving is not None:
-                arrived_out = tuple(lax.ppermute(v, "dp", [(1, 0), (2, 3)]) for v in leaving)
-        got_pair[tick] = (arrived_out, arrived_in)
-        if crossing is not None:
-            got_across[tick] = tuple(lax.ppermute(v, "dp", [(1, 2), (2, 1)]) for v in crossing)
-        if swapping is not None:
-            got_half[tick] = flip(swapping[0], "ctx", 1)
+            got_in[tick] = send(entering, "dp", [(0, 1), (3, 2)])
+        if tick in out_at:
+            chunk = out_at[tick]
+            leaving = jax.tree.map(added, pair[chunk], got_across[chunk])
+            total[chunk], token = lax.optimization_barrier((leaving, token))
+            got_out[chunk] = send(total[chunk], "dp", [(1, 0), (2, 3)])
+        if tick in half_at:
+            chunk = half_at[tick]
+            swapping = jax.tree.map(
+                lambda kept, got: jnp.where(middle, kept, got), total[chunk], got_out[chunk]
+            )
+            final[chunk], token = lax.optimization_barrier((swapping, token))
+            got_half[chunk] = flip(final[chunk][0], "ctx", 1)
+        if tick in store_at:
+            chunk = store_at[tick]
+            theirs, token = lax.optimization_barrier((got_half[chunk], token))
+            last_name, index = plan[chunk]
+            grads[last_name].store(index, final[chunk][0], theirs)
+            last_buffer = grads[last_name].buffer
         try:
             state = main.send(state)
         except StopIteration:
@@ -648,7 +645,8 @@
         if tick + 1 < count:
             name, index = plan[tick + 1]
             coming = sides[name] if coming is None else coming
-            part[tick + 1] = (grads[name].part(coming, index),) + rides(tick + 1)
+            rides = (results["gains"],) if tick + 1 == rider else ()
+            part[tick + 1] = (grads[name].part(coming, index),) + rides
 
     gains = final[rider][1].reshape(-1)
     grad_gain_attn = gains[:D]

time: 875 us -> 890 us (1.017)
  waiting for transfers between devices: 326 us -> 263 us
  starting transfers between devices: 166 us -> 210 us
  matrix products: 108 us -> 124 us
  other arithmetic: 121 us -> 133 us
    ppermute x66, waiting for transfers between devices: 227 us -> 137 us  [flip(): lax.ppermute(value, axis, [(place, place ^ distance) for place in range(c...]
    ppermute x47 -> x51, starting transfers between devices: 116 us -> 159 us  [send(): return tuple((lax.ppermute(value, axis, pairs) for value in values))]
    ppermute x47 -> x51, waiting for transfers between devices: 90.1 us -> 125 us  [send(): return tuple((lax.ppermute(value, axis, pairs) for value in values))]
    convert_element_type x32, other arithmetic: 60.2 us -> 70.3 us  [added(): (left.astype(jnp.float32) + right.astype(jnp.float32)).astype(left.dtype)]
  transfers between devices with their start and end apart: 115 -> 119, of which waited for: 39 -> 43; matrix products, arithmetic and copies ran while one was open for 26% -> 28% of each run, Pallas kernels for 9% -> 9%
where the time goes in v3:
time: 890 us; the launch traced here: 880 us
  waiting for transfers between devices  263 us (30%)
  starting transfers between devices  210 us (24%)
  other arithmetic  133 us (15%)
  matrix products  124 us (14%)
  Pallas kernels  96.6 us (11%)
  local copies, waits for them, and re-layouts  30.6 us (3%)
  blocking collectives  19 us (2%)
    ppermute x51, starting transfers between devices, send(): return tuple((lax.ppermute(value, axis, pairs) for value in values))  159 us
    ppermute x66, waiting for transfers between devices, flip(): lax.ppermute(value, axis, [(place, place ^ distance) for place in range(c...  137 us
    ppermute x51, waiting for transfers between devices, send(): return tuple((lax.ppermute(value, axis, pairs) for value in values))  125 us
    convert_element_type x32, other arithmetic, added(): (left.astype(jnp.float32) + right.astype(jnp.float32)).astype(left.dtype)  70.3 us
    dot_general x32, matrix products, contract_rows(): lax.dot_general(left, right, (((0,), (0,)), ((), ())), preferred_element_...  60 us
    pallas_call x16, Pallas kernels, store_chunk(): pl.pallas_call(store_kernel, grid_spec=pltpu.PrefetchScalarGridSpec(num_s...  59.5 us
    ppermute x66, starting transfers between devices, flip(): lax.ppermute(value, axis, [(place, place ^ distance) for place in range(c...  48.1 us
    dot_general x7, matrix products, times_transpose(): lax.dot_general(left, right, (((1,), (1,)), ((), ())), preferred_element_...  34.4 us
  transfers between devices with their start and end apart: 119, of which 43 were waited for; matrix products, arithmetic and copies ran while one was open for 28% of the time, Pallas kernels for 9%

profile of v3, /device:TPU:0, one launch (start us, length us, event | category | flops | bytes accessed | tf_op | source)
XLA Modules:
  0.0 879.8 jit_solution(12994266480061235660)
XLA Ops:
  5.3 10.5 %collective-permute-done.3.refs_0_ = bf16[128,2048]{1,0:T(8,128)(2,1)S(1)} collective-permute-done((bf16[128,2048]{1,0:T(8,128)(2,1)}, bf16[128,2048]{1,0:T(8,128)(2,1)S(1)}, u32[]{:S(2)}, u32[]{:S(2)}) %collective-permute-start.3) | collective-permute-done | bytes 524320 | tf_op jit(solution)/shard_map/ppermute | solution.py:22
  56.5 11.8 %attend.1 = (bf16[512,512]{1,0:T(8,128)(2,1)}, bf16[1024,512]{1,0:T(8,128)(2,1)}, bf16[1024,512]{1,0:T(8,128)(2,1)}, bf16[512,512]{1,0:T(8,128)(2,1)}, f32[4,512,1]{2,1,0:T(8,128)}) custom-call(f32[512,512]{1,0:T(8,128)} %get-tuple-element.289.query_ref, f32[512,512]{1,0:T(8,128)} %get-tuple-element.290.key_ref, ...), custom_call_target="tpu_custom_call" | custom-call | tf_op jit(solution)/shard_map/attend/pallas_call | solution.py:260
  75.3 12.6 %collective-permute-done.10 = bf16[128,2048]{1,0:T(8,128)(2,1)} collective-permute-done((bf16[128,2048]{1,0:T(8,128)(2,1)}, bf16[128,2048]{1,0:T(8,128)(2,1)}, u32[]{:S(2)}, u32[]{:S(2)}) %collective-permute-start.10) | collective-permute-done | bytes 524320 | tf_op jit(solution)/shard_map/ppermute | solution.py:22
  91.1 12.2 %collective-permute-done.13 = bf16[128,2048]{1,0:T(8,128)(2,1)S(1)} collective-permute-done((bf16[128,2048]{1,0:T(8,128)(2,1)S(1)}, bf16[128,2048]{1,0:T(8,128)(2,1)S(1)}, u32[]{:S(2)}, u32[]{:S(2)}) %collective-permute-start.13) | collective-permute-done | bytes 524320 | tf_op jit(solution)/shard_map/ppermute | solution.py:22
  105.5 10.1 %collective-permute-done.17 = bf16[128,2048]{1,0:T(8,128)(2,1)S(1)} collective-permute-done((bf16[128,2048]{1,0:T(8,128)(2,1)S(1)}, bf16[128,2048]{1,0:T(8,128)(2,1)S(1)}, u32[]{:S(2)}, u32[]{:S(2)}) %collective-permute-start.17) | collective-permute-done | bytes 524320 | tf_op jit(solution)/shard_map/ppermute | solution.py:22
  115.7 11.6 %fusion.64 = f32[512,2048]{1,0:T(8,128)} fusion(bf16[2048,2048]{1,0:T(8,128)(2,1)} %param.27, bf16[128,2048]{1,0:T(8,128)(2,1)S(1)} %collective-permute-done.15, bf16[128,2048]{1,0:T(8,128)(2,1)S(1)} %collective-permute-done.13, bf16[128,2048]{1,0:T(8,128)(2,1)S(1)} %collective-permute-done.12, bf16[128,2048]{1,0:T(8,128)(2,1)S(1)} %fusion.14), kind=kOutput, calls=%fused_computation.229 | convolution fusion | flops 4303355904 | bytes 14680064 | tf_op jit(solution)/shard_map/dot_general | solution.py:470
  127.4 9.9 %multiply_convert_fusion.2 = (bf16[512,2048]{1,0:T(8,128)(2,1)S(1)}, f32[512,2048]{1,0:T(8,128)}) fusion(f32[512,2048]{1,0:T(8,128)} %fusion.64, bf16[2048,2048]{1,0:T(8,128)(2,1)S(1)} %bitcast.126, bf16[128,2048]{1,0:T(8,128)(2,1)S(1)} %collective-permute-done.15, bf16[128,2048]{1,0:T(8,128)(2,1)S(1)} %collective-permute-done.13, ...), kind=kOutput, calls=%fused_computation.7 | convolution fusion | flops 4309647360 | bytes 20971520 | tf_op jit(solution)/shard_map/dot_general | solution.py:471
  156.8 9.1 %collective-permute-done.21 = bf16[128,2048]{1,0:T(8,128)(2,1)} collective-permute-done((bf16[128,2048]{1,0:T(8,128)(2,1)}, bf16[128,2048]{1,0:T(8,128)(2,1)}, u32[]{:S(2)}, u32[]{:S(2)}) %collective-permute-start.21) | collective-permute-done | bytes 524320 | tf_op jit(solution)/shard_map/ppermute | solution.py:22
  209.4 11.8 %multiply_convert_fusion = (bf16[512,2048]{1,0:T(8,128)(2,1)}, bf16[512,2048]{1,0:T(8,128)(2,1)}) fusion(f32[512,2048]{1,0:T(8,128)} %fusion.64, f32[512,2048]{1,0:T(8,128)} %get-tuple-element.611, bf16[512,2048]{1,0:T(8,128)(2,1)S(1)} %pad_maximum_fusion.1, bf16[2048,2048]{1,0:T(8,128)(2,1)} %param.29), kind=kOutput, calls=%fused_computation.5 | convolution fusion | flops 4308598784 | bytes 23068672 | tf_op jit(solution)/shard_map/dot_general | solution.py:104
  273.2 13.6 %collective-permute-done.33 = bf16[512,1024]{1,0:T(8,128)(2,1)S(1)} collective-permute-done((bf16[512,1024]{1,0:T(8,128)(2,1)}, bf16[512,1024]{1,0:T(8,128)(2,1)S(1)}, u32[]{:S(2)}, u32[]{:S(2)}) %collective-permute-start.33) | collective-permute-done | bytes 1048608 | tf_op jit(solution)/shard_map/ppermute | solution.py:22
  302.1 12.7 %collective-permute-done.39 = bf16[256,2048]{1,0:T(8,128)(2,1)S(1)} collective-permute-done((bf16[256,2048]{1,0:T(8,128)(2,1)S(1)}, bf16[256,2048]{1,0:T(8,128)(2,1)S(1)}, u32[]{:S(2)}, u32[]{:S(2)}) %collective-permute-start.39) | collective-permute-done | bytes 1048608 | tf_op jit(solution)/shard_map/ppermute | solution.py:604
  344.7 10.1 %collective-permute-done.51 = bf16[256,2048]{1,0:T(8,128)(2,1)} collective-permute-done((bf16[256,2048]{1,0:T(8,128)(2,1)}, bf16[256,2048]{1,0:T(8,128)(2,1)}, u32[]{:S(2)}, u32[]{:S(2)}) %collective-permute-start.51) | collective-permute-done | bytes 1048608 | tf_op jit(solution)/shard_map/ppermute | solution.py:604
  362.1 14.4 %collective-permute-done.47 = bf16[512,1024]{1,0:T(8,128)(2,1)S(1)} collective-permute-done((bf16[512,1024]{1,0:T(8,128)(2,1)S(1)}, bf16[512,1024]{1,0:T(8,128)(2,1)S(1)}, u32[]{:S(2)}, u32[]{:S(2)}) %collective-permute-start.47) | collective-permute-done | bytes 1048608 | tf_op jit(solution)/shard_map/ppermute | solution.py:604
  390.7 11.0 %attend_back.1 = (f32[512,512]{1,0:T(8,128)}, f32[512,512]{1,0:T(8,128)}, f32[512,512]{1,0:T(8,128)}, bf16[512,512]{1,0:T(8,128)(2,1)}, bf16[512,512]{1,0:T(8,128)(2,1)}) custom-call(bf16[512,512]{1,0:T(8,128)(2,1)} %get-tuple-element.365.query_low_ref, bf16[1024,512]{1,0:T(8,128)(2,1)} %get-tuple-element.366.key_low_ref, ...), custom_call_target="tpu_custom_call" | custom-call | tf_op jit(solution)/shard_map/attend_back/pallas_call | solution.py:287
  421.2 14.0 %collective-permute-done.57.theirs_ref = bf16[256,2048]{1,0:T(8,128)(2,1)S(1)} collective-permute-done((bf16[256,2048]{1,0:T(8,128)(2,1)S(1)}, bf16[256,2048]{1,0:T(8,128)(2,1)S(1)}, u32[]{:S(2)}, u32[]{:S(2)}) %collective-permute-start.57) | collective-permute-done | bytes 1048608 | tf_op jit(solution)/shard_map/ppermute | solution.py:22
  459.3 11.2 %all-reduce = (f32[2,4,128]{2,0,1:T(2,128)S(1)}, f32[4096]{0:T(1024)S(1)}) all-reduce(f32[2,4,128]{2,0,1:T(2,128)S(1)} %select_bitcast_fusion.3, f32[4096]{0:T(1024)S(1)} %pad_maximum_fusion.5), channel_id=1, replica_groups=mesh['dp'=4,'ctx'=2,'seq'=4] {'seq'}, use_global_device_ids=true, to_apply=%region_8.11 | all-reduce | flops 5120 | bytes 40960 | tf_op jit(solution)/shard_map/psum | solution.py:547
  563.4 10.2 %collective-permute-start.76 = (bf16[512,1024]{1,0:T(8,128)(2,1)}, bf16[512,1024]{1,0:T(8,128)(2,1)}, u32[]{:S(2)}, u32[]{:S(2)}) collective-permute-start(bf16[512,1024]{1,0:T(8,128)(2,1)} %add_convert_fusion.22), channel_id=1, source_target_pairs={{0,8},{24,16},{1,9},{25,17},{2,10},{26,18},{3,11},{27,19},{4,12},{... | collective-permute-start | bytes 3145736 | tf_op jit(solution)/shard_map/ppermute | solution.py:604
  586.7 11.0 %collective-permute-start.80 = (bf16[512,1024]{1,0:T(8,128)(2,1)}, bf16[512,1024]{1,0:T(8,128)(2,1)}, u32[]{:S(2)}, u32[]{:S(2)}) collective-permute-start(bf16[512,1024]{1,0:T(8,128)(2,1)} %add_convert_fusion.19), channel_id=1, source_target_pairs={{0,8},{24,16},{1,9},{25,17},{2,10},{26,18},{3,11},{27,19},{4,12},{... | collective-permute-start | bytes 3145736 | tf_op jit(solution)/shard_map/ppermute | solution.py:604
  647.4 19.6 %collective-permute-start.90 = (bf16[256,2048]{1,0:T(8,128)(2,1)}, bf16[256,2048]{1,0:T(8,128)(2,1)}, u32[]{:S(2)}, u32[]{:S(2)}) collective-permute-start(bf16[256,2048]{1,0:T(8,128)(2,1)} %fusion.5), channel_id=1, source_target_pairs={{0,8},{24,16},{1,9},{25,17},{2,10},{26,18},{3,11},{27,19},{4,12},{... | collective-permute-start | bytes 3145736 | tf_op jit(solution)/shard_map/ppermute | solution.py:604
  780.8 11.1 %collective-permute-done.117 = bf16[256,2048]{1,0:T(8,128)(2,1)} collective-permute-done((bf16[256,2048]{1,0:T(8,128)(2,1)}, bf16[256,2048]{1,0:T(8,128)(2,1)}, u32[]{:S(2)}, u32[]{:S(2)}) %collective-permute-start.117) | collective-permute-done | bytes 1048608 | tf_op jit(solution)/shard_map/ppermute | solution.py:604
  797.0 17.4 %collective-permute-done.115 = bf16[2048,256]{1,0:T(8,128)(2,1)} collective-permute-done((bf16[2048,256]{1,0:T(8,128)(2,1)S(1)}, bf16[2048,256]{1,0:T(8,128)(2,1)}, u32[]{:S(2)}, u32[]{:S(2)}) %collective-permute-start.115) | collective-permute-done | bytes 1048608 | tf_op jit(solution)/shard_map/ppermute | solution.py:604
  819.2 17.6 %collective-permute-done.112 = bf16[2048,256]{1,0:T(8,128)(2,1)S(1)} collective-permute-done((bf16[2048,256]{1,0:T(8,128)(2,1)S(1)}, bf16[2048,256]{1,0:T(8,128)(2,1)S(1)}, u32[]{:S(2)}, u32[]{:S(2)}) %collective-permute-start.112) | collective-permute-done | bytes 1048608 | tf_op jit(solution)/shard_map/ppermute | solution.py:604
  839.0 13.3 %collective-permute-done.109 = f32[40,128]{1,0:T(8,128)S(1)} collective-permute-done((f32[40,128]{1,0:T(8,128)S(1)}, f32[40,128]{1,0:T(8,128)S(1)}, u32[]{:S(2)}, u32[]{:S(2)}) %collective-permute-start.109) | collective-permute-done | bytes 20512 | tf_op jit(solution)/shard_map/ppermute | solution.py:604
  866.8 8.9 %collective-permute-done.110.theirs_ref = bf16[2048,256]{1,0:T(8,128)(2,1)} collective-permute-done((bf16[2048,256]{1,0:T(8,128)(2,1)}, bf16[2048,256]{1,0:T(8,128)(2,1)}, u32[]{:S(2)}, u32[]{:S(2)}) %collective-permute-start.110) | collective-permute-done | bytes 1048608 | tf_op jit(solution)/shard_map/ppermute | solution.py:22
  (611 shorter events, 580.5 us)
Async XLA Ops:
  264.8 188.3 %collective-permute-start.56 = (bf16[512,1024]{1,0:T(8,128)(2,1)}, bf16[512,1024]{1,0:T(8,128)(2,1)}, u32[]{:S(2)}, u32[]{:S(2)}) collective-permute-start(bf16[512,1024]{1,0:T(8,128)(2,1)} %get-tuple-element.575), channel_id=1, source_target_pairs={{0,4},{4,0},{1,5},{5,1},{2,6},{6,2},{3,7},{7,3},{8,12},{12,8},{9,1... | collective-permute-start | bytes 3145736 | tf_op jit(solution)/shard_map/ppermute | solution.py:22
  340.0 37.9 %collective-permute-start.41 = (bf16[128,2048]{1,0:T(8,128)(2,1)}, bf16[128,2048]{1,0:T(8,128)(2,1)}, u32[]{:S(2)}, u32[]{:S(2)}) collective-permute-start(bf16[128,2048]{1,0:T(8,128)(2,1)} %get-tuple-element.587), channel_id=1, source_target_pairs={{0,1},{1,0},{2,3},{3,2},{4,5},{5,4},{6,7},{7,6},{8,9},{9,8},{10,11... | collective-permute-start | bytes 1572872 | tf_op jit(solution)/shard_map/ppermute | solution.py:22
  380.3 35.3 %collective-permute-start.53 = (bf16[512,1024]{1,0:T(8,128)(2,1)}, bf16[512,1024]{1,0:T(8,128)(2,1)}, u32[]{:S(2)}, u32[]{:S(2)}) collective-permute-start(bf16[512,1024]{1,0:T(8,128)(2,1)} %add_convert_fusion.34), channel_id=1, source_target_pairs={{0,8},{24,16},{1,9},{25,17},{2,10},{26,18},{3,11},{27,19},{4,12},{... | collective-permute-start | bytes 3145736 | tf_op jit(solution)/shard_map/ppermute | solution.py:604
  418.6 35.9 %collective-permute-start.54 = (bf16[512,512]{1,0:T(8,128)(2,1)}, bf16[512,512]{1,0:T(8,128)(2,1)S(1)}, u32[]{:S(2)}, u32[]{:S(2)}) collective-permute-start(bf16[512,512]{1,0:T(8,128)(2,1)} %get-tuple-element.390), channel_id=1, source_target_pairs={{4,0},{5,1},{6,2},{7,3},{12,8},{13,9},{14,10},{15,11},{20,16},{21,... | collective-permute-start | bytes 1572872 | tf_op jit(solution)/shard_map/ppermute | solution.py:535
  419.9 37.8 %collective-permute-start.55 = (bf16[512,512]{1,0:T(8,128)(2,1)}, bf16[512,512]{1,0:T(8,128)(2,1)S(1)}, u32[]{:S(2)}, u32[]{:S(2)}) collective-permute-start(bf16[512,512]{1,0:T(8,128)(2,1)} %get-tuple-element.391), channel_id=1, source_target_pairs={{4,0},{5,1},{6,2},{7,3},{12,8},{13,9},{14,10},{15,11},{20,16},{21,... | collective-permute-start | bytes 1572872 | tf_op jit(solution)/shard_map/ppermute | solution.py:535
  436.1 60.0 %collective-permute-start.60 = (bf16[512,1024]{1,0:T(8,128)(2,1)}, bf16[512,1024]{1,0:T(8,128)(2,1)}, u32[]{:S(2)}, u32[]{:S(2)}) collective-permute-start(bf16[512,1024]{1,0:T(8,128)(2,1)} %add_convert_fusion.31), channel_id=1, source_target_pairs={{0,8},{24,16},{1,9},{25,17},{2,10},{26,18},{3,11},{27,19},{4,12},{... | collective-permute-start | bytes 3145736 | tf_op jit(solution)/shard_map/ppermute | solution.py:604
  441.8 50.7 %collective-permute-start.61 = (bf16[256,2048]{1,0:T(8,128)(2,1)}, bf16[256,2048]{1,0:T(8,128)(2,1)}, u32[]{:S(2)}, u32[]{:S(2)}) collective-permute-start(bf16[256,2048]{1,0:T(8,128)(2,1)} %broadcast_select_fusion.13.mine_ref), channel_id=1, source_target_pairs={{0,4},{4,0},{1,5},{5,1},{2,6},{6,2},{3,7},{7,3},{8,12},{12,8},{9,1... | collective-permute-start | bytes 3145736 | tf_op jit(solution)/shard_map/ppermute | solution.py:22
  453.0 37.1 %collective-permute-start.62 = (bf16[256,2048]{1,0:T(8,128)(2,1)}, bf16[256,2048]{1,0:T(8,128)(2,1)}, u32[]{:S(2)}, u32[]{:S(2)}) collective-permute-start(bf16[256,2048]{1,0:T(8,128)(2,1)} %add_convert_fusion.26), channel_id=1, source_target_pairs={{8,0},{16,24},{9,1},{17,25},{10,2},{18,26},{11,3},{19,27},{12,4},{... | collective-permute-start | bytes 3145736 | tf_op jit(solution)/shard_map/ppermute | solution.py:604
  474.3 51.5 %collective-permute-start.64 = (bf16[512,1024]{1,0:T(8,128)(2,1)}, bf16[512,1024]{1,0:T(8,128)(2,1)}, u32[]{:S(2)}, u32[]{:S(2)}) collective-permute-start(bf16[512,1024]{1,0:T(8,128)(2,1)} %add_convert_fusion.28), channel_id=1, source_target_pairs={{0,8},{24,16},{1,9},{25,17},{2,10},{26,18},{3,11},{27,19},{4,12},{... | collective-permute-start | bytes 3145736 | tf_op jit(solution)/shard_map/ppermute | solution.py:604
  485.5 35.6 %collective-permute-start.68 = (bf16[512,1024]{1,0:T(8,128)(2,1)}, bf16[512,1024]{1,0:T(8,128)(2,1)}, u32[]{:S(2)}, u32[]{:S(2)}) collective-permute-start(bf16[512,1024]{1,0:T(8,128)(2,1)} %add_convert_fusion.27), channel_id=1, source_target_pairs={{8,16},{16,8},{9,17},{17,9},{10,18},{18,10},{11,19},{19,11},{12,20... | collective-permute-start | bytes 3145736 | tf_op jit(solution)/shard_map/ppermute | solution.py:604
  525.8 113.8 %collective-permute-start.81 = (bf16[512,256]{1,0:T(8,128)(2,1)}, bf16[512,256]{1,0:T(8,128)(2,1)}, u32[]{:S(2)}, u32[]{:S(2)}) collective-permute-start(bf16[512,256]{1,0:T(8,128)(2,1)} %get-tuple-element.593), channel_id=1, source_target_pairs={{0,4},{4,0},{1,5},{5,1},{2,6},{6,2},{3,7},{7,3},{8,12},{12,8},{9,1... | collective-permute-start | bytes 786440 | tf_op jit(solution)/shard_map/ppermute | solution.py:22
  563.4 40.9 %collective-permute-start.76 = (bf16[512,1024]{1,0:T(8,128)(2,1)}, bf16[512,1024]{1,0:T(8,128)(2,1)}, u32[]{:S(2)}, u32[]{:S(2)}) collective-permute-start(bf16[512,1024]{1,0:T(8,128)(2,1)} %add_convert_fusion.22), channel_id=1, source_target_pairs={{0,8},{24,16},{1,9},{25,17},{2,10},{26,18},{3,11},{27,19},{4,12},{... | collective-permute-start | bytes 3145736 | tf_op jit(solution)/shard_map/ppermute | solution.py:604
  597.7 37.9 %collective-permute-start.82 = (bf16[512,1024]{1,0:T(8,128)(2,1)}, bf16[512,1024]{1,0:T(8,128)(2,1)}, u32[]{:S(2)}, u32[]{:S(2)}) collective-permute-start(bf16[512,1024]{1,0:T(8,128)(2,1)} %broadcast_select_fusion.8.mine_ref), channel_id=1, source_target_pairs={{0,4},{4,0},{1,5},{5,1},{2,6},{6,2},{3,7},{7,3},{8,12},{12,8},{9,1... | collective-permute-start | bytes 3145736 | tf_op jit(solution)/shard_map/ppermute | solution.py:22
  617.7 52.2 %collective-permute-start.85 = (bf16[512,1024]{1,0:T(8,128)(2,1)}, bf16[512,1024]{1,0:T(8,128)(2,1)}, u32[]{:S(2)}, u32[]{:S(2)}) collective-permute-start(bf16[512,1024]{1,0:T(8,128)(2,1)} %add_convert_fusion.16), channel_id=1, source_target_pairs={{0,8},{24,16},{1,9},{25,17},{2,10},{26,18},{3,11},{27,19},{4,12},{... | collective-permute-start | bytes 3145736 | tf_op jit(solution)/shard_map/ppermute | solution.py:604
  641.0 38.6 %collective-permute-start.88 = (bf16[512,1024]{1,0:T(8,128)(2,1)}, bf16[512,1024]{1,0:T(8,128)(2,1)}, u32[]{:S(2)}, u32[]{:S(2)}) collective-permute-start(bf16[512,1024]{1,0:T(8,128)(2,1)} %add_convert_fusion.12), channel_id=1, source_target_pairs={{8,0},{16,24},{9,1},{17,25},{10,2},{18,26},{11,3},{19,27},{12,4},{... | collective-permute-start | bytes 3145736 | tf_op jit(solution)/shard_map/ppermute | solution.py:604
  642.3 45.5 %collective-permute-start.94 = (bf16[512,1024]{1,0:T(8,128)(2,1)S(1)}, bf16[512,1024]{1,0:T(8,128)(2,1)}, u32[]{:S(2)}, u32[]{:S(2)}) collective-permute-start(bf16[512,1024]{1,0:T(8,128)(2,1)S(1)} %copy-done.29), channel_id=1, source_target_pairs={{8,16},{16,8},{9,17},{17,9},{10,18},{18,10},{11,19},{19,11},{12,20... | collective-permute-start | bytes 3145736 | tf_op jit(solution)/shard_map/ppermute | solution.py:604
  647.4 44.6 %collective-permute-start.90 = (bf16[256,2048]{1,0:T(8,128)(2,1)}, bf16[256,2048]{1,0:T(8,128)(2,1)}, u32[]{:S(2)}, u32[]{:S(2)}) collective-permute-start(bf16[256,2048]{1,0:T(8,128)(2,1)} %fusion.5), channel_id=1, source_target_pairs={{0,8},{24,16},{1,9},{25,17},{2,10},{26,18},{3,11},{27,19},{4,12},{... | collective-permute-start | bytes 3145736 | tf_op jit(solution)/shard_map/ppermute | solution.py:604
  681.3 44.8 %collective-permute-start.95 = (bf16[2048,256]{1,0:T(8,128)(2,1)}, bf16[2048,256]{1,0:T(8,128)(2,1)}, u32[]{:S(2)}, u32[]{:S(2)}) collective-permute-start(bf16[2048,256]{1,0:T(8,128)(2,1)} %fusion.6), channel_id=1, source_target_pairs={{0,8},{24,16},{1,9},{25,17},{2,10},{26,18},{3,11},{27,19},{4,12},{... | collective-permute-start | bytes 3145736 | tf_op jit(solution)/shard_map/ppermute | solution.py:604
  715.0 41.6 %collective-permute-start.104 = (bf16[2048,256]{1,0:T(8,128)(2,1)}, bf16[2048,256]{1,0:T(8,128)(2,1)}, u32[]{:S(2)}, u32[]{:S(2)}) collective-permute-start(bf16[2048,256]{1,0:T(8,128)(2,1)} %fusion.7), channel_id=1, source_target_pairs={{0,8},{24,16},{1,9},{25,17},{2,10},{26,18},{3,11},{27,19},{4,12},{... | collective-permute-start | bytes 3145736 | tf_op jit(solution)/shard_map/ppermute | solution.py:604
  765.4 49.0 %collective-permute-start.115 = (bf16[2048,256]{1,0:T(8,128)(2,1)S(1)}, bf16[2048,256]{1,0:T(8,128)(2,1)}, u32[]{:S(2)}, u32[]{:S(2)}) collective-permute-start(bf16[2048,256]{1,0:T(8,128)(2,1)S(1)} %add_convert_fusion), channel_id=1, source_target_pairs={{8,0},{16,24},{9,1},{17,25},{10,2},{18,26},{11,3},{19,27},{12,4},{... | collective-permute-start | bytes 3145736 | tf_op jit(solution)/shard_map/ppermute | solution.py:604
  779.5 57.3 %collective-permute-start.112 = (bf16[2048,256]{1,0:T(8,128)(2,1)S(1)}, bf16[2048,256]{1,0:T(8,128)(2,1)S(1)}, u32[]{:S(2)}, u32[]{:S(2)}) collective-permute-start(bf16[2048,256]{1,0:T(8,128)(2,1)S(1)} %add_convert_fusion.1), channel_id=1, source_target_pairs={{8,0},{16,24},{9,1},{17,25},{10,2},{18,26},{11,3},{19,27},{12,4},{... | collective-permute-start | bytes 3145736 | tf_op jit(solution)/shard_map/ppermute | solution.py:604
  793.3 61.2 %collective-permute-start.118 = (bf16[256,2048]{1,0:T(8,128)(2,1)S(1)}, bf16[256,2048]{1,0:T(8,128)(2,1)}, u32[]{:S(2)}, u32[]{:S(2)}) collective-permute-start(bf16[256,2048]{1,0:T(8,128)(2,1)S(1)} %broadcast_select_fusion.11.mine_ref), channel_id=1, source_target_pairs={{0,4},{4,0},{1,5},{5,1},{2,6},{6,2},{3,7},{7,3},{8,12},{12,8},{9,1... | collective-permute-start | bytes 3145736 | tf_op jit(solution)/shard_map/ppermute | solution.py:22
  795.7 56.6 %collective-permute-start.108 = (bf16[2048,256]{1,0:T(8,128)(2,1)S(1)}, bf16[2048,256]{1,0:T(8,128)(2,1)S(1)}, u32[]{:S(2)}, u32[]{:S(2)}) collective-permute-start(bf16[2048,256]{1,0:T(8,128)(2,1)S(1)} %add_convert_fusion.2), channel_id=1, source_target_pairs={{8,0},{16,24},{9,1},{17,25},{10,2},{18,26},{11,3},{19,27},{12,4},{... | collective-permute-start | bytes 3145736 | tf_op jit(solution)/shard_map/ppermute | solution.py:604
  815.8 42.4 %collective-permute-start.116 = (bf16[2048,256]{1,0:T(8,128)(2,1)S(1)}, bf16[2048,256]{1,0:T(8,128)(2,1)}, u32[]{:S(2)}, u32[]{:S(2)}) collective-permute-start(bf16[2048,256]{1,0:T(8,128)(2,1)S(1)} %broadcast_select_fusion.mine_ref), channel_id=1, source_target_pairs={{0,4},{4,0},{1,5},{5,1},{2,6},{6,2},{3,7},{7,3},{8,12},{12,8},{9,1... | collective-permute-start | bytes 3145736 | tf_op jit(solution)/shard_map/ppermute | solution.py:22
  (188 other events, 2966.5 us)

commit v4 on v3

--- a/solution.py
+++ b/solution.py
@@ -14,7 +14,10 @@
 EPS = 1e-06
 ROPE_BASE = 500000.0
 NEG_FILL = -1e30
-CHUNKS = 4
+PAIRS = [(0, 1), (1, 0), (2, 3), (3, 2)]
+INWARD = [(0, 1), (3, 2)]
+OUTWARD = [(1, 0), (2, 3)]
+ACROSS = [(1, 2), (2, 1), (0, 0), (3, 3)]
 
 
 def flip(value, axis, distance):
@@ -111,7 +114,7 @@
     return lax.dynamic_slice_in_dim(value, place * width, width, axis=1)
 
 
-def swap_halves(value):
+def both_halves(value):
     place = lax.axis_index("ctx")
     return half_columns(value, place), flip(half_columns(value, 1 - place), "ctx", 1)
 
@@ -308,81 +311,98 @@
     )(query_low, key_low, value, grad, lse, *turns)
 
 
-def store_kernel(place_ref, mine_ref, theirs_ref, *refs):
-    out_ref = refs[-1]
-
-    @pl.when(pl.program_id(0) == 0)
-    def _():
-        out_ref[...] = mine_ref[...].astype(jnp.float32)
-
-    @pl.when(pl.program_id(0) == 1)
-    def _():
-        out_ref[...] = theirs_ref[...].astype(jnp.float32)
-
-
-def store_chunk(buffer, mine, theirs, shape, index, chunks, by_rows):
+def store_kernel(place_ref, mine_ref, theirs_ref, *refs, outs):
+    width = mine_ref.shape[1] // outs
+    for side, half_ref in enumerate((mine_ref, theirs_ref)):
+
+        @pl.when(pl.program_id(0) == side)
+        def _():
+            for k, out_ref in enumerate(refs[-outs:]):
+                out_ref[...] = half_ref[:, k * width : (k + 1) * width].astype(jnp.float32)
+
+
+def store_chunk(buffers, mine, theirs, shapes, where_to):
     place = lax.axis_index("ctx").astype(jnp.int32).reshape(1)
     rows, columns = mine.shape
-    if by_rows:
-        where_to = lambda i, place_ref: ((place_ref[0] ^ i) * chunks + index, 0)
-    else:
-        where_to = lambda i, place_ref: (index, place_ref[0] ^ i)
-    whole = pl.BlockSpec((rows, columns), lambda i, place_ref: (0, 0))
+    outs = len(shapes)
+    block = min(128, rows)
+    steps = rows // block
     operands = [place, mine, theirs]
-    in_specs = [whole, whole]
+    in_specs = [
+        pl.BlockSpec((block, columns), lambda i, r, p: (r * (1 - i) + (steps - 1) * i, 0)),
+        pl.BlockSpec((block, columns), lambda i, r, p: (r * i, 0)),
+    ]
     aliases = {}
-    if buffer is not None:
-        operands.append(buffer)
-        in_specs.append(pl.BlockSpec(memory_space=pl.ANY))
-        aliases = {3: 0}
+    if buffers is not None:
+        operands.extend(buffers)
+        in_specs.extend([pl.BlockSpec(memory_space=pl.ANY)] * outs)
+        aliases = {3 + k: k for k in range(outs)}
+
+    def out_at(i, r, p):
+        row, column = where_to(p[0] ^ i)
+        return row * steps + r, column
+
     return pl.pallas_call(
-        store_kernel,
+        functools.partial(store_kernel, outs=outs),
         grid_spec=pltpu.PrefetchScalarGridSpec(
             num_scalar_prefetch=1,
-            grid=(2,),
+            grid=(2, steps),
             in_specs=in_specs,
-            out_specs=pl.BlockSpec((rows, columns), where_to),
+            out_specs=[pl.BlockSpec((block, columns // outs), out_at)] * outs,
         ),
-        out_shape=jax.ShapeDtypeStruct(shape, jnp.float32),
+        out_shape=[jax.ShapeDtypeStruct(shape, jnp.float32) for shape in shapes],
         input_output_aliases=aliases,
         name="store",
     )(*operands)
 
 
-class Gradient:
-    def __init__(self, name, shape, chunks, by_rows):
-        self.name, self.shape, self.chunks, self.by_rows = name, shape, chunks, by_rows
-        self.buffer = None
-        self.kept = {}
+class Gradients:
+    def __init__(self, shapes, row_chunks, column_chunks, by_rows):
+        self.shapes, self.by_rows = shapes, by_rows
+        self.row_chunks, self.column_chunks = row_chunks, column_chunks
+        self.chunks = row_chunks * column_chunks
+        self.buffers = None
+        self.kept = []
 
     def part(self, sides, index):
-        left_own, left_other, grad_own, grad_other = sides
-        rows = left_own.shape[1] // self.chunks
-        cut = functools.partial(
-            lax.slice_in_dim, start_index=index * rows, limit_index=(index + 1) * rows, axis=1
-        )
-        part = contract_rows(cut(left_own), grad_own) + contract_rows(cut(left_other), grad_other)
-        return part.astype(jnp.bfloat16)
+        left, grad = sides
+        row, column = divmod(index, self.column_chunks)
+        rows, columns = left.shape[1] // self.row_chunks, grad.shape[1] // self.column_chunks
+        left = lax.slice_in_dim(left, row * rows, (row + 1) * rows, axis=1)
+        grad = lax.slice_in_dim(grad, column * columns, (column + 1) * columns, axis=1)
+        return contract_rows(left, grad).astype(jnp.bfloat16)
 
     def store(self, index, mine, theirs):
-        if not self.by_rows and mine.shape[1] % 128:
-            self.kept[index] = (mine, theirs)
+        row, column = divmod(index, self.column_chunks)
+        if (mine.shape[1] // len(self.shapes)) % 128:
+            self.kept.append((mine, theirs))
             return
-        self.buffer = store_chunk(
-            self.buffer, mine, theirs, self.shape, index, self.chunks, self.by_rows
-        )
-
-    def result(self):
-        if self.buffer is not None:
-            return self.buffer
+        if self.by_rows:
+            where_to = lambda half: (half * self.row_chunks + row, column)
+        else:
+            where_to = lambda half: (row, half)
+        self.buffers = store_chunk(self.buffers, mine, theirs, self.shapes, where_to)
+
+    def results(self):
+        if self.buffers is not None:
+            return self.buffers
         first = lax.axis_index("ctx") == 0
-        pieces = [
-            jnp.concatenate(
-                [jnp.where(first, mine, theirs), jnp.where(first, theirs, mine)], axis=1
-            )
-            for _, (mine, theirs) in sorted(self.kept.items())
-        ]
-        return jnp.concatenate(pieces, axis=0).astype(jnp.float32)
+        width = self.kept[0][0].shape[1] // len(self.shapes)
+        found = []
+        for k in range(len(self.shapes)):
+            cut = lambda value: value[:, k * width : (k + 1) * width]
+            pieces = [
+                jnp.concatenate(
+                    [
+                        jnp.where(first, cut(mine), cut(theirs)),
+                        jnp.where(first, cut(theirs), cut(mine)),
+                    ],
+                    axis=1,
+                )
+                for mine, theirs in self.kept
+            ]
+            found.append(jnp.concatenate(pieces, axis=0).astype(jnp.float32))
+        return found
 
 
 def added(left, right):
@@ -456,16 +476,16 @@
     def to_owners(partial):
         return scatter_rows(row_blocks(partial, seq_count), "seq")
 
-    attn_halves = swap_halves(attn_low)
+    attn_other = flip(attn_low, "ctx", 1)
     attn_proj = to_owners(jnp.dot(attn_low, w_out, preferred_element_type=jnp.float32))
-    attn_proj, attn_halves = lax.optimization_barrier((attn_proj, attn_halves))
+    attn_proj, attn_other = lax.optimization_barrier((attn_proj, attn_other))
     inv_attn = lax.rsqrt(jnp.mean(attn_proj * attn_proj, axis=1, keepdims=True) + EPS)
     attn_unit = attn_proj * inv_attn
     hidden = tokens.astype(jnp.float32) + attn_unit * gain_attn
     hidden_low = hidden.astype(jnp.bfloat16)
     hidden_flip = flip(hidden_low, "ctx", 1)
     hidden_blocks, hidden_flip = gather_beside(hidden_low, "seq", hidden_flip)
-    hidden_own = stacked(hidden_blocks)
+    hidden_own = lax.optimization_barrier(stacked(hidden_blocks))
     hidden_rest = gather_rows(hidden_flip, "seq")
     gate_proj = jnp.dot(hidden_own, w_gate, preferred_element_type=jnp.float32)
     up_proj = jnp.dot(hidden_own, w_up, preferred_element_type=jnp.float32)
@@ -473,7 +493,7 @@
     swish = gate_proj * gate_sig
     inner_low = (swish * up_proj).astype(jnp.bfloat16)
     inner_low, hidden_rest = lax.optimization_barrier((inner_low, hidden_rest))
-    inner_halves = swap_halves(inner_low)
+    inner_halves = both_halves(inner_low)
     ffn = to_owners(jnp.dot(inner_low, w_down, preferred_element_type=jnp.float32))
     ffn, inner_halves = lax.optimization_barrier((ffn, inner_halves))
     inv_ffn = lax.rsqrt(jnp.mean(ffn * ffn, axis=1, keepdims=True) + EPS)
@@ -488,49 +508,43 @@
     gain_ffn_part = jnp.sum(grad_out * ffn_unit, axis=0)
     grad_ffn_low = norm_back(ffn_unit, inv_ffn, grad_out * gain_ffn).astype(jnp.bfloat16)
     grad_ffn_own, grad_ffn_other, _ = gather_both(grad_ffn_low, "seq")
-    grad_ffn_own, grad_ffn_other = stacked(grad_ffn_own), stacked(grad_ffn_other)
-    hidden_other = stacked(hidden_rest)
+    grad_ffn_both = stacked(grad_ffn_own + grad_ffn_other)
 
     grads = {
-        "down": Gradient("down", w_down.shape, CHUNKS, True),
-        "gate": Gradient("gate", w_gate.shape, CHUNKS, False),
-        "up": Gradient("up", w_up.shape, CHUNKS, False),
-        "out": Gradient("out", w_out.shape, 1, True),
-        "value": Gradient("value", w_value.shape, 1, False),
-        "key": Gradient("key", w_key.shape, 1, False),
-        "query": Gradient("query", w_query.shape, 1, False),
+        "down": Gradients([w_down.shape], 2, 2, True),
+        "gate": Gradients([w_gate.shape], 4, 1, False),
+        "up": Gradients([w_up.shape], 4, 1, False),
+        "out": Gradients([w_out.shape], 1, 1, False),
+        "in": Gradients([w_query.shape, w_key.shape, w_value.shape], 4, 1, False),
     }
-    sides = {"down": (*inner_halves, grad_ffn_own, grad_ffn_other)}
+    sides = {"down": (stacked(inner_halves), grad_ffn_both)}
     results = {}
 
     def stages():
-        (grad_ffn,) = yield (grad_ffn_own,)
+        (grad_ffn,) = yield (grad_ffn_both[:half_rows],)
         grad_inner = times_transpose(grad_ffn, w_down)
         grad_gate = (grad_inner * up_proj * gate_sig * (1.0 + gate_proj * (1.0 - gate_sig))).astype(
             jnp.bfloat16
         )
         grad_up = (grad_inner * swish).astype(jnp.bfloat16)
         grad_gate, grad_up = yield (grad_gate, grad_up)
-        gate_halves = swap_halves(grad_gate)
-        sides["gate"] = (hidden_own, hidden_other, *gate_halves)
+        hidden_both = stacked([hidden_own] + hidden_rest)
+        sides["gate"] = (hidden_both, stacked(both_halves(grad_gate)))
         gate_share = times_transpose(grad_gate, w_gate)
         gate_share, grad_up = yield (gate_share, grad_up)
-        up_halves = swap_halves(grad_up)
-        sides["up"] = (hidden_own, hidden_other, *up_halves)
+        sides["up"] = (hidden_both, stacked(both_halves(grad_up)))
         partial = gate_share + times_transpose(grad_up, w_up)
         (partial,) = yield (partial,)
         grad_hidden = grad_out + to_owners(partial)
         (grad_hidden,) = yield (grad_hidden,)
         gain_attn_part = jnp.sum(grad_hidden * attn_unit, axis=0)
         grad_proj_low = norm_back(attn_unit, inv_attn, grad_hidden * gain_attn).astype(jnp.bfloat16)
-        grad_proj_flip = flip(grad_proj_low, "ctx", 1)
         grad_proj_own = stacked(gather_rows(grad_proj_low, "seq"))
-        grad_proj_own, grad_proj_flip = yield (grad_proj_own, grad_proj_flip)
-        grad_proj_rest = gather_rows(grad_proj_flip, "seq")
+        (grad_proj_own,) = yield (grad_proj_own,)
+        sides["out"] = (stacked([attn_low, attn_other]), stacked(both_halves(grad_proj_own)))
         grad_attn_low = times_transpose(grad_proj_own, w_out).astype(jnp.bfloat16)
         backs = attend_back(query_low, key_low, value_low, grad_attn_low, lse, turns, block_rows)
-        backs, grad_proj_rest = yield (backs, grad_proj_rest)
-        sides["out"] = (*attn_halves, grad_proj_own, stacked(grad_proj_rest))
+        backs = yield backs
         grad_query_norm, own_dk, own_dv, prev_dk, prev_dv = backs
         back_dk, back_dv = lax.ppermute((prev_dk, prev_dv), "ctx", [(1, 0)])
         grad_query_norm, own_dk, own_dv, back_dk, back_dv = yield (
@@ -567,77 +581,83 @@
         grad_value_low, grad_key_low, grad_query_low, gains = yield (
             grad_value_low, grad_key_low, grad_query_low, gains
         )
-        value_halves = swap_halves(grad_value_low)
-        key_halves = swap_halves(grad_key_low)
-        query_halves = swap_halves(grad_query_low)
-        sides["value"] = (tokens_own, tokens_other, *value_halves)
-        sides["key"] = (tokens_own, tokens_other, *key_halves)
-        sides["query"] = (tokens_own, tokens_other, *query_halves)
-        gains = gains + flip(gains, "ctx", 1)
+        place = ctx_place
+        lows = (grad_query_low, grad_key_low, grad_value_low)
+        mine = jnp.concatenate([half_columns(low, place) for low in lows], axis=1)
+        given = jnp.concatenate([half_columns(low, 1 - place) for low in lows], axis=1)
+        sides["in"] = (
+            stacked([tokens_own, tokens_other]),
+            stacked([mine, flip(given, "ctx", 1)]),
+        )
+        gains_other = flip(gains, "ctx", 1)
         partial = (
             times_transpose(grad_query_low, w_query)
             + times_transpose(grad_key_low, w_key)
             + times_transpose(grad_value_low, w_value)
         )
-        partial, gains = yield (partial, gains)
-        results["gains"] = gains
+        partial, gains, gains_other = yield (partial, gains, gains_other)
+        gains = gains + gains_other
+        gains_pair = lax.ppermute(gains, "dp", PAIRS)
         grad_tokens = grad_hidden + to_owners(partial)
-        (grad_tokens,) = yield (grad_tokens,)
+        grad_tokens, gains, gains_pair = yield (grad_tokens, gains, gains_pair)
         results["tokens"] = grad_tokens
+        gains = gains + gains_pair
+        gains_across = lax.ppermute(gains, "dp", ACROSS)
+        gains, gains_across = yield (gains, gains_across)
+        gains = gains + gains_across
+        gains_out = lax.ppermute(gains, "dp", PAIRS)
+        gains, gains_out = yield (gains, gains_out)
+        results["gains"] = jnp.where(middle, gains, gains_out)
 
     plan = [(name, index) for name in grads for index in range(grads[name].chunks)]
     count = len(plan)
-    rider = count - 1
-    across_at = {chunk + (2 if chunk else 1): chunk for chunk in range(count)}
-    out_at = {tick + 1: chunk for tick, chunk in across_at.items()}
-    half_at = {tick + 1: chunk for tick, chunk in out_at.items()}
-    store_at = {tick + 1: chunk for tick, chunk in half_at.items()}
-    part, pair, total, final = {}, {}, {}, {}
+    part, pair, sent, final = {}, {}, {}, {}
     got_in, got_across, got_out, got_half = {}, {}, {}, {}
     main = stages()
     state = next(main)
-    last_name, last_buffer = None, None
+    last_name, last_buffers = None, None
     token = picked
-    part[0] = (grads[plan[0][0]].part(sides[plan[0][0]], 0),)
-
-    def send(values, axis, pairs):
-        return tuple(lax.ppermute(value, axis, pairs) for value in values)
-
-    for tick in range(max(store_at) + 1):
+    part[0] = grads[plan[0][0]].part(sides[plan[0][0]], 0)
+
+    for tick in range(count + 5):
+        crossing = None
+        if tick - 1 in part:
+            crossing = added(part[tick - 1], got_in[tick - 1])
+        coming = sides.get(plan[tick + 1][0]) if tick + 1 < count else None
+        held = (crossing, state, coming, last_buffers, token)
+        crossing, state, coming, last_buffers, token = lax.optimization_barrier(held)
+        if last_name:
+            grads[last_name].buffers = last_buffers
+        if crossing is not None:
+            pair[tick - 1] = crossing
+            got_across[tick - 1] = lax.ppermute(crossing, "dp", ACROSS)
         entering = part.get(tick)
-        chunk = across_at.get(tick)
-        crossing = None
-        if chunk is not None:
-            crossing = jax.tree.map(added, part[chunk], got_in[chunk])
-        coming = sides.get(plan[tick + 1][0]) if tick + 1 < count else None
-        held = (entering, crossing, state, coming, last_buffer, token)
-        entering, crossing, state, coming, last_buffer, token = lax.optimization_barrier(held)
-        if last_name:
-            grads[last_name].buffer = last_buffer
-        if crossing is not None:
-            pair[chunk] = crossing
-            got_across[chunk] = send(crossing, "dp", [(1, 2), (2, 1)])
-        if entering is not None:
-            part[tick] = entering
-            got_in[tick] = send(entering, "dp", [(0, 1), (3, 2)])
-        if tick in out_at:
-            chunk = out_at[tick]
-            leaving = jax.tree.map(added, pair[chunk], got_across[chunk])
-            total[chunk], token = lax.optimization_barrier((leaving, token))
-            got_out[chunk] = send(total[chunk], "dp", [(1, 0), (2, 3)])
-        if tick in half_at:
-            chunk = half_at[tick]
-            swapping = jax.tree.map(
-                lambda kept, got: jnp.where(middle, kept, got), total[chunk], got_out[chunk]
-            )
-            final[chunk], token = lax.optimization_barrier((swapping, token))
-            got_half[chunk] = flip(final[chunk][0], "ctx", 1)
-        if tick in store_at:
-            chunk = store_at[tick]
-            theirs, token = lax.optimization_barrier((got_half[chunk], token))
-            last_name, index = plan[chunk]
-            grads[last_name].store(index, final[chunk][0], theirs)
-            last_buffer = grads[last_name].buffer
+        leaving = None
+        if tick - 2 in pair:
+            leaving = added(pair[tick - 2], got_across[tick - 2])
+        if entering is not None and leaving is not None and entering.shape == leaving.shape:
+            held = (jnp.where(middle, leaving, entering), token)
+            sent[tick - 2], token = lax.optimization_barrier(held)
+            got_in[tick] = got_out[tick - 2] = lax.ppermute(sent[tick - 2], "dp", PAIRS)
+        else:
+            entering, leaving, token = lax.optimization_barrier((entering, leaving, token))
+            if entering is not None:
+                part[tick] = entering
+                got_in[tick] = lax.ppermute(entering, "dp", PAIRS if leaving is None else INWARD)
+            if leaving is not None:
+                sent[tick - 2] = leaving
+                got_out[tick - 2] = lax.ppermute(
+                    leaving, "dp", PAIRS if entering is None else OUTWARD
+                )
+        if tick - 3 in sent:
+            swapping = jnp.where(middle, sent[tick - 3], got_out[tick - 3])
+            final[tick - 3], token = lax.optimization_barrier((swapping, token))
+            got_half[tick - 3] = flip(final[tick - 3], "ctx", 1)
+        if tick - 4 in final:
+            theirs, token = lax.optimization_barrier((got_half[tick - 4], token))
+            last_name, index = plan[tick - 4]
+            grads[last_name].store(index, final[tick - 4], theirs)
+            last_buffers = grads[last_name].buffers
         try:
             state = main.send(state)
         except StopIteration:
@@ -645,10 +665,10 @@
         if tick + 1 < count:
             name, index = plan[tick + 1]
             coming = sides[name] if coming is None else coming
-            rides = (results["gains"],) if tick + 1 == rider else ()
-            part[tick + 1] = (grads[name].part(coming, index),) + rides
-
-    gains = final[rider][1].reshape(-1)
+            part[tick + 1] = grads[name].part(coming, index)
+
+    gains = results["gains"].reshape(-1)
+    grad_w_query, grad_w_key, grad_w_value = grads["in"].results()
     grad_gain_attn = gains[:D]
     grad_gain_ffn = gains[D : 2 * D]
     grad_gain_query = gains[2 * D : 2 * D + head_width]
@@ -656,16 +676,16 @@
     return (
         out_tokens,
         results["tokens"],
-        grads["query"].result(),
-        grads["key"].result(),
-        grads["value"].result(),
+        grad_w_query,
+        grad_w_key,
+        grad_w_value,
         grad_gain_query,
         grad_gain_key,
-        grads["out"].result(),
+        *grads["out"].results(),
         grad_gain_attn,
-        grads["gate"].result(),
-        grads["up"].result(),
-        grads["down"].result(),
+        *grads["gate"].results(),
+        *grads["up"].results(),
+        *grads["down"].results(),
         grad_gain_ffn,
     )
 

time: 890 us -> 900 us (1.011)
  Pallas kernels: 96.6 us -> 141 us
  matrix products: 124 us -> 96.9 us
  waiting for transfers between devices: 263 us -> 249 us
    pallas_call x16 -> x17, Pallas kernels: 59.5 us -> 104 us  [store_chunk(): pl.pallas_call(functools.partial(store_kernel, outs=outs), grid_spec=pltp...]
    convert_element_type x32 -> x21, other arithmetic: 70.3 us -> 39.7 us  [added(): (left.astype(jnp.float32) + right.astype(jnp.float32)).astype(left.dtype)]
    select_n x17 -> x31, other arithmetic: 26.2 us -> 56.4 us  [the longest x13 31.2 us: body(): held = (jnp.where(middle, leaving, entering), token)]
    ppermute x51 -> x41, waiting for transfers between devices: 125 us -> 98.4 us  [the longest x13 43 us: body(): got_in[tick] = got_out[tick - 2] = lax.ppermute(sent[tick - 2], 'dp', PAIRS)]
    ppermute x2, waiting for transfers between devices: 1.47 us -> 26.1 us  [stages(): back_dk, back_dv = lax.ppermute((prev_dk, prev_dv), 'ctx', [(1, 0)])]
    dot_general x32 -> x17, matrix products: 60 us -> 41.9 us  [contract_rows(): lax.dot_general(left, right, (((0,), (0,)), ((), ())), preferred_element_...]
    ppermute x66 -> x62, waiting for transfers between devices: 137 us -> 124 us  [flip(): lax.ppermute(value, axis, [(place, place ^ distance) for place in range(c...]
    ppermute x51 -> x41, starting transfers between devices: 159 us -> 166 us  [the longest x17 85.1 us: body(): got_across[tick - 1] = lax.ppermute(crossing, 'dp', ACROSS)]
  transfers between devices with their start and end apart: 119 -> 105, of which waited for: 43 -> 36; matrix products, arithmetic and copies ran while one was open for 28% -> 27% of each run, Pallas kernels for 9% -> 13%
where the time goes in v4:
time: 900 us; the launch traced here: 887 us
  waiting for transfers between devices  249 us (28%)
  starting transfers between devices  211 us (23%)
  Pallas kernels  141 us (16%)
  other arithmetic  139 us (15%)
  matrix products  96.9 us (11%)
  local copies, waits for them, and re-layouts  28.1 us (3%)
  blocking collectives  18.7 us (2%)
    ppermute x62, waiting for transfers between devices, flip(): lax.ppermute(value, axis, [(place, place ^ distance) for place in range(c...  124 us
    pallas_call x17, Pallas kernels, store_chunk(): pl.pallas_call(functools.partial(store_kernel, outs=outs), grid_spec=pltp...  104 us
    ppermute x17, starting transfers between devices, body(): got_across[tick - 1] = lax.ppermute(crossing, 'dp', ACROSS)  85.1 us
    ppermute x13, waiting for transfers between devices, body(): got_in[tick] = got_out[tick - 2] = lax.ppermute(sent[tick - 2], 'dp', PAIRS)  43 us
    ppermute x62, starting transfers between devices, flip(): lax.ppermute(value, axis, [(place, place ^ distance) for place in range(c...  42.3 us
    dot_general x17, matrix products, contract_rows(): lax.dot_general(left, right, (((0,), (0,)), ((), ())), preferred_element_...  41.9 us
    convert_element_type x21, other arithmetic, added(): (left.astype(jnp.float32) + right.astype(jnp.float32)).astype(left.dtype)  39.7 us
    dot_general x7, matrix products, times_transpose(): lax.dot_general(left, right, (((1,), (1,)), ((), ())), preferred_element_...  34.2 us
  transfers between devices with their start and end apart: 105, of which 36 were waited for; matrix products, arithmetic and copies ran while one was open for 27% of the time, Pallas kernels for 13%

profile of v4, /device:TPU:0, one launch (start us, length us, event | category | flops | bytes accessed | tf_op | source)
XLA Modules:
  0.0 887.3 jit_solution(17996622792552563810)
XLA Ops:
  5.3 10.5 %collective-permute-done.3.refs_0_ = bf16[128,2048]{1,0:T(8,128)(2,1)S(1)} collective-permute-done((bf16[128,2048]{1,0:T(8,128)(2,1)}, bf16[128,2048]{1,0:T(8,128)(2,1)S(1)}, u32[]{:S(2)}, u32[]{:S(2)}) %collective-permute-start.3) | collective-permute-done | bytes 524320 | tf_op jit(solution)/shard_map/ppermute | solution.py:25
  56.4 11.8 %attend.1 = (bf16[512,512]{1,0:T(8,128)(2,1)}, bf16[1024,512]{1,0:T(8,128)(2,1)}, bf16[1024,512]{1,0:T(8,128)(2,1)}, bf16[512,512]{1,0:T(8,128)(2,1)}, f32[4,512,1]{2,1,0:T(8,128)}) custom-call(f32[512,512]{1,0:T(8,128)} %get-tuple-element.267.query_ref, f32[512,512]{1,0:T(8,128)} %get-tuple-element.268.key_ref, ...), custom_call_target="tpu_custom_call" | custom-call | tf_op jit(solution)/shard_map/attend/pallas_call | solution.py:263
  73.7 13.1 %collective-permute-done.10 = bf16[128,2048]{1,0:T(8,128)(2,1)S(1)} collective-permute-done((bf16[128,2048]{1,0:T(8,128)(2,1)S(1)}, bf16[128,2048]{1,0:T(8,128)(2,1)S(1)}, u32[]{:S(2)}, u32[]{:S(2)}) %collective-permute-start.10) | collective-permute-done | bytes 524320 | tf_op jit(solution)/shard_map/ppermute | solution.py:25
  90.2 11.4 %collective-permute-done.13 = bf16[128,2048]{1,0:T(8,128)(2,1)} collective-permute-done((bf16[128,2048]{1,0:T(8,128)(2,1)}, bf16[128,2048]{1,0:T(8,128)(2,1)}, u32[]{:S(2)}, u32[]{:S(2)}) %collective-permute-start.13) | collective-permute-done | bytes 524320 | tf_op jit(solution)/shard_map/ppermute | solution.py:25
  136.7 11.4 %collective-permute-done.21 = bf16[128,2048]{1,0:T(8,128)(2,1)S(1)} collective-permute-done((bf16[128,2048]{1,0:T(8,128)(2,1)S(1)}, bf16[128,2048]{1,0:T(8,128)(2,1)S(1)}, u32[]{:S(2)}, u32[]{:S(2)}) %collective-permute-start.21) | collective-permute-done | bytes 524320 | tf_op jit(solution)/shard_map/ppermute | solution.py:25
  148.3 10.6 %collective-permute-done.22 = bf16[512,1024]{1,0:T(8,128)(2,1)S(1)} collective-permute-done((bf16[512,1024]{1,0:T(8,128)(2,1)S(1)}, bf16[512,1024]{1,0:T(8,128)(2,1)S(1)}, u32[]{:S(2)}, u32[]{:S(2)}) %collective-permute-start.22) | collective-permute-done | bytes 1048608 | tf_op jit(solution)/shard_map/ppermute | solution.py:25
  162.7 11.4 %collective-permute-done.24 = bf16[128,2048]{1,0:T(8,128)(2,1)S(1)} collective-permute-done((bf16[128,2048]{1,0:T(8,128)(2,1)S(1)}, bf16[128,2048]{1,0:T(8,128)(2,1)S(1)}, u32[]{:S(2)}, u32[]{:S(2)}) %collective-permute-start.24) | collective-permute-done | bytes 524320 | tf_op jit(solution)/shard_map/ppermute | solution.py:25
  191.4 10.5 %multiply_convert_fusion = (bf16[512,2048]{1,0:T(8,128)(2,1)S(1)}, bf16[512,2048]{1,0:T(8,128)(2,1)S(1)}) fusion(f32[512,2048]{1,0:T(8,128)} %copy-done.94, f32[512,2048]{1,0:T(8,128)} %get-tuple-element.569, bf16[512,2048]{1,0:T(8,128)(2,1)S(1)} %copy-done.64, bf16[2048,2048]{1,0:T(8,128)(2,1)} %param.29), kind=kOutput, calls=%fused_computation.5 | convolution fusion | flops 4308598784 | bytes 23068672 | tf_op jit(solution)/shard_map/dot_general | solution.py:107
  205.1 10.4 %collective-permute-done.31 = bf16[512,1024]{1,0:T(8,128)(2,1)} collective-permute-done((bf16[512,1024]{1,0:T(8,128)(2,1)}, bf16[512,1024]{1,0:T(8,128)(2,1)}, u32[]{:S(2)}, u32[]{:S(2)}) %collective-permute-start.31) | collective-permute-done | bytes 1048608 | tf_op jit(solution)/shard_map/ppermute | solution.py:646
  231.8 10.1 %collective-permute-done.32 = bf16[512,1024]{1,0:T(8,128)(2,1)S(1)} collective-permute-done((bf16[512,1024]{1,0:T(8,128)(2,1)S(1)}, bf16[512,1024]{1,0:T(8,128)(2,1)S(1)}, u32[]{:S(2)}, u32[]{:S(2)}) %collective-permute-start.32) | collective-permute-done | bytes 1048608 | tf_op jit(solution)/shard_map/ppermute | solution.py:646
  280.4 15.4 %collective-permute-done.37 = bf16[512,1024]{1,0:T(8,128)(2,1)S(1)} collective-permute-done((bf16[512,1024]{1,0:T(8,128)(2,1)S(1)}, bf16[512,1024]{1,0:T(8,128)(2,1)S(1)}, u32[]{:S(2)}, u32[]{:S(2)}) %collective-permute-start.37) | collective-permute-done | bytes 1048608 | tf_op jit(solution)/shard_map/ppermute | solution.py:641
  346.3 9.8 %collective-permute-start.51 = (bf16[512,1024]{1,0:T(8,128)(2,1)}, bf16[512,1024]{1,0:T(8,128)(2,1)}, u32[]{:S(2)}, u32[]{:S(2)}) collective-permute-start(bf16[512,1024]{1,0:T(8,128)(2,1)} %add_convert_fusion.17), channel_id=1, source_target_pairs={{8,16},{16,8},{0,0},{24,24},{9,17},{17,9},{1,1},{25,25},{10,18},{1... | collective-permute-start | bytes 3145736 | tf_op jit(solution)/shard_map/ppermute | solution.py:633
  365.9 11.1 %attend_back.1 = (f32[512,512]{1,0:T(8,128)}, f32[512,512]{1,0:T(8,128)}, f32[512,512]{1,0:T(8,128)}, bf16[512,512]{1,0:T(8,128)(2,1)}, bf16[512,512]{1,0:T(8,128)(2,1)}) custom-call(bf16[512,512]{1,0:T(8,128)(2,1)} %get-tuple-element.336.query_low_ref, bf16[1024,512]{1,0:T(8,128)(2,1)} %get-tuple-element.337.key_low_ref, ...), custom_call_target="tpu_custom_call" | custom-call | tf_op jit(solution)/shard_map/attend_back/pallas_call | solution.py:290
  421.7 14.9 %collective-permute-done.53 = bf16[512,512]{1,0:T(8,128)(2,1)} collective-permute-done((bf16[512,512]{1,0:T(8,128)(2,1)}, bf16[512,512]{1,0:T(8,128)(2,1)}, u32[]{:S(2)}, u32[]{:S(2)}) %collective-permute-start.53) | collective-permute-done | bytes 524320 | tf_op jit(solution)/shard_map/ppermute | solution.py:549
  436.5 11.2 %collective-permute-done.54 = bf16[512,512]{1,0:T(8,128)(2,1)} collective-permute-done((bf16[512,512]{1,0:T(8,128)(2,1)}, bf16[512,512]{1,0:T(8,128)(2,1)}, u32[]{:S(2)}, u32[]{:S(2)}) %collective-permute-start.54) | collective-permute-done | bytes 524320 | tf_op jit(solution)/shard_map/ppermute | solution.py:549
  454.8 11.0 %all-reduce = (f32[2,4,128]{2,0,1:T(2,128)S(1)}, f32[4096]{0:T(1024)S(1)}) all-reduce(f32[2,4,128]{2,0,1:T(2,128)S(1)} %select_bitcast_fusion.3, f32[4096]{0:T(1024)S(1)} %pad_maximum_fusion.10), channel_id=1, replica_groups=mesh['dp'=4,'ctx'=2,'seq'=4] {'seq'}, use_global_device_ids=true, to_apply=%region_8.11 | all-reduce | flops 5120 | bytes 40960 | tf_op jit(solution)/shard_map/psum | solution.py:561
  548.5 9.6 %collective-permute-start.70 = (bf16[512,1024]{1,0:T(8,128)(2,1)}, bf16[512,1024]{1,0:T(8,128)(2,1)}, u32[]{:S(2)}, u32[]{:S(2)}) collective-permute-start(bf16[512,1024]{1,0:T(8,128)(2,1)} %add_convert_fusion.9), channel_id=1, source_target_pairs={{8,16},{16,8},{0,0},{24,24},{9,17},{17,9},{1,1},{25,25},{10,18},{1... | collective-permute-start | bytes 3145736 | tf_op jit(solution)/shard_map/ppermute | solution.py:633
  628.7 11.1 %collective-permute-start.81 = (bf16[512,1024]{1,0:T(8,128)(2,1)S(1)}, bf16[512,1024]{1,0:T(8,128)(2,1)}, u32[]{:S(2)}, u32[]{:S(2)}) collective-permute-start(bf16[512,1024]{1,0:T(8,128)(2,1)S(1)} %fusion.30), channel_id=1, source_target_pairs={{0,8},{8,0},{16,24},{24,16},{1,9},{9,1},{17,25},{25,17},{2,10},{10... | collective-permute-start | bytes 3145736 | tf_op jit(solution)/shard_map/ppermute | solution.py:641
  653.6 17.4 %collective-permute-done.78 = f32[40,128]{1,0:T(8,128)S(1)} collective-permute-done((f32[40,128]{1,0:T(8,128)S(1)}, f32[40,128]{1,0:T(8,128)S(1)}, u32[]{:S(2)}, u32[]{:S(2)}) %collective-permute-start.78) | collective-permute-done | bytes 20512 | tf_op jit(solution)/shard_map/ppermute | solution.py:608
  689.4 16.8 %collective-permute-start.85 = (bf16[512,768]{1,0:T(8,128)(2,1)}, bf16[512,768]{1,0:T(8,128)(2,1)}, u32[]{:S(2)}, u32[]{:S(2)}) collective-permute-start(bf16[512,768]{1,0:T(8,128)(2,1)} %convolution_convert_fusion.11), channel_id=1, source_target_pairs={{0,8},{24,16},{1,9},{25,17},{2,10},{26,18},{3,11},{27,19},{4,12},{... | collective-permute-start | bytes 2359304 | tf_op jit(solution)/shard_map/ppermute | solution.py:646
  805.7 9.7 %collective-permute-start.98 = (bf16[512,768]{1,0:T(8,128)(2,1)S(1)}, bf16[512,768]{1,0:T(8,128)(2,1)S(1)}, u32[]{:S(2)}, u32[]{:S(2)}) collective-permute-start(bf16[512,768]{1,0:T(8,128)(2,1)S(1)} %add_convert_fusion.27), channel_id=1, source_target_pairs={{0,8},{8,0},{16,24},{24,16},{1,9},{9,1},{17,25},{25,17},{2,10},{10... | collective-permute-start | bytes 2359304 | tf_op jit(solution)/shard_map/ppermute | solution.py:649
  820.6 11.8 %collective-permute-done.98 = bf16[512,768]{1,0:T(8,128)(2,1)S(1)} collective-permute-done((bf16[512,768]{1,0:T(8,128)(2,1)S(1)}, bf16[512,768]{1,0:T(8,128)(2,1)S(1)}, u32[]{:S(2)}, u32[]{:S(2)}) %collective-permute-start.98) | collective-permute-done | bytes 786464 | tf_op jit(solution)/shard_map/ppermute | solution.py:649
  843.2 10.9 %collective-permute-done.103.theirs_ref = bf16[512,768]{1,0:T(8,128)(2,1)} collective-permute-done((bf16[512,768]{1,0:T(8,128)(2,1)S(1)}, bf16[512,768]{1,0:T(8,128)(2,1)}, u32[]{:S(2)}, u32[]{:S(2)}) %collective-permute-start.103) | collective-permute-done | bytes 786464 | tf_op jit(solution)/shard_map/ppermute | solution.py:25
  860.1 10.8 %collective-permute-done.102.theirs_ref = bf16[512,768]{1,0:T(8,128)(2,1)} collective-permute-done((bf16[512,768]{1,0:T(8,128)(2,1)S(1)}, bf16[512,768]{1,0:T(8,128)(2,1)}, u32[]{:S(2)}, u32[]{:S(2)}) %collective-permute-start.102) | collective-permute-done | bytes 786464 | tf_op jit(solution)/shard_map/ppermute | solution.py:25
  (597 shorter events, 601.1 us)
Async XLA Ops:
  256.6 129.7 %collective-permute-start.55 = (bf16[512,1024]{1,0:T(8,128)(2,1)}, bf16[512,1024]{1,0:T(8,128)(2,1)}, u32[]{:S(2)}, u32[]{:S(2)}) collective-permute-start(bf16[512,1024]{1,0:T(8,128)(2,1)} %get-tuple-element.536), channel_id=1, source_target_pairs={{0,4},{4,0},{1,5},{5,1},{2,6},{6,2},{3,7},{7,3},{8,12},{12,8},{9,1... | collective-permute-start | bytes 3145736 | tf_op jit(solution)/shard_map/ppermute | solution.py:25
  279.7 41.1 %collective-permute-start.47 = (bf16[512,1024]{1,0:T(8,128)(2,1)S(1)}, bf16[512,1024]{1,0:T(8,128)(2,1)S(1)}, u32[]{:S(2)}, u32[]{:S(2)}) collective-permute-start(bf16[512,1024]{1,0:T(8,128)(2,1)S(1)} %broadcast_select_fusion.12.mine_ref), channel_id=1, source_target_pairs={{0,4},{4,0},{1,5},{5,1},{2,6},{6,2},{3,7},{7,3},{8,12},{12,8},{9,1... | collective-permute-start | bytes 3145736 | tf_op jit(solution)/shard_map/ppermute | solution.py:25
  343.3 36.2 %collective-permute-start.48 = (bf16[512,1024]{1,0:T(8,128)(2,1)}, bf16[512,1024]{1,0:T(8,128)(2,1)}, u32[]{:S(2)}, u32[]{:S(2)}) collective-permute-start(bf16[512,1024]{1,0:T(8,128)(2,1)} %fusion.23), channel_id=1, source_target_pairs={{0,8},{8,0},{16,24},{24,16},{1,9},{9,1},{17,25},{25,17},{2,10},{10... | collective-permute-start | bytes 3145736 | tf_op jit(solution)/shard_map/ppermute | solution.py:641
  346.3 36.1 %collective-permute-start.51 = (bf16[512,1024]{1,0:T(8,128)(2,1)}, bf16[512,1024]{1,0:T(8,128)(2,1)}, u32[]{:S(2)}, u32[]{:S(2)}) collective-permute-start(bf16[512,1024]{1,0:T(8,128)(2,1)} %add_convert_fusion.17), channel_id=1, source_target_pairs={{8,16},{16,8},{0,0},{24,24},{9,17},{17,9},{1,1},{25,25},{10,18},{1... | collective-permute-start | bytes 3145736 | tf_op jit(solution)/shard_map/ppermute | solution.py:633
  359.2 44.9 %collective-permute-start.56 = (bf16[512,1024]{1,0:T(8,128)(2,1)}, bf16[512,1024]{1,0:T(8,128)(2,1)}, u32[]{:S(2)}, u32[]{:S(2)}) collective-permute-start(bf16[512,1024]{1,0:T(8,128)(2,1)} %broadcast_select_fusion.10.mine_ref), channel_id=1, source_target_pairs={{0,4},{4,0},{1,5},{5,1},{2,6},{6,2},{3,7},{7,3},{8,12},{12,8},{9,1... | collective-permute-start | bytes 3145736 | tf_op jit(solution)/shard_map/ppermute | solution.py:25
  388.0 59.8 %collective-permute-start.50 = (bf16[512,1024]{1,0:T(8,128)(2,1)}, bf16[512,1024]{1,0:T(8,128)(2,1)}, u32[]{:S(2)}, u32[]{:S(2)}) collective-permute-start(bf16[512,1024]{1,0:T(8,128)(2,1)} %add_convert_fusion.16), channel_id=1, source_target_pairs={{8,16},{16,8},{0,0},{24,24},{9,17},{17,9},{1,1},{25,25},{10,18},{1... | collective-permute-start | bytes 3145736 | tf_op jit(solution)/shard_map/ppermute | solution.py:633
  399.0 182.8 %collective-permute-start.73 = (bf16[512,1024]{1,0:T(8,128)(2,1)}, bf16[512,1024]{1,0:T(8,128)(2,1)}, u32[]{:S(2)}, u32[]{:S(2)}) collective-permute-start(bf16[512,1024]{1,0:T(8,128)(2,1)} %get-tuple-element.532), channel_id=1, source_target_pairs={{0,4},{4,0},{1,5},{5,1},{2,6},{6,2},{3,7},{7,3},{8,12},{12,8},{9,1... | collective-permute-start | bytes 3145736 | tf_op jit(solution)/shard_map/ppermute | solution.py:25
  400.5 36.1 %collective-permute-start.53 = (bf16[512,512]{1,0:T(8,128)(2,1)}, bf16[512,512]{1,0:T(8,128)(2,1)}, u32[]{:S(2)}, u32[]{:S(2)}) collective-permute-start(bf16[512,512]{1,0:T(8,128)(2,1)} %get-tuple-element.363), channel_id=1, source_target_pairs={{4,0},{5,1},{6,2},{7,3},{12,8},{13,9},{14,10},{15,11},{20,16},{21,... | collective-permute-start | bytes 1572872 | tf_op jit(solution)/shard_map/ppermute | solution.py:549
  404.1 43.7 %collective-permute-start.54 = (bf16[512,512]{1,0:T(8,128)(2,1)}, bf16[512,512]{1,0:T(8,128)(2,1)}, u32[]{:S(2)}, u32[]{:S(2)}) collective-permute-start(bf16[512,512]{1,0:T(8,128)(2,1)} %get-tuple-element.364), channel_id=1, source_target_pairs={{4,0},{5,1},{6,2},{7,3},{12,8},{13,9},{14,10},{15,11},{20,16},{21,... | collective-permute-start | bytes 1572872 | tf_op jit(solution)/shard_map/ppermute | solution.py:549
  414.8 55.4 %collective-permute-start.58 = (bf16[512,1024]{1,0:T(8,128)(2,1)}, bf16[512,1024]{1,0:T(8,128)(2,1)}, u32[]{:S(2)}, u32[]{:S(2)}) collective-permute-start(bf16[512,1024]{1,0:T(8,128)(2,1)} %broadcast_select_fusion.9.mine_ref), channel_id=1, source_target_pairs={{0,4},{4,0},{1,5},{5,1},{2,6},{6,2},{3,7},{7,3},{8,12},{12,8},{9,1... | collective-permute-start | bytes 3145736 | tf_op jit(solution)/shard_map/ppermute | solution.py:25
  450.9 42.2 %collective-permute-start.57 = (bf16[512,1024]{1,0:T(8,128)(2,1)}, bf16[512,1024]{1,0:T(8,128)(2,1)}, u32[]{:S(2)}, u32[]{:S(2)}) collective-permute-start(bf16[512,1024]{1,0:T(8,128)(2,1)} %fusion.25), channel_id=1, source_target_pairs={{0,8},{8,0},{16,24},{24,16},{1,9},{9,1},{17,25},{25,17},{2,10},{10... | collective-permute-start | bytes 3145736 | tf_op jit(solution)/shard_map/ppermute | solution.py:641
  470.2 35.6 %collective-permute-start.60 = (bf16[512,1024]{1,0:T(8,128)(2,1)}, bf16[512,1024]{1,0:T(8,128)(2,1)}, u32[]{:S(2)}, u32[]{:S(2)}) collective-permute-start(bf16[512,1024]{1,0:T(8,128)(2,1)} %add_convert_fusion.13), channel_id=1, source_target_pairs={{8,16},{16,8},{0,0},{24,24},{9,17},{17,9},{1,1},{25,25},{10,18},{1... | collective-permute-start | bytes 3145736 | tf_op jit(solution)/shard_map/ppermute | solution.py:633
  479.8 36.8 %collective-permute-start.63 = (bf16[512,1024]{1,0:T(8,128)(2,1)}, bf16[512,1024]{1,0:T(8,128)(2,1)}, u32[]{:S(2)}, u32[]{:S(2)}) collective-permute-start(bf16[512,1024]{1,0:T(8,128)(2,1)} %broadcast_select_fusion.8.mine_ref), channel_id=1, source_target_pairs={{0,4},{4,0},{1,5},{5,1},{2,6},{6,2},{3,7},{7,3},{8,12},{12,8},{9,1... | collective-permute-start | bytes 3145736 | tf_op jit(solution)/shard_map/ppermute | solution.py:25
  496.2 44.2 %collective-permute-start.59 = (bf16[512,1024]{1,0:T(8,128)(2,1)}, bf16[512,1024]{1,0:T(8,128)(2,1)}, u32[]{:S(2)}, u32[]{:S(2)}) collective-permute-start(bf16[512,1024]{1,0:T(8,128)(2,1)} %add_convert_fusion.12), channel_id=1, source_target_pairs={{8,16},{16,8},{0,0},{24,24},{9,17},{17,9},{1,1},{25,25},{10,18},{1... | collective-permute-start | bytes 3145736 | tf_op jit(solution)/shard_map/ppermute | solution.py:633
  567.1 34.4 %collective-permute-start.74 = (bf16[512,1024]{1,0:T(8,128)(2,1)S(1)}, bf16[512,1024]{1,0:T(8,128)(2,1)S(1)}, u32[]{:S(2)}, u32[]{:S(2)}) collective-permute-start(bf16[512,1024]{1,0:T(8,128)(2,1)S(1)} %copy-done.35), channel_id=1, source_target_pairs={{0,4},{4,0},{1,5},{5,1},{2,6},{6,2},{3,7},{7,3},{8,12},{12,8},{9,1... | collective-permute-start | bytes 3145736 | tf_op jit(solution)/shard_map/ppermute | solution.py:25
  596.9 43.2 %collective-permute-start.79 = (bf16[512,768]{1,0:T(8,128)(2,1)}, bf16[512,768]{1,0:T(8,128)(2,1)}, u32[]{:S(2)}, u32[]{:S(2)}) collective-permute-start(bf16[512,768]{1,0:T(8,128)(2,1)} %pad_maximum_fusion.8), channel_id=1, source_target_pairs={{0,4},{4,0},{1,5},{5,1},{2,6},{6,2},{3,7},{7,3},{8,12},{12,8},{9,1... | collective-permute-start | bytes 2359304 | tf_op jit(solution)/shard_map/ppermute | solution.py:25
  602.6 41.6 %collective-permute-start.80 = (bf16[512,1024]{1,0:T(8,128)(2,1)}, bf16[512,1024]{1,0:T(8,128)(2,1)}, u32[]{:S(2)}, u32[]{:S(2)}) collective-permute-start(bf16[512,1024]{1,0:T(8,128)(2,1)} %broadcast_select_fusion.5.mine_ref), channel_id=1, source_target_pairs={{0,4},{4,0},{1,5},{5,1},{2,6},{6,2},{3,7},{7,3},{8,12},{12,8},{9,1... | collective-permute-start | bytes 3145736 | tf_op jit(solution)/shard_map/ppermute | solution.py:25
  619.6 53.3 %collective-permute-start.82 = (bf16[512,1024]{1,0:T(8,128)(2,1)}, bf16[512,1024]{1,0:T(8,128)(2,1)}, u32[]{:S(2)}, u32[]{:S(2)}) collective-permute-start(bf16[512,1024]{1,0:T(8,128)(2,1)} %broadcast_select_fusion.4.mine_ref), channel_id=1, source_target_pairs={{0,4},{4,0},{1,5},{5,1},{2,6},{6,2},{3,7},{7,3},{8,12},{12,8},{9,1... | collective-permute-start | bytes 3145736 | tf_op jit(solution)/shard_map/ppermute | solution.py:25
  628.7 52.2 %collective-permute-start.81 = (bf16[512,1024]{1,0:T(8,128)(2,1)S(1)}, bf16[512,1024]{1,0:T(8,128)(2,1)}, u32[]{:S(2)}, u32[]{:S(2)}) collective-permute-start(bf16[512,1024]{1,0:T(8,128)(2,1)S(1)} %fusion.30), channel_id=1, source_target_pairs={{0,8},{8,0},{16,24},{24,16},{1,9},{9,1},{17,25},{25,17},{2,10},{10... | collective-permute-start | bytes 3145736 | tf_op jit(solution)/shard_map/ppermute | solution.py:641
  683.1 34.5 %collective-permute-start.83 = (bf16[512,1024]{1,0:T(8,128)(2,1)S(1)}, bf16[512,1024]{1,0:T(8,128)(2,1)}, u32[]{:S(2)}, u32[]{:S(2)}) collective-permute-start(bf16[512,1024]{1,0:T(8,128)(2,1)S(1)} %add_convert_fusion.2), channel_id=1, source_target_pairs={{8,16},{16,8},{0,0},{24,24},{9,17},{17,9},{1,1},{25,25},{10,18},{1... | collective-permute-start | bytes 3145736 | tf_op jit(solution)/shard_map/ppermute | solution.py:633
  689.4 36.4 %collective-permute-start.85 = (bf16[512,768]{1,0:T(8,128)(2,1)}, bf16[512,768]{1,0:T(8,128)(2,1)}, u32[]{:S(2)}, u32[]{:S(2)}) collective-permute-start(bf16[512,768]{1,0:T(8,128)(2,1)} %convolution_convert_fusion.11), channel_id=1, source_target_pairs={{0,8},{24,16},{1,9},{25,17},{2,10},{26,18},{3,11},{27,19},{4,12},{... | collective-permute-start | bytes 2359304 | tf_op jit(solution)/shard_map/ppermute | solution.py:646
  816.8 37.2 %collective-permute-start.103 = (bf16[512,768]{1,0:T(8,128)(2,1)S(1)}, bf16[512,768]{1,0:T(8,128)(2,1)}, u32[]{:S(2)}, u32[]{:S(2)}) collective-permute-start(bf16[512,768]{1,0:T(8,128)(2,1)S(1)} %broadcast_select_fusion.13.mine_ref), channel_id=1, source_target_pairs={{0,4},{4,0},{1,5},{5,1},{2,6},{6,2},{3,7},{7,3},{8,12},{12,8},{9,1... | collective-permute-start | bytes 2359304 | tf_op jit(solution)/shard_map/ppermute | solution.py:25
  820.5 50.4 %collective-permute-start.102 = (bf16[512,768]{1,0:T(8,128)(2,1)S(1)}, bf16[512,768]{1,0:T(8,128)(2,1)}, u32[]{:S(2)}, u32[]{:S(2)}) collective-permute-start(bf16[512,768]{1,0:T(8,128)(2,1)S(1)} %broadcast_select_fusion.14.mine_ref), channel_id=1, source_target_pairs={{0,4},{4,0},{1,5},{5,1},{2,6},{6,2},{3,7},{7,3},{8,12},{12,8},{9,1... | collective-permute-start | bytes 2359304 | tf_op jit(solution)/shard_map/ppermute | solution.py:25
  832.5 48.4 %collective-permute-start.99 = (bf16[512,768]{1,0:T(8,128)(2,1)S(1)}, bf16[512,768]{1,0:T(8,128)(2,1)}, u32[]{:S(2)}, u32[]{:S(2)}) collective-permute-start(bf16[512,768]{1,0:T(8,128)(2,1)S(1)} %broadcast_select_fusion.15.mine_ref), channel_id=1, source_target_pairs={{0,4},{4,0},{1,5},{5,1},{2,6},{6,2},{3,7},{7,3},{8,12},{12,8},{9,1... | collective-permute-start | bytes 2359304 | tf_op jit(solution)/shard_map/ppermute | solution.py:25
  (180 other events, 2496.0 us)

commit v5 on v4

--- a/solution.py
+++ b/solution.py
@@ -17,7 +17,7 @@
 PAIRS = [(0, 1), (1, 0), (2, 3), (3, 2)]
 INWARD = [(0, 1), (3, 2)]
 OUTWARD = [(1, 0), (2, 3)]
-ACROSS = [(1, 2), (2, 1), (0, 0), (3, 3)]
+ACROSS = [(1, 2), (2, 1)]
 
 
 def flip(value, axis, distance):
@@ -325,7 +325,7 @@
     place = lax.axis_index("ctx").astype(jnp.int32).reshape(1)
     rows, columns = mine.shape
     outs = len(shapes)
-    block = min(128, rows)
+    block = min(512, rows)
     steps = rows // block
     operands = [place, mine, theirs]
     in_specs = [
@@ -407,6 +407,42 @@
 
 def added(left, right):
     return (left.astype(jnp.float32) + right.astype(jnp.float32)).astype(left.dtype)
+
+
+def combine_kernel(
+    middle_ref, part_ref, got_ref, pair_ref, across_ref, sent_ref, next_ref,
+    pair_out_ref, sent_out_ref, final_out_ref,
+):
+    @pl.when(middle_ref[0] == 1)
+    def _():
+        pair_out_ref[...] = added(part_ref[...], got_ref[...])
+        sent_out_ref[...] = added(pair_ref[...], across_ref[...])
+        final_out_ref[...] = sent_ref[...]
+
+    @pl.when(middle_ref[0] == 0)
+    def _():
+        pair_out_ref[...] = part_ref[...]
+        sent_out_ref[...] = next_ref[...]
+        final_out_ref[...] = got_ref[...]
+
+
+def combine(middle, part, got, pair, across, sent, coming):
+    rows, columns = part.shape
+    block = min(256, rows)
+    every = pl.BlockSpec((block, columns), lambda r, m: (r, 0))
+    middles = pl.BlockSpec((block, columns), lambda r, m: (r * m[0], 0))
+    ends = pl.BlockSpec((block, columns), lambda r, m: (r * (1 - m[0]), 0))
+    return pl.pallas_call(
+        combine_kernel,
+        grid_spec=pltpu.PrefetchScalarGridSpec(
+            num_scalar_prefetch=1,
+            grid=(rows // block,),
+            in_specs=[every, every, middles, middles, middles, ends],
+            out_specs=[every] * 3,
+        ),
+        out_shape=[jax.ShapeDtypeStruct(part.shape, part.dtype)] * 3,
+        name="combine",
+    )(middle.astype(jnp.int32).reshape(1), part, got, pair, across, sent, coming)
 
 
 def body(
@@ -511,9 +547,9 @@
     grad_ffn_both = stacked(grad_ffn_own + grad_ffn_other)
 
     grads = {
-        "down": Gradients([w_down.shape], 2, 2, True),
-        "gate": Gradients([w_gate.shape], 4, 1, False),
-        "up": Gradients([w_up.shape], 4, 1, False),
+        "down": Gradients([w_down.shape], 1, 2, True),
+        "gate": Gradients([w_gate.shape], 2, 1, False),
+        "up": Gradients([w_up.shape], 2, 1, False),
         "out": Gradients([w_out.shape], 1, 1, False),
         "in": Gradients([w_query.shape, w_key.shape, w_value.shape], 4, 1, False),
     }
@@ -527,16 +563,13 @@
             jnp.bfloat16
         )
         grad_up = (grad_inner * swish).astype(jnp.bfloat16)
-        grad_gate, grad_up = yield (grad_gate, grad_up)
         hidden_both = stacked([hidden_own] + hidden_rest)
         sides["gate"] = (hidden_both, stacked(both_halves(grad_gate)))
         gate_share = times_transpose(grad_gate, w_gate)
-        gate_share, grad_up = yield (gate_share, grad_up)
         sides["up"] = (hidden_both, stacked(both_halves(grad_up)))
         partial = gate_share + times_transpose(grad_up, w_up)
         (partial,) = yield (partial,)
         grad_hidden = grad_out + to_owners(partial)
-        (grad_hidden,) = yield (grad_hidden,)
         gain_attn_part = jnp.sum(grad_hidden * attn_unit, axis=0)
         grad_proj_low = norm_back(attn_unit, inv_attn, grad_hidden * gain_attn).astype(jnp.bfloat16)
         grad_proj_own = stacked(gather_rows(grad_proj_low, "seq"))
@@ -544,7 +577,6 @@
         sides["out"] = (stacked([attn_low, attn_other]), stacked(both_halves(grad_proj_own)))
         grad_attn_low = times_transpose(grad_proj_own, w_out).astype(jnp.bfloat16)
         backs = attend_back(query_low, key_low, value_low, grad_attn_low, lse, turns, block_rows)
-        backs = yield backs
         grad_query_norm, own_dk, own_dv, prev_dk, prev_dv = backs
         back_dk, back_dv = lax.ppermute((prev_dk, prev_dv), "ctx", [(1, 0)])
         grad_query_norm, own_dk, own_dv, back_dk, back_dv = yield (
@@ -578,9 +610,6 @@
             jnp.bfloat16
         )
         gains = jnp.concatenate([gain_sums, gain_query_part, gain_key_part]).reshape(-1, 128)
-        grad_value_low, grad_key_low, grad_query_low, gains = yield (
-            grad_value_low, grad_key_low, grad_query_low, gains
-        )
         place = ctx_place
         lows = (grad_query_low, grad_key_low, grad_value_low)
         mine = jnp.concatenate([half_columns(low, place) for low in lows], axis=1)
@@ -620,39 +649,55 @@
     part[0] = grads[plan[0][0]].part(sides[plan[0][0]], 0)
 
     for tick in range(count + 5):
-        crossing = None
-        if tick - 1 in part:
-            crossing = added(part[tick - 1], got_in[tick - 1])
         coming = sides.get(plan[tick + 1][0]) if tick + 1 < count else None
-        held = (crossing, state, coming, last_buffers, token)
-        crossing, state, coming, last_buffers, token = lax.optimization_barrier(held)
+        arrived = (got_in.get(tick - 1), got_out.get(tick - 3), got_across.get(tick - 2))
+        if tick - 1 in got_in and got_in[tick - 1] is arrived[1]:
+            arrived = (arrived[0], None, arrived[2])
+        held = (arrived, part.get(tick), state, coming, last_buffers, token)
+        arrived, entering, state, coming, last_buffers, token = lax.optimization_barrier(held)
         if last_name:
             grads[last_name].buffers = last_buffers
+        if entering is not None:
+            part[tick] = entering
+        if tick - 1 in part:
+            got_in[tick - 1] = arrived[0]
+        if tick - 3 in sent:
+            got_out[tick - 3] = arrived[0] if arrived[1] is None else arrived[1]
+        if tick - 2 in pair:
+            got_across[tick - 2] = arrived[2]
+        alike = entering is not None and tick - 2 in pair and entering.shape == pair[tick - 2].shape
+        if alike and tick - 3 in sent and arrived[1] is None and arrived[0].shape == entering.shape:
+            pair[tick - 1], sent[tick - 2], final[tick - 3] = combine(
+                middle, part[tick - 1], arrived[0], pair[tick - 2], arrived[2], sent[tick - 3],
+                entering,
+            )
+        else:
+            if tick - 1 in part:
+                pair[tick - 1] = added(part[tick - 1], got_in[tick - 1])
+            if tick - 2 in pair:
+                leaving = added(pair[tick - 2], got_across[tick - 2])
+                sent[tick - 2] = jnp.where(middle, leaving, entering) if alike else leaving
+            if tick - 3 in sent:
+                final[tick - 3] = jnp.where(middle, sent[tick - 3], got_out[tick - 3])
+        held = (pair.get(tick - 1), sent.get(tick - 2), final.get(tick - 3), state, token)
+        crossing, leaving, swapping, state, token = lax.optimization_barrier(held)
         if crossing is not None:
             pair[tick - 1] = crossing
             got_across[tick - 1] = lax.ppermute(crossing, "dp", ACROSS)
-        entering = part.get(tick)
-        leaving = None
-        if tick - 2 in pair:
-            leaving = added(pair[tick - 2], got_across[tick - 2])
-        if entering is not None and leaving is not None and entering.shape == leaving.shape:
-            held = (jnp.where(middle, leaving, entering), token)
-            sent[tick - 2], token = lax.optimization_barrier(held)
-            got_in[tick] = got_out[tick - 2] = lax.ppermute(sent[tick - 2], "dp", PAIRS)
+        if leaving is not None:
+            sent[tick - 2] = leaving
+        if alike:
+            got_in[tick] = got_out[tick - 2] = lax.ppermute(leaving, "dp", PAIRS)
         else:
-            entering, leaving, token = lax.optimization_barrier((entering, leaving, token))
             if entering is not None:
-                part[tick] = entering
                 got_in[tick] = lax.ppermute(entering, "dp", PAIRS if leaving is None else INWARD)
             if leaving is not None:
-                sent[tick - 2] = leaving
                 got_out[tick - 2] = lax.ppermute(
                     leaving, "dp", PAIRS if entering is None else OUTWARD
                 )
-        if tick - 3 in sent:
-            swapping = jnp.where(middle, sent[tick - 3], got_out[tick - 3])
-            final[tick - 3], token = lax.optimization_barrier((swapping, token))
-            got_half[tick - 3] = flip(final[tick - 3], "ctx", 1)
+        if swapping is not None:
+            final[tick - 3] = swapping
+            got_half[tick - 3] = flip(swapping, "ctx", 1)
         if tick - 4 in final:
             theirs, token = lax.optimization_barrier((got_half[tick - 4], token))
             last_name, index = plan[tick - 4]

time: 900 us -> 828 us (0.920)
  starting transfers between devices: 211 us -> 112 us
  waiting for transfers between devices: 249 us -> 348 us
  other arithmetic: 139 us -> 96.4 us
  Pallas kernels: 141 us -> 114 us
    ppermute x62 -> x56, waiting for transfers between devices: 124 us -> 228 us  [flip(): lax.ppermute(value, axis, [(place, place ^ distance) for place in range(c...]
    ppermute x17 -> x11, starting transfers between devices: 85.1 us -> 20.6 us  [body(): got_across[tick - 1] = lax.ppermute(crossing, 'dp', ACROSS)]
    pallas_call x17 -> x11, Pallas kernels: 104 us -> 55.1 us  [store_chunk(): pl.pallas_call(functools.partial(store_kernel, outs=outs), grid_spec=pltp...]
    select_n x30 -> x9, other arithmetic: 56.4 us -> 18.9 us  [the longest x7 10.9 us: body(): final[tick - 3] = jnp.where(middle, sent[tick - 3], got_out[tick - 3])]
    ppermute x13 -> x6, waiting for transfers between devices: 43 us -> 12.2 us  [body(): got_in[tick] = got_out[tick - 2] = lax.ppermute(leaving, 'dp', PAIRS)]
    pallas_call x0 -> x4, Pallas kernels: none -> 22.1 us  [combine(): pl.pallas_call(combine_kernel, grid_spec=pltpu.PrefetchScalarGridSpec(num...]
    ppermute x13 -> x6, starting transfers between devices: 32.6 us -> 16.4 us  [body(): got_in[tick] = got_out[tick - 2] = lax.ppermute(leaving, 'dp', PAIRS)]
    ppermute x4 -> x5, starting transfers between devices: 20.8 us -> 6.19 us  [body(): lax.ppermute(leaving, 'dp', PAIRS if entering is None else OUTWARD)]
  transfers between devices with their start and end apart: 105 -> 88, of which waited for: 36 -> 45; matrix products, arithmetic and copies ran while one was open for 27% -> 21% of each run, Pallas kernels for 13% -> 11%
where the time goes in v5:
time: 828 us; the launch traced here: 821 us
  waiting for transfers between devices  348 us (42%)
  Pallas kernels  114 us (14%)
  starting transfers between devices  112 us (14%)
  matrix products  103 us (12%)
  other arithmetic  96.4 us (12%)
  local copies, waits for them, and re-layouts  25.3 us (3%)
  blocking collectives  18.6 us (2%)
    ppermute x56, waiting for transfers between devices, flip(): lax.ppermute(value, axis, [(place, place ^ distance) for place in range(c...  228 us
    pallas_call x11, Pallas kernels, store_chunk(): pl.pallas_call(functools.partial(store_kernel, outs=outs), grid_spec=pltp...  55.1 us
    dot_general x11, matrix products, contract_rows(): lax.dot_general(left, right, (((0,), (0,)), ((), ())), preferred_element_...  42.2 us
    dot_general x7, matrix products, times_transpose(): lax.dot_general(left, right, (((1,), (1,)), ((), ())), preferred_element_...  38.4 us
    ppermute x56, starting transfers between devices, flip(): lax.ppermute(value, axis, [(place, place ^ distance) for place in range(c...  35.8 us
    convert_element_type x12, other arithmetic, added(): (left.astype(jnp.float32) + right.astype(jnp.float32)).astype(left.dtype)  35.8 us
    ppermute x5, waiting for transfers between devices, body(): lax.ppermute(entering, 'dp', PAIRS if leaving is None else INWARD)  33.9 us
    ppermute x5, waiting for transfers between devices, body(): lax.ppermute(leaving, 'dp', PAIRS if entering is None else OUTWARD)  29.8 us
  transfers between devices with their start and end apart: 88, of which 45 were waited for; matrix products, arithmetic and copies ran while one was open for 21% of the time, Pallas kernels for 11%

profile of v5, /device:TPU:0, one launch (start us, length us, event | category | flops | bytes accessed | tf_op | source)
XLA Modules:
  0.0 821.0 jit_solution(3903011673116139944)
XLA Ops:
  5.3 10.5 %collective-permute-done.3.refs_0_ = bf16[128,2048]{1,0:T(8,128)(2,1)S(1)} collective-permute-done((bf16[128,2048]{1,0:T(8,128)(2,1)}, bf16[128,2048]{1,0:T(8,128)(2,1)S(1)}, u32[]{:S(2)}, u32[]{:S(2)}) %collective-permute-start.3) | collective-permute-done | bytes 524320 | tf_op jit(solution)/shard_map/ppermute | solution.py:25
  56.2 11.9 %attend.1 = (bf16[512,512]{1,0:T(8,128)(2,1)}, bf16[1024,512]{1,0:T(8,128)(2,1)}, bf16[1024,512]{1,0:T(8,128)(2,1)}, bf16[512,512]{1,0:T(8,128)(2,1)}, f32[4,512,1]{2,1,0:T(8,128)}) custom-call(f32[512,512]{1,0:T(8,128)} %get-tuple-element.247.query_ref, f32[512,512]{1,0:T(8,128)} %get-tuple-element.248.key_ref, ...), custom_call_target="tpu_custom_call" | custom-call | tf_op jit(solution)/shard_map/attend/pallas_call | solution.py:263
  73.6 13.1 %collective-permute-done.10 = bf16[128,2048]{1,0:T(8,128)(2,1)S(1)} collective-permute-done((bf16[128,2048]{1,0:T(8,128)(2,1)S(1)}, bf16[128,2048]{1,0:T(8,128)(2,1)S(1)}, u32[]{:S(2)}, u32[]{:S(2)}) %collective-permute-start.10) | collective-permute-done | bytes 524320 | tf_op jit(solution)/shard_map/ppermute | solution.py:25
  89.4 11.1 %collective-permute-done.13 = bf16[128,2048]{1,0:T(8,128)(2,1)S(1)} collective-permute-done((bf16[128,2048]{1,0:T(8,128)(2,1)S(1)}, bf16[128,2048]{1,0:T(8,128)(2,1)S(1)}, u32[]{:S(2)}, u32[]{:S(2)}) %collective-permute-start.13) | collective-permute-done | bytes 524320 | tf_op jit(solution)/shard_map/ppermute | solution.py:25
  136.7 12.8 %collective-permute-done.21 = bf16[128,2048]{1,0:T(8,128)(2,1)S(1)} collective-permute-done((bf16[128,2048]{1,0:T(8,128)(2,1)S(1)}, bf16[128,2048]{1,0:T(8,128)(2,1)S(1)}, u32[]{:S(2)}, u32[]{:S(2)}) %collective-permute-start.21) | collective-permute-done | bytes 524320 | tf_op jit(solution)/shard_map/ppermute | solution.py:25
  163.0 12.7 %collective-permute-done.24 = bf16[128,2048]{1,0:T(8,128)(2,1)S(1)} collective-permute-done((bf16[128,2048]{1,0:T(8,128)(2,1)S(1)}, bf16[128,2048]{1,0:T(8,128)(2,1)S(1)}, u32[]{:S(2)}, u32[]{:S(2)}) %collective-permute-start.24) | collective-permute-done | bytes 524320 | tf_op jit(solution)/shard_map/ppermute | solution.py:25
  191.0 11.4 %multiply_convert_fusion = (bf16[512,2048]{1,0:T(8,128)(2,1)}, bf16[512,2048]{1,0:T(8,128)(2,1)S(1)}) fusion(f32[512,2048]{1,0:T(8,128)} %copy-done.81, f32[512,2048]{1,0:T(8,128)} %get-tuple-element.530, bf16[512,2048]{1,0:T(8,128)(2,1)S(1)} %pad_maximum_fusion.1, bf16[2048,2048]{1,0:T(8,128)(2,1)} %param.29), kind=kOutput, calls=%fused_computation.11 | convolution fusion | flops 4308598784 | bytes 23068672 | tf_op jit(solution)/shard_map/dot_general | solution.py:107
  229.0 9.6 %collective-permute-done.32 = bf16[512,1024]{1,0:T(8,128)(2,1)S(1)} collective-permute-done((bf16[512,1024]{1,0:T(8,128)(2,1)S(1)}, bf16[512,1024]{1,0:T(8,128)(2,1)S(1)}, u32[]{:S(2)}, u32[]{:S(2)}) %collective-permute-start.32) | collective-permute-done | bytes 1048608 | tf_op jit(solution)/shard_map/ppermute | solution.py:25
  240.1 19.9 %collective-permute-done.31 = bf16[1024,1024]{1,0:T(8,128)(2,1)S(1)} collective-permute-done((bf16[1024,1024]{1,0:T(8,128)(2,1)}, bf16[1024,1024]{1,0:T(8,128)(2,1)S(1)}, u32[]{:S(2)}, u32[]{:S(2)}) %collective-permute-start.31) | collective-permute-done | bytes 2097184 | tf_op jit(solution)/shard_map/ppermute | solution.py:693
  304.3 11.1 %collective-permute-done.33 = bf16[1024,1024]{1,0:T(8,128)(2,1)} collective-permute-done((bf16[1024,1024]{1,0:T(8,128)(2,1)}, bf16[1024,1024]{1,0:T(8,128)(2,1)}, u32[]{:S(2)}, u32[]{:S(2)}) %collective-permute-start.33) | collective-permute-done | bytes 2097184 | tf_op jit(solution)/shard_map/ppermute | solution.py:693
  336.7 11.1 %attend_back.1 = (f32[512,512]{1,0:T(8,128)}, f32[512,512]{1,0:T(8,128)}, f32[512,512]{1,0:T(8,128)}, bf16[512,512]{1,0:T(8,128)(2,1)}, bf16[512,512]{1,0:T(8,128)(2,1)}) custom-call(bf16[512,512]{1,0:T(8,128)(2,1)} %get-tuple-element.298.query_low_ref, bf16[1024,512]{1,0:T(8,128)(2,1)} %get-tuple-element.299.key_low_ref, ...), custom_call_target="tpu_custom_call" | custom-call | tf_op jit(solution)/shard_map/attend_back/pallas_call | solution.py:290
  364.7 11.2 %collective-permute-done.44 = bf16[512,512]{1,0:T(8,128)(2,1)S(1)} collective-permute-done((bf16[512,512]{1,0:T(8,128)(2,1)}, bf16[512,512]{1,0:T(8,128)(2,1)S(1)}, u32[]{:S(2)}, u32[]{:S(2)}) %collective-permute-start.44) | collective-permute-done | bytes 524320 | tf_op jit(solution)/shard_map/ppermute | solution.py:581
  391.6 11.1 %all-reduce = (f32[2,4,128]{2,0,1:T(2,128)S(1)}, f32[4096]{0:T(1024)S(1)}) all-reduce(f32[2,4,128]{2,0,1:T(2,128)S(1)} %select_bitcast_fusion.3, f32[4096]{0:T(1024)S(1)} %pad_maximum_fusion.10), channel_id=1, replica_groups=mesh['dp'=4,'ctx'=2,'seq'=4] {'seq'}, use_global_device_ids=true, to_apply=%region_8.11 | all-reduce | flops 5120 | bytes 40960 | tf_op jit(solution)/shard_map/psum | solution.py:593
  420.0 10.0 %collective-permute-done.46.got_ref = bf16[1024,1024]{1,0:T(8,128)(2,1)} collective-permute-done((bf16[1024,1024]{1,0:T(8,128)(2,1)}, bf16[1024,1024]{1,0:T(8,128)(2,1)}, u32[]{:S(2)}, u32[]{:S(2)}) %collective-permute-start.46) | collective-permute-done | bytes 2097184 | tf_op jit(solution)/shard_map/ppermute | solution.py:690
  478.2 12.4 %collective-permute-done.54 = f32[40,128]{1,0:T(8,128)S(1)} collective-permute-done((f32[40,128]{1,0:T(8,128)S(1)}, f32[40,128]{1,0:T(8,128)S(1)}, u32[]{:S(2)}, u32[]{:S(2)}) %collective-permute-start.54) | collective-permute-done | bytes 20512 | tf_op jit(solution)/shard_map/ppermute | solution.py:629
  506.6 26.6 %collective-permute-done.60 = bf16[512,768]{1,0:T(8,128)(2,1)S(1)} collective-permute-done((bf16[512,768]{1,0:T(8,128)(2,1)S(1)}, bf16[512,768]{1,0:T(8,128)(2,1)S(1)}, u32[]{:S(2)}, u32[]{:S(2)}) %collective-permute-start.60) | collective-permute-done | bytes 786464 | tf_op jit(solution)/shard_map/ppermute | solution.py:25
  569.7 10.8 %collective-permute-done.66.theirs_ref = bf16[1024,1024]{1,0:T(8,128)(2,1)} collective-permute-done((bf16[1024,1024]{1,0:T(8,128)(2,1)}, bf16[1024,1024]{1,0:T(8,128)(2,1)}, u32[]{:S(2)}, u32[]{:S(2)}) %collective-permute-start.66) | collective-permute-done | bytes 2097184 | tf_op jit(solution)/shard_map/ppermute | solution.py:25
  591.5 15.6 %collective-permute-done.65 = f32[40,128]{1,0:T(8,128)S(1)} collective-permute-done((f32[40,128]{1,0:T(8,128)S(1)}, f32[40,128]{1,0:T(8,128)S(1)}, u32[]{:S(2)}, u32[]{:S(2)}) %collective-permute-start.65) | collective-permute-done | bytes 20512 | tf_op jit(solution)/shard_map/ppermute | solution.py:637
  619.4 10.2 %collective-permute-start.67 = (bf16[512,768]{1,0:T(8,128)(2,1)}, bf16[512,768]{1,0:T(8,128)(2,1)}, u32[]{:S(2)}, u32[]{:S(2)}) collective-permute-start(bf16[512,768]{1,0:T(8,128)(2,1)} %convolution_convert_fusion.4), channel_id=1, source_target_pairs={{0,8},{24,16},{1,9},{25,17},{2,10},{26,18},{3,11},{27,19},{4,12},{... | collective-permute-start | bytes 2359304 | tf_op jit(solution)/shard_map/ppermute | solution.py:693
  643.5 22.8 %collective-permute-done.68 = bf16[1024,1024]{1,0:T(8,128)(2,1)} collective-permute-done((bf16[1024,1024]{1,0:T(8,128)(2,1)}, bf16[1024,1024]{1,0:T(8,128)(2,1)}, u32[]{:S(2)}, u32[]{:S(2)}) %collective-permute-start.68) | collective-permute-done | bytes 2097184 | tf_op jit(solution)/shard_map/ppermute | solution.py:695
  710.7 19.6 %collective-permute-done.77.theirs_ref = bf16[1024,1024]{1,0:T(8,128)(2,1)} collective-permute-done((bf16[1024,1024]{1,0:T(8,128)(2,1)S(1)}, bf16[1024,1024]{1,0:T(8,128)(2,1)}, u32[]{:S(2)}, u32[]{:S(2)}) %collective-permute-start.77) | collective-permute-done | bytes 2097184 | tf_op jit(solution)/shard_map/ppermute | solution.py:25
  742.1 10.6 %collective-permute-done.80.theirs_ref = bf16[512,1024]{1,0:T(8,128)(2,1)} collective-permute-done((bf16[512,1024]{1,0:T(8,128)(2,1)S(1)}, bf16[512,1024]{1,0:T(8,128)(2,1)}, u32[]{:S(2)}, u32[]{:S(2)}) %collective-permute-start.80) | collective-permute-done | bytes 1048608 | tf_op jit(solution)/shard_map/ppermute | solution.py:25
  779.1 9.9 %collective-permute-done.85.theirs_ref = bf16[512,768]{1,0:T(8,128)(2,1)} collective-permute-done((bf16[512,768]{1,0:T(8,128)(2,1)S(1)}, bf16[512,768]{1,0:T(8,128)(2,1)}, u32[]{:S(2)}, u32[]{:S(2)}) %collective-permute-start.85) | collective-permute-done | bytes 786464 | tf_op jit(solution)/shard_map/ppermute | solution.py:25
  795.1 10.6 %collective-permute-done.87.theirs_ref = bf16[512,768]{1,0:T(8,128)(2,1)S(1)} collective-permute-done((bf16[512,768]{1,0:T(8,128)(2,1)S(1)}, bf16[512,768]{1,0:T(8,128)(2,1)S(1)}, u32[]{:S(2)}, u32[]{:S(2)}) %collective-permute-start.87) | collective-permute-done | bytes 786464 | tf_op jit(solution)/shard_map/ppermute | solution.py:25
  (497 shorter events, 501.4 us)
Async XLA Ops:
  212.0 48.0 %collective-permute-start.31 = (bf16[1024,1024]{1,0:T(8,128)(2,1)}, bf16[1024,1024]{1,0:T(8,128)(2,1)S(1)}, u32[]{:S(2)}, u32[]{:S(2)}) collective-permute-start(bf16[1024,1024]{1,0:T(8,128)(2,1)} %fusion.29), channel_id=1, source_target_pairs={{0,8},{8,0},{16,24},{24,16},{1,9},{9,1},{17,25},{25,17},{2,10},{10... | collective-permute-start | bytes 6291464 | tf_op jit(solution)/shard_map/ppermute | solution.py:693
  267.7 47.7 %collective-permute-start.33 = (bf16[1024,1024]{1,0:T(8,128)(2,1)}, bf16[1024,1024]{1,0:T(8,128)(2,1)}, u32[]{:S(2)}, u32[]{:S(2)}) collective-permute-start(bf16[1024,1024]{1,0:T(8,128)(2,1)} %fusion.14), channel_id=1, source_target_pairs={{0,8},{8,0},{16,24},{24,16},{1,9},{9,1},{17,25},{25,17},{2,10},{10... | collective-permute-start | bytes 6291464 | tf_op jit(solution)/shard_map/ppermute | solution.py:693
  269.3 46.1 %collective-permute-start.34 = (bf16[1024,1024]{1,0:T(8,128)(2,1)}, bf16[1024,1024]{1,0:T(8,128)(2,1)}, u32[]{:S(2)}, u32[]{:S(2)}) collective-permute-start(bf16[1024,1024]{1,0:T(8,128)(2,1)} %add_convert_fusion.5), channel_id=1, source_target_pairs={{8,16},{16,8},{9,17},{17,9},{10,18},{18,10},{11,19},{19,11},{12,20... | collective-permute-start | bytes 6291464 | tf_op jit(solution)/shard_map/ppermute | solution.py:686
  287.3 44.3 %collective-permute-start.45 = (bf16[512,1024]{1,0:T(8,128)(2,1)}, bf16[512,1024]{1,0:T(8,128)(2,1)}, u32[]{:S(2)}, u32[]{:S(2)}) collective-permute-start(bf16[512,1024]{1,0:T(8,128)(2,1)} %get-tuple-element.497), channel_id=1, source_target_pairs={{0,4},{4,0},{1,5},{5,1},{2,6},{6,2},{3,7},{7,3},{8,12},{12,8},{9,1... | collective-permute-start | bytes 3145736 | tf_op jit(solution)/shard_map/ppermute | solution.py:25
  325.0 50.9 %collective-permute-start.41 = (bf16[1024,1024]{1,0:T(8,128)(2,1)}, bf16[1024,1024]{1,0:T(8,128)(2,1)}, u32[]{:S(2)}, u32[]{:S(2)}) collective-permute-start(bf16[1024,1024]{1,0:T(8,128)(2,1)} %fusion.1.sent_ref), channel_id=1, source_target_pairs={{0,8},{8,0},{16,24},{24,16},{1,9},{9,1},{17,25},{25,17},{2,10},{10... | collective-permute-start | bytes 6291464 | tf_op jit(solution)/shard_map/ppermute | solution.py:690
  329.6 46.3 %collective-permute-start.42 = (bf16[1024,1024]{1,0:T(8,128)(2,1)}, bf16[1024,1024]{1,0:T(8,128)(2,1)}, u32[]{:S(2)}, u32[]{:S(2)}) collective-permute-start(bf16[1024,1024]{1,0:T(8,128)(2,1)} %add_convert_fusion.4.pair_ref), channel_id=1, source_target_pairs={{8,16},{16,8},{9,17},{17,9},{10,18},{18,10},{11,19},{19,11},{12,20... | collective-permute-start | bytes 6291464 | tf_op jit(solution)/shard_map/ppermute | solution.py:686
  352.4 94.9 %collective-permute-start.55 = (bf16[512,1024]{1,0:T(8,128)(2,1)}, bf16[512,1024]{1,0:T(8,128)(2,1)}, u32[]{:S(2)}, u32[]{:S(2)}) collective-permute-start(bf16[512,1024]{1,0:T(8,128)(2,1)} %get-tuple-element.493), channel_id=1, source_target_pairs={{0,4},{4,0},{1,5},{5,1},{2,6},{6,2},{3,7},{7,3},{8,12},{12,8},{9,1... | collective-permute-start | bytes 3145736 | tf_op jit(solution)/shard_map/ppermute | solution.py:25
  383.1 46.9 %collective-permute-start.46 = (bf16[1024,1024]{1,0:T(8,128)(2,1)}, bf16[1024,1024]{1,0:T(8,128)(2,1)}, u32[]{:S(2)}, u32[]{:S(2)}) collective-permute-start(bf16[1024,1024]{1,0:T(8,128)(2,1)} %get-tuple-element.321.sent_ref), channel_id=1, source_target_pairs={{0,8},{8,0},{16,24},{24,16},{1,9},{9,1},{17,25},{25,17},{2,10},{10... | collective-permute-start | bytes 6291464 | tf_op jit(solution)/shard_map/ppermute | solution.py:690
  385.8 44.2 %collective-permute-start.47 = (bf16[1024,1024]{1,0:T(8,128)(2,1)}, bf16[1024,1024]{1,0:T(8,128)(2,1)}, u32[]{:S(2)}, u32[]{:S(2)}) collective-permute-start(bf16[1024,1024]{1,0:T(8,128)(2,1)} %get-tuple-element.322.pair_ref), channel_id=1, source_target_pairs={{8,16},{16,8},{9,17},{17,9},{10,18},{18,10},{11,19},{19,11},{12,20... | collective-permute-start | bytes 6291464 | tf_op jit(solution)/shard_map/ppermute | solution.py:686
  407.2 47.0 %collective-permute-start.56 = (bf16[1024,1024]{1,0:T(8,128)(2,1)}, bf16[1024,1024]{1,0:T(8,128)(2,1)}, u32[]{:S(2)}, u32[]{:S(2)}) collective-permute-start(bf16[1024,1024]{1,0:T(8,128)(2,1)} %get-tuple-element.349.mine_ref), channel_id=1, source_target_pairs={{0,4},{4,0},{1,5},{5,1},{2,6},{6,2},{3,7},{7,3},{8,12},{12,8},{9,1... | collective-permute-start | bytes 6291464 | tf_op jit(solution)/shard_map/ppermute | solution.py:25
  439.0 51.6 %collective-permute-start.49 = (bf16[1024,1024]{1,0:T(8,128)(2,1)}, bf16[1024,1024]{1,0:T(8,128)(2,1)}, u32[]{:S(2)}, u32[]{:S(2)}) collective-permute-start(bf16[1024,1024]{1,0:T(8,128)(2,1)} %get-tuple-element.341.sent_ref), channel_id=1, source_target_pairs={{0,8},{8,0},{16,24},{24,16},{1,9},{9,1},{17,25},{25,17},{2,10},{10... | collective-permute-start | bytes 6291464 | tf_op jit(solution)/shard_map/ppermute | solution.py:690
  443.8 46.9 %collective-permute-start.50 = (bf16[1024,1024]{1,0:T(8,128)(2,1)}, bf16[1024,1024]{1,0:T(8,128)(2,1)}, u32[]{:S(2)}, u32[]{:S(2)}) collective-permute-start(bf16[1024,1024]{1,0:T(8,128)(2,1)} %get-tuple-element.342.pair_ref), channel_id=1, source_target_pairs={{8,16},{16,8},{9,17},{17,9},{10,18},{18,10},{11,19},{19,11},{12,20... | collective-permute-start | bytes 6291464 | tf_op jit(solution)/shard_map/ppermute | solution.py:686
  470.3 67.3 %collective-permute-start.61 = (bf16[1024,1024]{1,0:T(8,128)(2,1)}, bf16[1024,1024]{1,0:T(8,128)(2,1)}, u32[]{:S(2)}, u32[]{:S(2)}) collective-permute-start(bf16[1024,1024]{1,0:T(8,128)(2,1)} %get-tuple-element.372.mine_ref), channel_id=1, source_target_pairs={{0,4},{4,0},{1,5},{5,1},{2,6},{6,2},{3,7},{7,3},{8,12},{12,8},{9,1... | collective-permute-start | bytes 6291464 | tf_op jit(solution)/shard_map/ppermute | solution.py:25
  497.0 49.7 %collective-permute-start.57 = (bf16[1024,1024]{1,0:T(8,128)(2,1)}, bf16[1024,1024]{1,0:T(8,128)(2,1)}, u32[]{:S(2)}, u32[]{:S(2)}) collective-permute-start(bf16[1024,1024]{1,0:T(8,128)(2,1)} %get-tuple-element.364), channel_id=1, source_target_pairs={{0,8},{8,0},{16,24},{24,16},{1,9},{9,1},{17,25},{25,17},{2,10},{10... | collective-permute-start | bytes 6291464 | tf_op jit(solution)/shard_map/ppermute | solution.py:690
  501.1 45.5 %collective-permute-start.58 = (bf16[1024,1024]{1,0:T(8,128)(2,1)}, bf16[1024,1024]{1,0:T(8,128)(2,1)}, u32[]{:S(2)}, u32[]{:S(2)}) collective-permute-start(bf16[1024,1024]{1,0:T(8,128)(2,1)} %get-tuple-element.365), channel_id=1, source_target_pairs={{8,16},{16,8},{9,17},{17,9},{10,18},{18,10},{11,19},{19,11},{12,20... | collective-permute-start | bytes 6291464 | tf_op jit(solution)/shard_map/ppermute | solution.py:686
  535.1 45.4 %collective-permute-start.66 = (bf16[1024,1024]{1,0:T(8,128)(2,1)}, bf16[1024,1024]{1,0:T(8,128)(2,1)}, u32[]{:S(2)}, u32[]{:S(2)}) collective-permute-start(bf16[1024,1024]{1,0:T(8,128)(2,1)} %get-tuple-element.389.mine_ref), channel_id=1, source_target_pairs={{0,4},{4,0},{1,5},{5,1},{2,6},{6,2},{3,7},{7,3},{8,12},{12,8},{9,1... | collective-permute-start | bytes 6291464 | tf_op jit(solution)/shard_map/ppermute | solution.py:25
  557.4 49.7 %collective-permute-start.63 = (bf16[1024,1024]{1,0:T(8,128)(2,1)}, bf16[1024,1024]{1,0:T(8,128)(2,1)}, u32[]{:S(2)}, u32[]{:S(2)}) collective-permute-start(bf16[1024,1024]{1,0:T(8,128)(2,1)} %add_convert_fusion.1), channel_id=1, source_target_pairs={{8,0},{16,24},{9,1},{17,25},{10,2},{18,26},{11,3},{19,27},{12,4},{... | collective-permute-start | bytes 6291464 | tf_op jit(solution)/shard_map/ppermute | solution.py:695
  558.7 48.5 %collective-permute-start.64 = (bf16[1024,1024]{1,0:T(8,128)(2,1)}, bf16[1024,1024]{1,0:T(8,128)(2,1)}, u32[]{:S(2)}, u32[]{:S(2)}) collective-permute-start(bf16[1024,1024]{1,0:T(8,128)(2,1)} %add_convert_fusion.2), channel_id=1, source_target_pairs={{8,16},{16,8},{9,17},{17,9},{10,18},{18,10},{11,19},{19,11},{12,20... | collective-permute-start | bytes 6291464 | tf_op jit(solution)/shard_map/ppermute | solution.py:686
  560.7 46.4 %collective-permute-start.62 = (bf16[512,1024]{1,0:T(8,128)(2,1)S(1)}, bf16[512,1024]{1,0:T(8,128)(2,1)}, u32[]{:S(2)}, u32[]{:S(2)}) collective-permute-start(bf16[512,1024]{1,0:T(8,128)(2,1)S(1)} %convolution_convert_fusion), channel_id=1, source_target_pairs={{0,8},{24,16},{1,9},{25,17},{2,10},{26,18},{3,11},{27,19},{4,12},{... | collective-permute-start | bytes 3145736 | tf_op jit(solution)/shard_map/ppermute | solution.py:693
  586.9 45.6 %collective-permute-start.70 = (bf16[1024,1024]{1,0:T(8,128)(2,1)S(1)}, bf16[1024,1024]{1,0:T(8,128)(2,1)}, u32[]{:S(2)}, u32[]{:S(2)}) collective-permute-start(bf16[1024,1024]{1,0:T(8,128)(2,1)S(1)} %broadcast_select_fusion.2.mine_ref), channel_id=1, source_target_pairs={{0,4},{4,0},{1,5},{5,1},{2,6},{6,2},{3,7},{7,3},{8,12},{12,8},{9,1... | collective-permute-start | bytes 6291464 | tf_op jit(solution)/shard_map/ppermute | solution.py:25
  616.5 49.8 %collective-permute-start.68 = (bf16[1024,1024]{1,0:T(8,128)(2,1)}, bf16[1024,1024]{1,0:T(8,128)(2,1)}, u32[]{:S(2)}, u32[]{:S(2)}) collective-permute-start(bf16[1024,1024]{1,0:T(8,128)(2,1)} %add_convert_fusion), channel_id=1, source_target_pairs={{8,0},{16,24},{9,1},{17,25},{10,2},{18,26},{11,3},{19,27},{12,4},{... | collective-permute-start | bytes 6291464 | tf_op jit(solution)/shard_map/ppermute | solution.py:695
  629.6 52.6 %collective-permute-start.74 = (bf16[1024,1024]{1,0:T(8,128)(2,1)}, bf16[1024,1024]{1,0:T(8,128)(2,1)}, u32[]{:S(2)}, u32[]{:S(2)}) collective-permute-start(bf16[1024,1024]{1,0:T(8,128)(2,1)} %broadcast_select_fusion.1.mine_ref), channel_id=1, source_target_pairs={{0,4},{4,0},{1,5},{5,1},{2,6},{6,2},{3,7},{7,3},{8,12},{12,8},{9,1... | collective-permute-start | bytes 6291464 | tf_op jit(solution)/shard_map/ppermute | solution.py:25
  681.7 48.6 %collective-permute-start.77 = (bf16[1024,1024]{1,0:T(8,128)(2,1)S(1)}, bf16[1024,1024]{1,0:T(8,128)(2,1)}, u32[]{:S(2)}, u32[]{:S(2)}) collective-permute-start(bf16[1024,1024]{1,0:T(8,128)(2,1)S(1)} %broadcast_select_fusion.mine_ref), channel_id=1, source_target_pairs={{0,4},{4,0},{1,5},{5,1},{2,6},{6,2},{3,7},{7,3},{8,12},{12,8},{9,1... | collective-permute-start | bytes 6291464 | tf_op jit(solution)/shard_map/ppermute | solution.py:25
  707.0 45.8 %collective-permute-start.80 = (bf16[512,1024]{1,0:T(8,128)(2,1)S(1)}, bf16[512,1024]{1,0:T(8,128)(2,1)}, u32[]{:S(2)}, u32[]{:S(2)}) collective-permute-start(bf16[512,1024]{1,0:T(8,128)(2,1)S(1)} %broadcast_select_fusion.3.mine_ref), channel_id=1, source_target_pairs={{0,4},{4,0},{1,5},{5,1},{2,6},{6,2},{3,7},{7,3},{8,12},{12,8},{9,1... | collective-permute-start | bytes 3145736 | tf_op jit(solution)/shard_map/ppermute | solution.py:25
  (150 other events, 1884.6 us)

commit v6 on v5

--- a/solution.py
+++ b/solution.py
@@ -12,6 +12,7 @@
 
 
 EPS = 1e-06
+STEP = 2
 ROPE_BASE = 500000.0
 NEG_FILL = -1e30
 PAIRS = [(0, 1), (1, 0), (2, 3), (3, 2)]
@@ -547,9 +548,9 @@
     grad_ffn_both = stacked(grad_ffn_own + grad_ffn_other)
 
     grads = {
-        "down": Gradients([w_down.shape], 1, 2, True),
-        "gate": Gradients([w_gate.shape], 2, 1, False),
-        "up": Gradients([w_up.shape], 2, 1, False),
+        "down": Gradients([w_down.shape], 2, 2, True),
+        "gate": Gradients([w_gate.shape], 4, 1, False),
+        "up": Gradients([w_up.shape], 4, 1, False),
         "out": Gradients([w_out.shape], 1, 1, False),
         "in": Gradients([w_query.shape, w_key.shape, w_value.shape], 4, 1, False),
     }
@@ -563,25 +564,32 @@
             jnp.bfloat16
         )
         grad_up = (grad_inner * swish).astype(jnp.bfloat16)
+        grad_gate, grad_up = yield (grad_gate, grad_up)
+        gate_halves = both_halves(grad_gate)
+        up_halves = both_halves(grad_up)
+        gate_share = times_transpose(grad_gate, w_gate)
+        gate_share, gate_halves = yield (gate_share, gate_halves)
         hidden_both = stacked([hidden_own] + hidden_rest)
-        sides["gate"] = (hidden_both, stacked(both_halves(grad_gate)))
-        gate_share = times_transpose(grad_gate, w_gate)
-        sides["up"] = (hidden_both, stacked(both_halves(grad_up)))
+        sides["gate"] = (hidden_both, stacked(gate_halves))
         partial = gate_share + times_transpose(grad_up, w_up)
         (partial,) = yield (partial,)
         grad_hidden = grad_out + to_owners(partial)
+        grad_hidden, up_halves = yield (grad_hidden, up_halves)
+        sides["up"] = (hidden_both, stacked(up_halves))
         gain_attn_part = jnp.sum(grad_hidden * attn_unit, axis=0)
         grad_proj_low = norm_back(attn_unit, inv_attn, grad_hidden * gain_attn).astype(jnp.bfloat16)
         grad_proj_own = stacked(gather_rows(grad_proj_low, "seq"))
         (grad_proj_own,) = yield (grad_proj_own,)
-        sides["out"] = (stacked([attn_low, attn_other]), stacked(both_halves(grad_proj_own)))
+        proj_halves = both_halves(grad_proj_own)
         grad_attn_low = times_transpose(grad_proj_own, w_out).astype(jnp.bfloat16)
         backs = attend_back(query_low, key_low, value_low, grad_attn_low, lse, turns, block_rows)
+        backs = yield backs
         grad_query_norm, own_dk, own_dv, prev_dk, prev_dv = backs
         back_dk, back_dv = lax.ppermute((prev_dk, prev_dv), "ctx", [(1, 0)])
-        grad_query_norm, own_dk, own_dv, back_dk, back_dv = yield (
-            grad_query_norm, own_dk, own_dv, back_dk, back_dv
+        grad_query_norm, own_dk, own_dv, back_dk, back_dv, proj_halves = yield (
+            grad_query_norm, own_dk, own_dv, back_dk, back_dv, proj_halves
         )
+        sides["out"] = (stacked([attn_low, attn_other]), stacked(proj_halves))
         grad_value_low = (own_dv + back_dv.astype(jnp.float32)).astype(jnp.bfloat16)
         grad_key_norm = own_dk + back_dk.astype(jnp.float32)
         query_unit = query_proj * inv_query
@@ -610,14 +618,13 @@
             jnp.bfloat16
         )
         gains = jnp.concatenate([gain_sums, gain_query_part, gain_key_part]).reshape(-1, 128)
-        place = ctx_place
+        grad_value_low, grad_key_low, grad_query_low, gains = yield (
+            grad_value_low, grad_key_low, grad_query_low, gains
+        )
         lows = (grad_query_low, grad_key_low, grad_value_low)
-        mine = jnp.concatenate([half_columns(low, place) for low in lows], axis=1)
-        given = jnp.concatenate([half_columns(low, 1 - place) for low in lows], axis=1)
-        sides["in"] = (
-            stacked([tokens_own, tokens_other]),
-            stacked([mine, flip(given, "ctx", 1)]),
-        )
+        mine = jnp.concatenate([half_columns(low, ctx_place) for low in lows], axis=1)
+        given = jnp.concatenate([half_columns(low, 1 - ctx_place) for low in lows], axis=1)
+        theirs = flip(given, "ctx", 1)
         gains_other = flip(gains, "ctx", 1)
         partial = (
             times_transpose(grad_query_low, w_query)
@@ -628,7 +635,8 @@
         gains = gains + gains_other
         gains_pair = lax.ppermute(gains, "dp", PAIRS)
         grad_tokens = grad_hidden + to_owners(partial)
-        grad_tokens, gains, gains_pair = yield (grad_tokens, gains, gains_pair)
+        grad_tokens, gains, gains_pair, theirs = yield (grad_tokens, gains, gains_pair, theirs)
+        sides["in"] = (stacked([tokens_own, tokens_other]), stacked([mine, theirs]))
         results["tokens"] = grad_tokens
         gains = gains + gains_pair
         gains_across = lax.ppermute(gains, "dp", ACROSS)
@@ -648,10 +656,10 @@
     token = picked
     part[0] = grads[plan[0][0]].part(sides[plan[0][0]], 0)
 
-    for tick in range(count + 5):
+    for tick in range(count + 4 * STEP + 1):
         coming = sides.get(plan[tick + 1][0]) if tick + 1 < count else None
-        arrived = (got_in.get(tick - 1), got_out.get(tick - 3), got_across.get(tick - 2))
-        if tick - 1 in got_in and got_in[tick - 1] is arrived[1]:
+        arrived = (got_in.get(tick - STEP), got_out.get(tick - 3 * STEP), got_across.get(tick - 2 * STEP))
+        if tick - STEP in got_in and got_in[tick - STEP] is arrived[1]:
             arrived = (arrived[0], None, arrived[2])
         held = (arrived, part.get(tick), state, coming, last_buffers, token)
         arrived, entering, state, coming, last_buffers, token = lax.optimization_barrier(held)
@@ -659,49 +667,49 @@
             grads[last_name].buffers = last_buffers
         if entering is not None:
             part[tick] = entering
-        if tick - 1 in part:
-            got_in[tick - 1] = arrived[0]
-        if tick - 3 in sent:
-            got_out[tick - 3] = arrived[0] if arrived[1] is None else arrived[1]
-        if tick - 2 in pair:
-            got_across[tick - 2] = arrived[2]
-        alike = entering is not None and tick - 2 in pair and entering.shape == pair[tick - 2].shape
-        if alike and tick - 3 in sent and arrived[1] is None and arrived[0].shape == entering.shape:
-            pair[tick - 1], sent[tick - 2], final[tick - 3] = combine(
-                middle, part[tick - 1], arrived[0], pair[tick - 2], arrived[2], sent[tick - 3],
+        if tick - STEP in part:
+            got_in[tick - STEP] = arrived[0]
+        if tick - 3 * STEP in sent:
+            got_out[tick - 3 * STEP] = arrived[0] if arrived[1] is None else arrived[1]
+        if tick - 2 * STEP in pair:
+            got_across[tick - 2 * STEP] = arrived[2]
+        alike = entering is not None and tick - 2 * STEP in pair and entering.shape == pair[tick - 2 * STEP].shape
+        if alike and tick - 3 * STEP in sent and arrived[1] is None and arrived[0].shape == entering.shape:
+            pair[tick - STEP], sent[tick - 2 * STEP], final[tick - 3 * STEP] = combine(
+                middle, part[tick - STEP], arrived[0], pair[tick - 2 * STEP], arrived[2], sent[tick - 3 * STEP],
                 entering,
             )
         else:
-            if tick - 1 in part:
-                pair[tick - 1] = added(part[tick - 1], got_in[tick - 1])
-            if tick - 2 in pair:
-                leaving = added(pair[tick - 2], got_across[tick - 2])
-                sent[tick - 2] = jnp.where(middle, leaving, entering) if alike else leaving
-            if tick - 3 in sent:
-                final[tick - 3] = jnp.where(middle, sent[tick - 3], got_out[tick - 3])
-        held = (pair.get(tick - 1), sent.get(tick - 2), final.get(tick - 3), state, token)
+            if tick - STEP in part:
+                pair[tick - STEP] = added(part[tick - STEP], got_in[tick - STEP])
+            if tick - 2 * STEP in pair:
+                leaving = added(pair[tick - 2 * STEP], got_across[tick - 2 * STEP])
+                sent[tick - 2 * STEP] = jnp.where(middle, leaving, entering) if alike else leaving
+            if tick - 3 * STEP in sent:
+                final[tick - 3 * STEP] = jnp.where(middle, sent[tick - 3 * STEP], got_out[tick - 3 * STEP])
+        held = (pair.get(tick - STEP), sent.get(tick - 2 * STEP), final.get(tick - 3 * STEP), state, token)
         crossing, leaving, swapping, state, token = lax.optimization_barrier(held)
         if crossing is not None:
-            pair[tick - 1] = crossing
-            got_across[tick - 1] = lax.ppermute(crossing, "dp", ACROSS)
+            pair[tick - STEP] = crossing
+            got_across[tick - STEP] = lax.ppermute(crossing, "dp", ACROSS)
         if leaving is not None:
-            sent[tick - 2] = leaving
+            sent[tick - 2 * STEP] = leaving
         if alike:
-            got_in[tick] = got_out[tick - 2] = lax.ppermute(leaving, "dp", PAIRS)
+            got_in[tick] = got_out[tick - 2 * STEP] = lax.ppermute(leaving, "dp", PAIRS)
         else:
             if entering is not None:
                 got_in[tick] = lax.ppermute(entering, "dp", PAIRS if leaving is None else INWARD)
             if leaving is not None:
-                got_out[tick - 2] = lax.ppermute(
+                got_out[tick - 2 * STEP] = lax.ppermute(
                     leaving, "dp", PAIRS if entering is None else OUTWARD
                 )
         if swapping is not None:
-            final[tick - 3] = swapping
-            got_half[tick - 3] = flip(swapping, "ctx", 1)
-        if tick - 4 in final:
-            theirs, token = lax.optimization_barrier((got_half[tick - 4], token))
-            last_name, index = plan[tick - 4]
-            grads[last_name].store(index, final[tick - 4], theirs)
+            final[tick - 3 * STEP] = swapping
+            got_half[tick - 3 * STEP] = flip(swapping, "ctx", 1)
+        if tick - 4 * STEP in final:
+            theirs, token = lax.optimization_barrier((got_half[tick - 4 * STEP], token))
+            last_name, index = plan[tick - 4 * STEP]
+            grads[last_name].store(index, final[tick - 4 * STEP], theirs)
             last_buffers = grads[last_name].buffers
         try:
             state = main.send(state)

time: 828 us -> 825 us (level)
  waiting for transfers between devices: 348 us -> 280 us
  starting transfers between devices: 112 us -> 140 us
  matrix products: 103 us -> 114 us
  Pallas kernels: 114 us -> 124 us
  local copies, waits for them, and re-layouts: 25.3 us -> 34.7 us
    ppermute x5 -> x8, waiting for transfers between devices: 33.9 us -> 5.84 us  [body(): lax.ppermute(entering, 'dp', PAIRS if leaving is None else INWARD)]
    ppermute x5 -> x8, waiting for transfers between devices: 29.8 us -> 2.58 us  [body(): lax.ppermute(leaving, 'dp', PAIRS if entering is None else OUTWARD)]
    ppermute x17 -> x26, starting transfers between devices: 37.1 us -> 53.2 us  [the longest x17 28.7 us: body(): got_across[tick - STEP] = lax.ppermute(crossing, 'dp', ACROSS)]
    ppermute x56 -> x62, waiting for transfers between devices: 228 us -> 213 us  [flip(): lax.ppermute(value, axis, [(place, place ^ distance) for place in range(c...]
    dot_general x11 -> x17, matrix products: 42.2 us -> 56.6 us  [contract_rows(): lax.dot_general(left, right, (((0,), (0,)), ((), ())), preferred_element_...]
    ppermute x17 -> x26, waiting for transfers between devices: 12.2 us -> 24.1 us  [the longest x9 24 us: body(): got_in[tick] = got_out[tick - 2 * STEP] = lax.ppermute(leaving, 'dp', PAIRS)]
    ppermute x5 -> x8, starting transfers between devices: 6.19 us -> 15.2 us  [body(): lax.ppermute(leaving, 'dp', PAIRS if entering is None else OUTWARD)]
    convert_element_type x12 -> x18, other arithmetic: 35.8 us -> 42 us  [added(): (left.astype(jnp.float32) + right.astype(jnp.float32)).astype(left.dtype)]
  transfers between devices with their start and end apart: 88 -> 109, of which waited for: 45 -> 42; matrix products, arithmetic and copies ran while one was open for 21% -> 26% of each run, Pallas kernels for 11% -> 13%
where the time goes in v6:
time: 825 us; the launch traced here: 818 us
  waiting for transfers between devices  280 us (34%)
  starting transfers between devices  140 us (17%)
  Pallas kernels  124 us (15%)
  matrix products  114 us (14%)
  other arithmetic  104 us (13%)
  local copies, waits for them, and re-layouts  34.7 us (4%)
  blocking collectives  18.5 us (2%)
    ppermute x62, waiting for transfers between devices, flip(): lax.ppermute(value, axis, [(place, place ^ distance) for place in range(c...  213 us
    pallas_call x17, Pallas kernels, store_chunk(): pl.pallas_call(functools.partial(store_kernel, outs=outs), grid_spec=pltp...  61 us
    dot_general x17, matrix products, contract_rows(): lax.dot_general(left, right, (((0,), (0,)), ((), ())), preferred_element_...  56.6 us
    convert_element_type x18, other arithmetic, added(): (left.astype(jnp.float32) + right.astype(jnp.float32)).astype(left.dtype)  42 us
    ppermute x62, starting transfers between devices, flip(): lax.ppermute(value, axis, [(place, place ^ distance) for place in range(c...  40.1 us
    dot_general x7, matrix products, times_transpose(): lax.dot_general(left, right, (((1,), (1,)), ((), ())), preferred_element_...  34.3 us
    ppermute x17, starting transfers between devices, body(): got_across[tick - STEP] = lax.ppermute(crossing, 'dp', ACROSS)  28.7 us
    pallas_call x7, Pallas kernels, combine(): pl.pallas_call(combine_kernel, grid_spec=pltpu.PrefetchScalarGridSpec(num...  25.7 us
  transfers between devices with their start and end apart: 109, of which 42 were waited for; matrix products, arithmetic and copies ran while one was open for 26% of the time, Pallas kernels for 13%

profile of v6, /device:TPU:0, one launch (start us, length us, event | category | flops | bytes accessed | tf_op | source)
XLA Modules:
  0.0 817.9 jit_solution(7669403720503455395)
XLA Ops:
  5.3 10.5 %collective-permute-done.3.refs_0_ = bf16[128,2048]{1,0:T(8,128)(2,1)S(1)} collective-permute-done((bf16[128,2048]{1,0:T(8,128)(2,1)}, bf16[128,2048]{1,0:T(8,128)(2,1)S(1)}, u32[]{:S(2)}, u32[]{:S(2)}) %collective-permute-start.3) | collective-permute-done | bytes 524320 | tf_op jit(solution)/shard_map/ppermute | solution.py:26
  27.8 8.4 %project.2 = (bf16[512,2048]{1,0:T(8,128)(2,1)}, f32[512,512]{1,0:T(8,128)}, f32[512,512]{1,0:T(8,128)}, bf16[512,512]{1,0:T(8,128)(2,1)}, f32[512,1]{1,0:T(8,128)}, /*index=5*/f32[512,1]{1,0:T(8,128)}) custom-call(bf16[128,2048]{1,0:T(8,128)(2,1)} %refs_0_.1, bf16[128,2048]{1,0:T(8,128)(2,1)} %collective-permute-done.refs_1_, bf16[128,2048]{1,0:T(8,128)(2,1)} %copy-done.51, ...), custom_call_target="tpu_custom_call" | custom-call | tf_op jit(solution)/shard_map/project/pallas_call | solution.py:156
  46.1 7.5 psum.21
  56.2 11.8 %attend.1 = (bf16[512,512]{1,0:T(8,128)(2,1)}, bf16[1024,512]{1,0:T(8,128)(2,1)}, bf16[1024,512]{1,0:T(8,128)(2,1)}, bf16[512,512]{1,0:T(8,128)(2,1)}, f32[4,512,1]{2,1,0:T(8,128)}) custom-call(f32[512,512]{1,0:T(8,128)} %get-tuple-element.383.query_ref, f32[512,512]{1,0:T(8,128)} %get-tuple-element.384.key_ref, ...), custom_call_target="tpu_custom_call" | custom-call | tf_op jit(solution)/shard_map/attend/pallas_call | solution.py:264
  73.5 13.1 %collective-permute-done.10 = bf16[128,2048]{1,0:T(8,128)(2,1)S(1)} collective-permute-done((bf16[128,2048]{1,0:T(8,128)(2,1)S(1)}, bf16[128,2048]{1,0:T(8,128)(2,1)S(1)}, u32[]{:S(2)}, u32[]{:S(2)}) %collective-permute-start.10) | collective-permute-done | bytes 524320 | tf_op jit(solution)/shard_map/ppermute | solution.py:26
  89.3 11.9 %collective-permute-done.13 = bf16[128,2048]{1,0:T(8,128)(2,1)S(1)} collective-permute-done((bf16[128,2048]{1,0:T(8,128)(2,1)S(1)}, bf16[128,2048]{1,0:T(8,128)(2,1)S(1)}, u32[]{:S(2)}, u32[]{:S(2)}) %collective-permute-start.13) | collective-permute-done | bytes 524320 | tf_op jit(solution)/shard_map/ppermute | solution.py:26
  103.7 7.8 fusion.63
  140.0 9.4 %collective-permute-done.21 = bf16[128,2048]{1,0:T(8,128)(2,1)S(1)} collective-permute-done((bf16[128,2048]{1,0:T(8,128)(2,1)S(1)}, bf16[128,2048]{1,0:T(8,128)(2,1)S(1)}, u32[]{:S(2)}, u32[]{:S(2)}) %collective-permute-start.21) | collective-permute-done | bytes 524320 | tf_op jit(solution)/shard_map/ppermute | solution.py:26
  149.6 9.3 %collective-permute-done.22 = bf16[512,1024]{1,0:T(8,128)(2,1)S(1)} collective-permute-done((bf16[512,1024]{1,0:T(8,128)(2,1)S(1)}, bf16[512,1024]{1,0:T(8,128)(2,1)S(1)}, u32[]{:S(2)}, u32[]{:S(2)}) %collective-permute-start.22) | collective-permute-done | bytes 1048608 | tf_op jit(solution)/shard_map/ppermute | solution.py:26
  165.2 10.4 %collective-permute-done.24 = bf16[128,2048]{1,0:T(8,128)(2,1)S(1)} collective-permute-done((bf16[128,2048]{1,0:T(8,128)(2,1)S(1)}, bf16[128,2048]{1,0:T(8,128)(2,1)S(1)}, u32[]{:S(2)}, u32[]{:S(2)}) %collective-permute-start.24) | collective-permute-done | bytes 524320 | tf_op jit(solution)/shard_map/ppermute | solution.py:26
  193.1 10.5 %multiply_convert_fusion = (bf16[512,2048]{1,0:T(8,128)(2,1)S(1)}, bf16[512,2048]{1,0:T(8,128)(2,1)S(1)}) fusion(f32[512,2048]{1,0:T(8,128)} %copy-done.81, f32[512,2048]{1,0:T(8,128)} %get-tuple-element.801, bf16[512,2048]{1,0:T(8,128)(2,1)S(1)} %pad_maximum_fusion.1, bf16[2048,2048]{1,0:T(8,128)(2,1)} %param.29), kind=kOutput, calls=%fused_computation.5 | convolution fusion | flops 4308598784 | bytes 23068672 | tf_op jit(solution)/shard_map/dot_general | solution.py:108
  209.1 7.4 fusion.64
  216.6 12.2 %collective-permute-done.32 = bf16[512,1024]{1,0:T(8,128)(2,1)S(1)} collective-permute-done((bf16[512,1024]{1,0:T(8,128)(2,1)S(1)}, bf16[512,1024]{1,0:T(8,128)(2,1)S(1)}, u32[]{:S(2)}, u32[]{:S(2)}) %collective-permute-start.32) | collective-permute-done | bytes 1048608 | tf_op jit(solution)/shard_map/ppermute | solution.py:26
  265.8 10.5 %collective-permute-done.39 = bf16[512,1024]{1,0:T(8,128)(2,1)} collective-permute-done((bf16[512,1024]{1,0:T(8,128)(2,1)}, bf16[512,1024]{1,0:T(8,128)(2,1)}, u32[]{:S(2)}, u32[]{:S(2)}) %collective-permute-start.39) | collective-permute-done | bytes 1048608 | tf_op jit(solution)/shard_map/ppermute | solution.py:26
  331.7 10.9 %attend_back.1 = (f32[512,512]{1,0:T(8,128)}, f32[512,512]{1,0:T(8,128)}, f32[512,512]{1,0:T(8,128)}, bf16[512,512]{1,0:T(8,128)(2,1)}, bf16[512,512]{1,0:T(8,128)(2,1)}) custom-call(bf16[512,512]{1,0:T(8,128)(2,1)} %get-tuple-element.462.query_low_ref, bf16[1024,512]{1,0:T(8,128)(2,1)} %get-tuple-element.463.key_low_ref, ...), custom_call_target="tpu_custom_call" | custom-call | tf_op jit(solution)/shard_map/attend_back/pallas_call | solution.py:291
  383.7 11.0 %all-reduce = (f32[2,4,128]{2,0,1:T(2,128)S(1)}, f32[4096]{0:T(1024)S(1)}) all-reduce(f32[2,4,128]{2,0,1:T(2,128)S(1)} %select_bitcast_fusion.3, f32[4096]{0:T(1024)S(1)} %pad_maximum_fusion.8), channel_id=1, replica_groups=mesh['dp'=4,'ctx'=2,'seq'=4] {'seq'}, use_global_device_ids=true, to_apply=%region_8.11 | all-reduce | flops 5120 | bytes 40960 | tf_op jit(solution)/shard_map/psum | solution.py:601
  432.7 24.0 %collective-permute-done.56.got_ref = bf16[512,1024]{1,0:T(8,128)(2,1)} collective-permute-done((bf16[512,1024]{1,0:T(8,128)(2,1)}, bf16[512,1024]{1,0:T(8,128)(2,1)}, u32[]{:S(2)}, u32[]{:S(2)}) %collective-permute-start.56) | collective-permute-done | bytes 1048608 | tf_op jit(solution)/shard_map/ppermute | solution.py:698
  469.8 14.8 %collective-permute-done.64 = bf16[512,768]{1,0:T(8,128)(2,1)S(1)} collective-permute-done((bf16[512,768]{1,0:T(8,128)(2,1)S(1)}, bf16[512,768]{1,0:T(8,128)(2,1)S(1)}, u32[]{:S(2)}, u32[]{:S(2)}) %collective-permute-start.64) | collective-permute-done | bytes 786464 | tf_op jit(solution)/shard_map/ppermute | solution.py:26
  507.5 8.8 %collective-permute-done.63 = f32[40,128]{1,0:T(8,128)S(1)} collective-permute-done((f32[40,128]{1,0:T(8,128)S(1)}, f32[40,128]{1,0:T(8,128)S(1)}, u32[]{:S(2)}, u32[]{:S(2)}) %collective-permute-start.63) | collective-permute-done | bytes 20512 | tf_op jit(solution)/shard_map/ppermute | solution.py:636
  541.4 12.8 %collective-permute-done.72 = f32[40,128]{1,0:T(8,128)S(1)} collective-permute-done((f32[40,128]{1,0:T(8,128)S(1)}, f32[40,128]{1,0:T(8,128)S(1)}, u32[]{:S(2)}, u32[]{:S(2)}) %collective-permute-start.72) | collective-permute-done | bytes 20512 | tf_op jit(solution)/shard_map/ppermute | solution.py:645
  669.5 7.8 collective-permute-done.91.theirs_ref
  740.8 7.6 collective-permute-done.103.theirs_ref
  752.1 18.7 %collective-permute-done.106.theirs_ref = bf16[512,1024]{1,0:T(8,128)(2,1)} collective-permute-done((bf16[512,1024]{1,0:T(8,128)(2,1)S(1)}, bf16[512,1024]{1,0:T(8,128)(2,1)}, u32[]{:S(2)}, u32[]{:S(2)}) %collective-permute-start.106) | collective-permute-done | bytes 1048608 | tf_op jit(solution)/shard_map/ppermute | solution.py:26
  790.8 13.7 %collective-permute-done.107.theirs_ref = bf16[512,768]{1,0:T(8,128)(2,1)} collective-permute-done((bf16[512,768]{1,0:T(8,128)(2,1)S(1)}, bf16[512,768]{1,0:T(8,128)(2,1)}, u32[]{:S(2)}, u32[]{:S(2)}) %collective-permute-start.107) | collective-permute-done | bytes 786464 | tf_op jit(solution)/shard_map/ppermute | solution.py:26
  (566 shorter events, 544.1 us)
Async XLA Ops:
  204.4 38.9 %collective-permute-start.35 = (bf16[512,1024]{1,0:T(8,128)(2,1)S(1)}, bf16[512,1024]{1,0:T(8,128)(2,1)S(1)}, u32[]{:S(2)}, u32[]{:S(2)}) collective-permute-start(bf16[512,1024]{1,0:T(8,128)(2,1)S(1)} %fusion.9), channel_id=1, source_target_pairs={{0,8},{8,0},{16,24},{24,16},{1,9},{9,1},{17,25},{25,17},{2,10},{10... | collective-permute-start | bytes 3145736 | tf_op jit(solution)/shard_map/ppermute | solution.py:701
  298.2 48.6 %collective-permute-start.40 = (bf16[512,1024]{1,0:T(8,128)(2,1)}, bf16[512,1024]{1,0:T(8,128)(2,1)}, u32[]{:S(2)}, u32[]{:S(2)}) collective-permute-start(bf16[512,1024]{1,0:T(8,128)(2,1)} %fusion.21.sent_ref), channel_id=1, source_target_pairs={{0,8},{8,0},{16,24},{24,16},{1,9},{9,1},{17,25},{25,17},{2,10},{10... | collective-permute-start | bytes 3145736 | tf_op jit(solution)/shard_map/ppermute | solution.py:698
  307.1 39.7 %collective-permute-start.41 = (bf16[512,1024]{1,0:T(8,128)(2,1)S(1)}, bf16[512,1024]{1,0:T(8,128)(2,1)}, u32[]{:S(2)}, u32[]{:S(2)}) collective-permute-start(bf16[512,1024]{1,0:T(8,128)(2,1)S(1)} %copy-done.26), channel_id=1, source_target_pairs={{8,16},{16,8},{9,17},{17,9},{10,18},{18,10},{11,19},{19,11},{12,20... | collective-permute-start | bytes 3145736 | tf_op jit(solution)/shard_map/ppermute | solution.py:694
  320.8 54.9 %collective-permute-start.49 = (bf16[512,1024]{1,0:T(8,128)(2,1)}, bf16[512,1024]{1,0:T(8,128)(2,1)}, u32[]{:S(2)}, u32[]{:S(2)}) collective-permute-start(bf16[512,1024]{1,0:T(8,128)(2,1)} %fusion.22.sent_ref), channel_id=1, source_target_pairs={{0,8},{8,0},{16,24},{24,16},{1,9},{9,1},{17,25},{25,17},{2,10},{10... | collective-permute-start | bytes 3145736 | tf_op jit(solution)/shard_map/ppermute | solution.py:698
  324.7 51.0 %collective-permute-start.50 = (bf16[512,1024]{1,0:T(8,128)(2,1)}, bf16[512,1024]{1,0:T(8,128)(2,1)}, u32[]{:S(2)}, u32[]{:S(2)}) collective-permute-start(bf16[512,1024]{1,0:T(8,128)(2,1)} %add_convert_fusion.7.pair_ref), channel_id=1, source_target_pairs={{8,16},{16,8},{9,17},{17,9},{10,18},{18,10},{11,19},{19,11},{12,20... | collective-permute-start | bytes 3145736 | tf_op jit(solution)/shard_map/ppermute | solution.py:694
  328.1 47.6 %collective-permute-start.53 = (bf16[512,1024]{1,0:T(8,128)(2,1)}, bf16[512,1024]{1,0:T(8,128)(2,1)}, u32[]{:S(2)}, u32[]{:S(2)}) collective-permute-start(bf16[512,1024]{1,0:T(8,128)(2,1)} %get-tuple-element.765), channel_id=1, source_target_pairs={{0,4},{4,0},{1,5},{5,1},{2,6},{6,2},{3,7},{7,3},{8,12},{12,8},{9,1... | collective-permute-start | bytes 3145736 | tf_op jit(solution)/shard_map/ppermute | solution.py:26
  366.1 38.5 %collective-permute-start.47 = (bf16[512,1024]{1,0:T(8,128)(2,1)}, bf16[512,1024]{1,0:T(8,128)(2,1)}, u32[]{:S(2)}, u32[]{:S(2)}) collective-permute-start(bf16[512,1024]{1,0:T(8,128)(2,1)} %get-tuple-element.490.sent_ref), channel_id=1, source_target_pairs={{0,8},{8,0},{16,24},{24,16},{1,9},{9,1},{17,25},{25,17},{2,10},{10... | collective-permute-start | bytes 3145736 | tf_op jit(solution)/shard_map/ppermute | solution.py:698
  375.7 51.2 %collective-permute-start.59 = (bf16[512,1024]{1,0:T(8,128)(2,1)}, bf16[512,1024]{1,0:T(8,128)(2,1)}, u32[]{:S(2)}, u32[]{:S(2)}) collective-permute-start(bf16[512,1024]{1,0:T(8,128)(2,1)} %get-tuple-element.547.mine_ref), channel_id=1, source_target_pairs={{0,4},{4,0},{1,5},{5,1},{2,6},{6,2},{3,7},{7,3},{8,12},{12,8},{9,1... | collective-permute-start | bytes 3145736 | tf_op jit(solution)/shard_map/ppermute | solution.py:26
  408.2 81.1 %collective-permute-start.54 = (bf16[512,1024]{1,0:T(8,128)(2,1)}, bf16[512,1024]{1,0:T(8,128)(2,1)}, u32[]{:S(2)}, u32[]{:S(2)}) collective-permute-start(bf16[512,1024]{1,0:T(8,128)(2,1)} %get-tuple-element.537.sent_ref), channel_id=1, source_target_pairs={{0,8},{8,0},{16,24},{24,16},{1,9},{9,1},{17,25},{25,17},{2,10},{10... | collective-permute-start | bytes 3145736 | tf_op jit(solution)/shard_map/ppermute | solution.py:698
  411.4 45.3 %collective-permute-start.56 = (bf16[512,1024]{1,0:T(8,128)(2,1)}, bf16[512,1024]{1,0:T(8,128)(2,1)}, u32[]{:S(2)}, u32[]{:S(2)}) collective-permute-start(bf16[512,1024]{1,0:T(8,128)(2,1)} %get-tuple-element.539.sent_ref), channel_id=1, source_target_pairs={{0,8},{8,0},{16,24},{24,16},{1,9},{9,1},{17,25},{25,17},{2,10},{10... | collective-permute-start | bytes 3145736 | tf_op jit(solution)/shard_map/ppermute | solution.py:698
  411.5 45.3 %collective-permute-start.57 = (bf16[512,1024]{1,0:T(8,128)(2,1)}, bf16[512,1024]{1,0:T(8,128)(2,1)}, u32[]{:S(2)}, u32[]{:S(2)}) collective-permute-start(bf16[512,1024]{1,0:T(8,128)(2,1)} %get-tuple-element.540.pair_ref), channel_id=1, source_target_pairs={{8,16},{16,8},{9,17},{17,9},{10,18},{18,10},{11,19},{19,11},{12,20... | collective-permute-start | bytes 3145736 | tf_op jit(solution)/shard_map/ppermute | solution.py:694
  426.9 64.1 %collective-permute-start.55 = (bf16[512,1024]{1,0:T(8,128)(2,1)}, bf16[512,1024]{1,0:T(8,128)(2,1)}, u32[]{:S(2)}, u32[]{:S(2)}) collective-permute-start(bf16[512,1024]{1,0:T(8,128)(2,1)} %get-tuple-element.538.pair_ref), channel_id=1, source_target_pairs={{8,16},{16,8},{9,17},{17,9},{10,18},{18,10},{11,19},{19,11},{12,20... | collective-permute-start | bytes 3145736 | tf_op jit(solution)/shard_map/ppermute | solution.py:694
  432.3 61.0 %collective-permute-start.65 = (bf16[512,1024]{1,0:T(8,128)(2,1)}, bf16[512,1024]{1,0:T(8,128)(2,1)}, u32[]{:S(2)}, u32[]{:S(2)}) collective-permute-start(bf16[512,1024]{1,0:T(8,128)(2,1)} %get-tuple-element.566.mine_ref), channel_id=1, source_target_pairs={{0,4},{4,0},{1,5},{5,1},{2,6},{6,2},{3,7},{7,3},{8,12},{12,8},{9,1... | collective-permute-start | bytes 3145736 | tf_op jit(solution)/shard_map/ppermute | solution.py:26
  491.0 42.2 %collective-permute-start.68 = (bf16[512,1024]{1,0:T(8,128)(2,1)}, bf16[512,1024]{1,0:T(8,128)(2,1)}, u32[]{:S(2)}, u32[]{:S(2)}) collective-permute-start(bf16[512,1024]{1,0:T(8,128)(2,1)} %get-tuple-element.585.sent_ref), channel_id=1, source_target_pairs={{0,8},{8,0},{16,24},{24,16},{1,9},{9,1},{17,25},{25,17},{2,10},{10... | collective-permute-start | bytes 3145736 | tf_op jit(solution)/shard_map/ppermute | solution.py:698
  493.3 41.7 %collective-permute-start.69 = (bf16[512,1024]{1,0:T(8,128)(2,1)}, bf16[512,1024]{1,0:T(8,128)(2,1)}, u32[]{:S(2)}, u32[]{:S(2)}) collective-permute-start(bf16[512,1024]{1,0:T(8,128)(2,1)} %get-tuple-element.586.pair_ref), channel_id=1, source_target_pairs={{8,16},{16,8},{9,17},{17,9},{10,18},{18,10},{11,19},{19,11},{12,20... | collective-permute-start | bytes 3145736 | tf_op jit(solution)/shard_map/ppermute | solution.py:694
  524.1 43.0 %collective-permute-start.66 = (bf16[512,1024]{1,0:T(8,128)(2,1)}, bf16[512,1024]{1,0:T(8,128)(2,1)}, u32[]{:S(2)}, u32[]{:S(2)}) collective-permute-start(bf16[512,1024]{1,0:T(8,128)(2,1)} %get-tuple-element.583.sent_ref), channel_id=1, source_target_pairs={{0,8},{8,0},{16,24},{24,16},{1,9},{9,1},{17,25},{25,17},{2,10},{10... | collective-permute-start | bytes 3145736 | tf_op jit(solution)/shard_map/ppermute | solution.py:698
  535.0 38.9 %collective-permute-start.78 = (bf16[512,1024]{1,0:T(8,128)(2,1)}, bf16[512,1024]{1,0:T(8,128)(2,1)}, u32[]{:S(2)}, u32[]{:S(2)}) collective-permute-start(bf16[512,1024]{1,0:T(8,128)(2,1)} %get-tuple-element.635.mine_ref), channel_id=1, source_target_pairs={{0,4},{4,0},{1,5},{5,1},{2,6},{6,2},{3,7},{7,3},{8,12},{12,8},{9,1... | collective-permute-start | bytes 3145736 | tf_op jit(solution)/shard_map/ppermute | solution.py:26
  540.1 42.9 %collective-permute-start.76 = (bf16[512,1024]{1,0:T(8,128)(2,1)}, bf16[512,1024]{1,0:T(8,128)(2,1)S(1)}, u32[]{:S(2)}, u32[]{:S(2)}) collective-permute-start(bf16[512,1024]{1,0:T(8,128)(2,1)} %get-tuple-element.631), channel_id=1, source_target_pairs={{0,8},{8,0},{16,24},{24,16},{1,9},{9,1},{17,25},{25,17},{2,10},{10... | collective-permute-start | bytes 3145736 | tf_op jit(solution)/shard_map/ppermute | solution.py:698
  584.6 43.3 %collective-permute-start.83 = (bf16[512,768]{1,0:T(8,128)(2,1)}, bf16[512,768]{1,0:T(8,128)(2,1)}, u32[]{:S(2)}, u32[]{:S(2)}) collective-permute-start(bf16[512,768]{1,0:T(8,128)(2,1)} %convolution_convert_fusion.12), channel_id=1, source_target_pairs={{0,8},{24,16},{1,9},{25,17},{2,10},{26,18},{3,11},{27,19},{4,12},{... | collective-permute-start | bytes 2359304 | tf_op jit(solution)/shard_map/ppermute | solution.py:701
  689.8 41.7 %collective-permute-start.98 = (bf16[512,1024]{1,0:T(8,128)(2,1)}, bf16[512,1024]{1,0:T(8,128)(2,1)}, u32[]{:S(2)}, u32[]{:S(2)}) collective-permute-start(bf16[512,1024]{1,0:T(8,128)(2,1)} %broadcast_select_fusion.1.mine_ref), channel_id=1, source_target_pairs={{0,4},{4,0},{1,5},{5,1},{2,6},{6,2},{3,7},{7,3},{8,12},{12,8},{9,1... | collective-permute-start | bytes 3145736 | tf_op jit(solution)/shard_map/ppermute | solution.py:26
  720.7 53.8 %collective-permute-start.105 = (bf16[512,768]{1,0:T(8,128)(2,1)}, bf16[512,768]{1,0:T(8,128)(2,1)}, u32[]{:S(2)}, u32[]{:S(2)}) collective-permute-start(bf16[512,768]{1,0:T(8,128)(2,1)} %add_convert_fusion.13), channel_id=1, source_target_pairs={{0,8},{8,0},{16,24},{24,16},{1,9},{9,1},{17,25},{25,17},{2,10},{10... | collective-permute-start | bytes 2359304 | tf_op jit(solution)/shard_map/ppermute | solution.py:703
  731.5 39.3 %collective-permute-start.106 = (bf16[512,1024]{1,0:T(8,128)(2,1)S(1)}, bf16[512,1024]{1,0:T(8,128)(2,1)}, u32[]{:S(2)}, u32[]{:S(2)}) collective-permute-start(bf16[512,1024]{1,0:T(8,128)(2,1)S(1)} %broadcast_select_fusion.mine_ref), channel_id=1, source_target_pairs={{0,4},{4,0},{1,5},{5,1},{2,6},{6,2},{3,7},{7,3},{8,12},{12,8},{9,1... | collective-permute-start | bytes 3145736 | tf_op jit(solution)/shard_map/ppermute | solution.py:26
  739.5 36.9 %collective-permute-start.102 = (bf16[512,768]{1,0:T(8,128)(2,1)}, bf16[512,768]{1,0:T(8,128)(2,1)}, u32[]{:S(2)}, u32[]{:S(2)}) collective-permute-start(bf16[512,768]{1,0:T(8,128)(2,1)} %add_convert_fusion.12), channel_id=1, source_target_pairs={{0,8},{8,0},{16,24},{24,16},{1,9},{9,1},{17,25},{25,17},{2,10},{10... | collective-permute-start | bytes 2359304 | tf_op jit(solution)/shard_map/ppermute | solution.py:703
  777.7 36.8 %collective-permute-start.104 = (bf16[512,768]{1,0:T(8,128)(2,1)S(1)}, bf16[512,768]{1,0:T(8,128)(2,1)}, u32[]{:S(2)}, u32[]{:S(2)}) collective-permute-start(bf16[512,768]{1,0:T(8,128)(2,1)S(1)} %broadcast_select_fusion.7.mine_ref), channel_id=1, source_target_pairs={{0,4},{4,0},{1,5},{5,1},{2,6},{6,2},{3,7},{7,3},{8,12},{12,8},{9,1... | collective-permute-start | bytes 2359304 | tf_op jit(solution)/shard_map/ppermute | solution.py:26
  (171 other events, 2463.1 us)

commit v7 on v6

--- a/solution.py
+++ b/solution.py
@@ -661,8 +661,8 @@
         arrived = (got_in.get(tick - STEP), got_out.get(tick - 3 * STEP), got_across.get(tick - 2 * STEP))
         if tick - STEP in got_in and got_in[tick - STEP] is arrived[1]:
             arrived = (arrived[0], None, arrived[2])
-        held = (arrived, part.get(tick), state, coming, last_buffers, token)
-        arrived, entering, state, coming, last_buffers, token = lax.optimization_barrier(held)
+        held = (arrived, part.get(tick), coming, last_buffers, token)
+        arrived, entering, coming, last_buffers, token = lax.optimization_barrier(held)
         if last_name:
             grads[last_name].buffers = last_buffers
         if entering is not None:

time: 825 us -> 809 us (0.981)
  other arithmetic: 104 us -> 87.9 us
    ppermute x8, waiting for transfers between devices: 5.84 us -> 45.7 us  [body(): lax.ppermute(entering, 'dp', PAIRS if leaving is None else INWARD)]
    ppermute x62, waiting for transfers between devices: 213 us -> 193 us  [flip(): lax.ppermute(value, axis, [(place, place ^ distance) for place in range(c...]
    ppermute x9, starting transfers between devices: 24.6 us -> 36.9 us  [body(): got_in[tick] = got_out[tick - 2 * STEP] = lax.ppermute(leaving, 'dp', PAIRS)]
    ppermute x9, waiting for transfers between devices: 24 us -> 13.3 us  [body(): got_in[tick] = got_out[tick - 2 * STEP] = lax.ppermute(leaving, 'dp', PAIRS)]
    ppermute x1, waiting for transfers between devices: 12.8 us -> 2.89 us  [stages(): gains_out = lax.ppermute(gains, 'dp', PAIRS)]
    convert_element_type x18, other arithmetic: 42 us -> 32.5 us  [added(): (left.astype(jnp.float32) + right.astype(jnp.float32)).astype(left.dtype)]
    dot_general x17, matrix products: 56.6 us -> 48.1 us  [contract_rows(): lax.dot_general(left, right, (((0,), (0,)), ((), ())), preferred_element_...]
  transfers between devices with their start and end apart: 109 -> 109, of which waited for: 42 -> 43; matrix products, arithmetic and copies ran while one was open for 26% -> 23% of each run, Pallas kernels for 13% -> 13%
where the time goes in v7:
time: 809 us; the launch traced here: 802 us
  waiting for transfers between devices  287 us (35%)
  starting transfers between devices  139 us (17%)
  Pallas kernels  123 us (15%)
  matrix products  109 us (13%)
  other arithmetic  87.9 us (11%)
  local copies, waits for them, and re-layouts  33.4 us (4%)
  blocking collectives  18.5 us (2%)
    ppermute x62, waiting for transfers between devices, flip(): lax.ppermute(value, axis, [(place, place ^ distance) for place in range(c...  193 us
    pallas_call x17, Pallas kernels, store_chunk(): pl.pallas_call(functools.partial(store_kernel, outs=outs), grid_spec=pltp...  60.7 us
    dot_general x17, matrix products, contract_rows(): lax.dot_general(left, right, (((0,), (0,)), ((), ())), preferred_element_...  48.1 us
    ppermute x8, waiting for transfers between devices, body(): lax.ppermute(entering, 'dp', PAIRS if leaving is None else INWARD)  45.7 us
    dot_general x7, matrix products, times_transpose(): lax.dot_general(left, right, (((1,), (1,)), ((), ())), preferred_element_...  38.3 us
    ppermute x62, starting transfers between devices, flip(): lax.ppermute(value, axis, [(place, place ^ distance) for place in range(c...  37.1 us
    ppermute x9, starting transfers between devices, body(): got_in[tick] = got_out[tick - 2 * STEP] = lax.ppermute(leaving, 'dp', PAIRS)  36.9 us
    convert_element_type x18, other arithmetic, added(): (left.astype(jnp.float32) + right.astype(jnp.float32)).astype(left.dtype)  32.5 us
  transfers between devices with their start and end apart: 109, of which 43 were waited for; matrix products, arithmetic and copies ran while one was open for 23% of the time, Pallas kernels for 13%

profile of v7, /device:TPU:0, one launch (start us, length us, event | category | flops | bytes accessed | tf_op | source)
XLA Modules:
  0.0 802.0 jit_solution(319601926734815946)
XLA Ops:
  5.3 10.5 %collective-permute-done.3.refs_0_ = bf16[128,2048]{1,0:T(8,128)(2,1)S(1)} collective-permute-done((bf16[128,2048]{1,0:T(8,128)(2,1)}, bf16[128,2048]{1,0:T(8,128)(2,1)S(1)}, u32[]{:S(2)}, u32[]{:S(2)}) %collective-permute-start.3) | collective-permute-done | bytes 524320 | tf_op jit(solution)/shard_map/ppermute | solution.py:26
  27.8 8.4 %project.2 = (bf16[512,2048]{1,0:T(8,128)(2,1)}, f32[512,512]{1,0:T(8,128)}, f32[512,512]{1,0:T(8,128)}, bf16[512,512]{1,0:T(8,128)(2,1)}, f32[512,1]{1,0:T(8,128)}, /*index=5*/f32[512,1]{1,0:T(8,128)}) custom-call(bf16[128,2048]{1,0:T(8,128)(2,1)} %refs_0_.1, bf16[128,2048]{1,0:T(8,128)(2,1)} %collective-permute-done.refs_1_, bf16[128,2048]{1,0:T(8,128)(2,1)} %copy-done.57, ...), custom_call_target="tpu_custom_call" | custom-call | tf_op jit(solution)/shard_map/project/pallas_call | solution.py:156
  56.2 11.8 %attend.1 = (bf16[512,512]{1,0:T(8,128)(2,1)}, bf16[1024,512]{1,0:T(8,128)(2,1)}, bf16[1024,512]{1,0:T(8,128)(2,1)}, bf16[512,512]{1,0:T(8,128)(2,1)}, f32[4,512,1]{2,1,0:T(8,128)}) custom-call(f32[512,512]{1,0:T(8,128)} %get-tuple-element.345.query_ref, f32[512,512]{1,0:T(8,128)} %get-tuple-element.346.key_ref, ...), custom_call_target="tpu_custom_call" | custom-call | tf_op jit(solution)/shard_map/attend/pallas_call | solution.py:264
  73.5 13.1 %collective-permute-done.10 = bf16[128,2048]{1,0:T(8,128)(2,1)S(1)} collective-permute-done((bf16[128,2048]{1,0:T(8,128)(2,1)S(1)}, bf16[128,2048]{1,0:T(8,128)(2,1)S(1)}, u32[]{:S(2)}, u32[]{:S(2)}) %collective-permute-start.10) | collective-permute-done | bytes 524320 | tf_op jit(solution)/shard_map/ppermute | solution.py:26
  89.3 11.1 %collective-permute-done.13 = bf16[128,2048]{1,0:T(8,128)(2,1)S(1)} collective-permute-done((bf16[128,2048]{1,0:T(8,128)(2,1)S(1)}, bf16[128,2048]{1,0:T(8,128)(2,1)S(1)}, u32[]{:S(2)}, u32[]{:S(2)}) %collective-permute-start.13) | collective-permute-done | bytes 524320 | tf_op jit(solution)/shard_map/ppermute | solution.py:26
  136.5 12.8 %collective-permute-done.21 = bf16[128,2048]{1,0:T(8,128)(2,1)S(1)} collective-permute-done((bf16[128,2048]{1,0:T(8,128)(2,1)S(1)}, bf16[128,2048]{1,0:T(8,128)(2,1)S(1)}, u32[]{:S(2)}, u32[]{:S(2)}) %collective-permute-start.21) | collective-permute-done | bytes 524320 | tf_op jit(solution)/shard_map/ppermute | solution.py:26
  149.5 9.3 %collective-permute-done.22 = bf16[512,1024]{1,0:T(8,128)(2,1)S(1)} collective-permute-done((bf16[512,1024]{1,0:T(8,128)(2,1)S(1)}, bf16[512,1024]{1,0:T(8,128)(2,1)S(1)}, u32[]{:S(2)}, u32[]{:S(2)}) %collective-permute-start.22) | collective-permute-done | bytes 1048608 | tf_op jit(solution)/shard_map/ppermute | solution.py:26
  162.9 12.7 %collective-permute-done.24 = bf16[128,2048]{1,0:T(8,128)(2,1)S(1)} collective-permute-done((bf16[128,2048]{1,0:T(8,128)(2,1)S(1)}, bf16[128,2048]{1,0:T(8,128)(2,1)S(1)}, u32[]{:S(2)}, u32[]{:S(2)}) %collective-permute-start.24) | collective-permute-done | bytes 524320 | tf_op jit(solution)/shard_map/ppermute | solution.py:26
  191.6 11.4 %multiply_convert_fusion = (bf16[512,2048]{1,0:T(8,128)(2,1)S(1)}, bf16[512,2048]{1,0:T(8,128)(2,1)}) fusion(f32[512,2048]{1,0:T(8,128)} %copy-done.97, f32[512,2048]{1,0:T(8,128)} %get-tuple-element.725, bf16[512,2048]{1,0:T(8,128)(2,1)S(1)} %copy-done.54, bf16[2048,2048]{1,0:T(8,128)(2,1)} %param.29), kind=kOutput, calls=%fused_computation.5 | convolution fusion | flops 4308598784 | bytes 23068672 | tf_op jit(solution)/shard_map/dot_general | solution.py:108
  203.0 8.4 %fusion.64 = f32[512,2048]{1,0:T(8,128)S(1)} fusion(bf16[512,2048]{1,0:T(8,128)(2,1)} %get-tuple-element.379, bf16[2048,2048]{1,0:T(8,128)(2,1)} %param.27), kind=kOutput, calls=%fused_computation.216 | convolution fusion | flops 4294967296 | bytes 14680064 | tf_op jit(solution)/shard_map/dot_general | solution.py:108
  225.7 13.0 %collective-permute-done.31 = bf16[512,1024]{1,0:T(8,128)(2,1)S(1)} collective-permute-done((bf16[512,1024]{1,0:T(8,128)(2,1)S(1)}, bf16[512,1024]{1,0:T(8,128)(2,1)S(1)}, u32[]{:S(2)}, u32[]{:S(2)}) %collective-permute-start.31) | collective-permute-done | bytes 1048608 | tf_op jit(solution)/shard_map/ppermute | solution.py:701
  244.7 16.4 %collective-permute-done.35 = bf16[512,1024]{1,0:T(8,128)(2,1)S(1)} collective-permute-done((bf16[512,1024]{1,0:T(8,128)(2,1)S(1)}, bf16[512,1024]{1,0:T(8,128)(2,1)S(1)}, u32[]{:S(2)}, u32[]{:S(2)}) %collective-permute-start.35) | collective-permute-done | bytes 1048608 | tf_op jit(solution)/shard_map/ppermute | solution.py:701
  269.0 14.6 %collective-permute-done.32 = bf16[512,1024]{1,0:T(8,128)(2,1)S(1)} collective-permute-done((bf16[512,1024]{1,0:T(8,128)(2,1)S(1)}, bf16[512,1024]{1,0:T(8,128)(2,1)S(1)}, u32[]{:S(2)}, u32[]{:S(2)}) %collective-permute-start.32) | collective-permute-done | bytes 1048608 | tf_op jit(solution)/shard_map/ppermute | solution.py:701
  286.8 10.2 %collective-permute-done.38 = bf16[128,2048]{1,0:T(8,128)(2,1)S(1)} collective-permute-done((bf16[128,2048]{1,0:T(8,128)(2,1)S(1)}, bf16[128,2048]{1,0:T(8,128)(2,1)S(1)}, u32[]{:S(2)}, u32[]{:S(2)}) %collective-permute-start.38) | collective-permute-done | bytes 524320 | tf_op jit(solution)/shard_map/ppermute | solution.py:26
  321.4 9.0 %collective-permute-done.40.got_ref = bf16[512,1024]{1,0:T(8,128)(2,1)S(1)} collective-permute-done((bf16[512,1024]{1,0:T(8,128)(2,1)S(1)}, bf16[512,1024]{1,0:T(8,128)(2,1)S(1)}, u32[]{:S(2)}, u32[]{:S(2)}) %collective-permute-start.40) | collective-permute-done | bytes 1048608 | tf_op jit(solution)/shard_map/ppermute | solution.py:698
  340.3 11.0 %attend_back.1 = (f32[512,512]{1,0:T(8,128)}, f32[512,512]{1,0:T(8,128)}, f32[512,512]{1,0:T(8,128)}, bf16[512,512]{1,0:T(8,128)(2,1)}, bf16[512,512]{1,0:T(8,128)(2,1)}) custom-call(bf16[512,512]{1,0:T(8,128)(2,1)} %get-tuple-element.425.query_low_ref, bf16[1024,512]{1,0:T(8,128)(2,1)} %get-tuple-element.426.key_low_ref, ...), custom_call_target="tpu_custom_call" | custom-call | tf_op jit(solution)/shard_map/attend_back/pallas_call | solution.py:291
  376.0 11.1 %collective-permute-done.52 = bf16[512,512]{1,0:T(8,128)(2,1)S(1)} collective-permute-done((bf16[512,512]{1,0:T(8,128)(2,1)}, bf16[512,512]{1,0:T(8,128)(2,1)S(1)}, u32[]{:S(2)}, u32[]{:S(2)}) %collective-permute-start.52) | collective-permute-done | bytes 524320 | tf_op jit(solution)/shard_map/ppermute | solution.py:588
  395.2 11.0 %all-reduce = (f32[2,4,128]{2,0,1:T(2,128)S(1)}, f32[4096]{0:T(1024)S(1)}) all-reduce(f32[2,4,128]{2,0,1:T(2,128)S(1)} %select_bitcast_fusion.3, f32[4096]{0:T(1024)S(1)} %pad_maximum_fusion.8), channel_id=1, replica_groups=mesh['dp'=4,'ctx'=2,'seq'=4] {'seq'}, use_global_device_ids=true, to_apply=%region_8.11 | all-reduce | flops 5120 | bytes 40960 | tf_op jit(solution)/shard_map/psum | solution.py:601
  467.4 9.7 %collective-permute-done.65 = bf16[512,768]{1,0:T(8,128)(2,1)} collective-permute-done((bf16[512,768]{1,0:T(8,128)(2,1)S(1)}, bf16[512,768]{1,0:T(8,128)(2,1)}, u32[]{:S(2)}, u32[]{:S(2)}) %collective-permute-start.65) | collective-permute-done | bytes 786464 | tf_op jit(solution)/shard_map/ppermute | solution.py:26
  494.3 8.4 %collective-permute-done.64 = f32[40,128]{1,0:T(8,128)S(1)} collective-permute-done((f32[40,128]{1,0:T(8,128)S(1)}, f32[40,128]{1,0:T(8,128)S(1)}, u32[]{:S(2)}, u32[]{:S(2)}) %collective-permute-start.64) | collective-permute-done | bytes 20512 | tf_op jit(solution)/shard_map/ppermute | solution.py:636
  520.9 12.9 %collective-permute-start.76 = (bf16[512,1024]{1,0:T(8,128)(2,1)}, bf16[512,1024]{1,0:T(8,128)(2,1)S(1)}, u32[]{:S(2)}, u32[]{:S(2)}) collective-permute-start(bf16[512,1024]{1,0:T(8,128)(2,1)} %get-tuple-element.555), channel_id=1, source_target_pairs={{0,8},{8,0},{16,24},{24,16},{1,9},{9,1},{17,25},{25,17},{2,10},{10... | collective-permute-start | bytes 3145736 | tf_op jit(solution)/shard_map/ppermute | solution.py:698
  651.2 10.1 %collective-permute-done.91.theirs_ref = bf16[512,1024]{1,0:T(8,128)(2,1)} collective-permute-done((bf16[512,1024]{1,0:T(8,128)(2,1)S(1)}, bf16[512,1024]{1,0:T(8,128)(2,1)}, u32[]{:S(2)}, u32[]{:S(2)}) %collective-permute-start.91) | collective-permute-done | bytes 1048608 | tf_op jit(solution)/shard_map/ppermute | solution.py:26
  734.7 19.0 %collective-permute-done.106.theirs_ref = bf16[512,1024]{1,0:T(8,128)(2,1)} collective-permute-done((bf16[512,1024]{1,0:T(8,128)(2,1)S(1)}, bf16[512,1024]{1,0:T(8,128)(2,1)}, u32[]{:S(2)}, u32[]{:S(2)}) %collective-permute-start.106) | collective-permute-done | bytes 1048608 | tf_op jit(solution)/shard_map/ppermute | solution.py:26
  773.7 13.7 %collective-permute-done.107.theirs_ref = bf16[512,768]{1,0:T(8,128)(2,1)} collective-permute-done((bf16[512,768]{1,0:T(8,128)(2,1)S(1)}, bf16[512,768]{1,0:T(8,128)(2,1)}, u32[]{:S(2)}, u32[]{:S(2)}) %collective-permute-start.107) | collective-permute-done | bytes 786464 | tf_op jit(solution)/shard_map/ppermute | solution.py:26
  (599 shorter events, 518.9 us)
Async XLA Ops:
  214.8 46.4 %collective-permute-start.35 = (bf16[512,1024]{1,0:T(8,128)(2,1)S(1)}, bf16[512,1024]{1,0:T(8,128)(2,1)S(1)}, u32[]{:S(2)}, u32[]{:S(2)}) collective-permute-start(bf16[512,1024]{1,0:T(8,128)(2,1)S(1)} %copy-done.62), channel_id=1, source_target_pairs={{0,8},{8,0},{16,24},{24,16},{1,9},{9,1},{17,25},{25,17},{2,10},{10... | collective-permute-start | bytes 3145736 | tf_op jit(solution)/shard_map/ppermute | solution.py:701
  238.7 44.9 %collective-permute-start.32 = (bf16[512,1024]{1,0:T(8,128)(2,1)S(1)}, bf16[512,1024]{1,0:T(8,128)(2,1)S(1)}, u32[]{:S(2)}, u32[]{:S(2)}) collective-permute-start(bf16[512,1024]{1,0:T(8,128)(2,1)S(1)} %fusion.12), channel_id=1, source_target_pairs={{0,8},{8,0},{16,24},{24,16},{1,9},{9,1},{17,25},{25,17},{2,10},{10... | collective-permute-start | bytes 3145736 | tf_op jit(solution)/shard_map/ppermute | solution.py:701
  240.7 43.7 %collective-permute-start.34 = (bf16[512,1024]{1,0:T(8,128)(2,1)S(1)}, bf16[512,1024]{1,0:T(8,128)(2,1)S(1)}, u32[]{:S(2)}, u32[]{:S(2)}) collective-permute-start(bf16[512,1024]{1,0:T(8,128)(2,1)S(1)} %add_convert_fusion.11), channel_id=1, source_target_pairs={{8,16},{16,8},{9,17},{17,9},{10,18},{18,10},{11,19},{19,11},{12,20... | collective-permute-start | bytes 3145736 | tf_op jit(solution)/shard_map/ppermute | solution.py:694
  267.2 39.2 %collective-permute-start.42 = (bf16[512,1024]{1,0:T(8,128)(2,1)S(1)}, bf16[512,1024]{1,0:T(8,128)(2,1)S(1)}, u32[]{:S(2)}, u32[]{:S(2)}) collective-permute-start(bf16[512,1024]{1,0:T(8,128)(2,1)S(1)} %fusion.15), channel_id=1, source_target_pairs={{0,8},{8,0},{16,24},{24,16},{1,9},{9,1},{17,25},{25,17},{2,10},{10... | collective-permute-start | bytes 3145736 | tf_op jit(solution)/shard_map/ppermute | solution.py:701
  313.7 45.3 %collective-permute-start.49 = (bf16[512,1024]{1,0:T(8,128)(2,1)}, bf16[512,1024]{1,0:T(8,128)(2,1)}, u32[]{:S(2)}, u32[]{:S(2)}) collective-permute-start(bf16[512,1024]{1,0:T(8,128)(2,1)} %fusion.22.sent_ref), channel_id=1, source_target_pairs={{0,8},{8,0},{16,24},{24,16},{1,9},{9,1},{17,25},{25,17},{2,10},{10... | collective-permute-start | bytes 3145736 | tf_op jit(solution)/shard_map/ppermute | solution.py:698
  317.5 42.7 %collective-permute-start.50 = (bf16[512,1024]{1,0:T(8,128)(2,1)S(1)}, bf16[512,1024]{1,0:T(8,128)(2,1)}, u32[]{:S(2)}, u32[]{:S(2)}) collective-permute-start(bf16[512,1024]{1,0:T(8,128)(2,1)S(1)} %add_convert_fusion.7.pair_ref), channel_id=1, source_target_pairs={{8,16},{16,8},{9,17},{17,9},{10,18},{18,10},{11,19},{19,11},{12,20... | collective-permute-start | bytes 3145736 | tf_op jit(solution)/shard_map/ppermute | solution.py:694
  332.5 54.6 %collective-permute-start.53 = (bf16[512,1024]{1,0:T(8,128)(2,1)}, bf16[512,1024]{1,0:T(8,128)(2,1)}, u32[]{:S(2)}, u32[]{:S(2)}) collective-permute-start(bf16[512,1024]{1,0:T(8,128)(2,1)} %get-tuple-element.689), channel_id=1, source_target_pairs={{0,4},{4,0},{1,5},{5,1},{2,6},{6,2},{3,7},{7,3},{8,12},{12,8},{9,1... | collective-permute-start | bytes 3145736 | tf_op jit(solution)/shard_map/ppermute | solution.py:26
  351.3 40.2 %collective-permute-start.47 = (bf16[512,1024]{1,0:T(8,128)(2,1)}, bf16[512,1024]{1,0:T(8,128)(2,1)}, u32[]{:S(2)}, u32[]{:S(2)}) collective-permute-start(bf16[512,1024]{1,0:T(8,128)(2,1)} %get-tuple-element.436.sent_ref), channel_id=1, source_target_pairs={{0,8},{8,0},{16,24},{24,16},{1,9},{9,1},{17,25},{25,17},{2,10},{10... | collective-permute-start | bytes 3145736 | tf_op jit(solution)/shard_map/ppermute | solution.py:698
  376.0 57.7 %collective-permute-start.58 = (bf16[512,1024]{1,0:T(8,128)(2,1)}, bf16[512,1024]{1,0:T(8,128)(2,1)}, u32[]{:S(2)}, u32[]{:S(2)}) collective-permute-start(bf16[512,1024]{1,0:T(8,128)(2,1)} %get-tuple-element.478.mine_ref), channel_id=1, source_target_pairs={{0,4},{4,0},{1,5},{5,1},{2,6},{6,2},{3,7},{7,3},{8,12},{12,8},{9,1... | collective-permute-start | bytes 3145736 | tf_op jit(solution)/shard_map/ppermute | solution.py:26
  420.5 39.6 %collective-permute-start.59 = (bf16[512,1024]{1,0:T(8,128)(2,1)}, bf16[512,1024]{1,0:T(8,128)(2,1)}, u32[]{:S(2)}, u32[]{:S(2)}) collective-permute-start(bf16[512,1024]{1,0:T(8,128)(2,1)} %get-tuple-element.484.mine_ref), channel_id=1, source_target_pairs={{0,4},{4,0},{1,5},{5,1},{2,6},{6,2},{3,7},{7,3},{8,12},{12,8},{9,1... | collective-permute-start | bytes 3145736 | tf_op jit(solution)/shard_map/ppermute | solution.py:26
  491.2 42.6 %collective-permute-start.71 = (bf16[512,1024]{1,0:T(8,128)(2,1)}, bf16[512,1024]{1,0:T(8,128)(2,1)}, u32[]{:S(2)}, u32[]{:S(2)}) collective-permute-start(bf16[512,1024]{1,0:T(8,128)(2,1)} %get-tuple-element.530.mine_ref), channel_id=1, source_target_pairs={{0,4},{4,0},{1,5},{5,1},{2,6},{6,2},{3,7},{7,3},{8,12},{12,8},{9,1... | collective-permute-start | bytes 3145736 | tf_op jit(solution)/shard_map/ppermute | solution.py:26
  502.8 38.7 %collective-permute-start.66 = (bf16[512,1024]{1,0:T(8,128)(2,1)}, bf16[512,1024]{1,0:T(8,128)(2,1)}, u32[]{:S(2)}, u32[]{:S(2)}) collective-permute-start(bf16[512,1024]{1,0:T(8,128)(2,1)} %get-tuple-element.511.sent_ref), channel_id=1, source_target_pairs={{0,8},{8,0},{16,24},{24,16},{1,9},{9,1},{17,25},{25,17},{2,10},{10... | collective-permute-start | bytes 3145736 | tf_op jit(solution)/shard_map/ppermute | solution.py:698
  507.0 41.7 %collective-permute-start.67 = (bf16[512,1024]{1,0:T(8,128)(2,1)}, bf16[512,1024]{1,0:T(8,128)(2,1)}, u32[]{:S(2)}, u32[]{:S(2)}) collective-permute-start(bf16[512,1024]{1,0:T(8,128)(2,1)} %get-tuple-element.512.pair_ref), channel_id=1, source_target_pairs={{8,16},{16,8},{9,17},{17,9},{10,18},{18,10},{11,19},{19,11},{12,20... | collective-permute-start | bytes 3145736 | tf_op jit(solution)/shard_map/ppermute | solution.py:694
  509.3 48.2 %collective-permute-start.78 = (bf16[512,1024]{1,0:T(8,128)(2,1)}, bf16[512,1024]{1,0:T(8,128)(2,1)}, u32[]{:S(2)}, u32[]{:S(2)}) collective-permute-start(bf16[512,1024]{1,0:T(8,128)(2,1)} %get-tuple-element.559.mine_ref), channel_id=1, source_target_pairs={{0,4},{4,0},{1,5},{5,1},{2,6},{6,2},{3,7},{7,3},{8,12},{12,8},{9,1... | collective-permute-start | bytes 3145736 | tf_op jit(solution)/shard_map/ppermute | solution.py:26
  520.9 45.7 %collective-permute-start.76 = (bf16[512,1024]{1,0:T(8,128)(2,1)}, bf16[512,1024]{1,0:T(8,128)(2,1)S(1)}, u32[]{:S(2)}, u32[]{:S(2)}) collective-permute-start(bf16[512,1024]{1,0:T(8,128)(2,1)} %get-tuple-element.555), channel_id=1, source_target_pairs={{0,8},{8,0},{16,24},{24,16},{1,9},{9,1},{17,25},{25,17},{2,10},{10... | collective-permute-start | bytes 3145736 | tf_op jit(solution)/shard_map/ppermute | solution.py:698
  567.6 42.7 %collective-permute-start.83 = (bf16[512,768]{1,0:T(8,128)(2,1)}, bf16[512,768]{1,0:T(8,128)(2,1)}, u32[]{:S(2)}, u32[]{:S(2)}) collective-permute-start(bf16[512,768]{1,0:T(8,128)(2,1)} %convolution_convert_fusion.12), channel_id=1, source_target_pairs={{0,8},{24,16},{1,9},{25,17},{2,10},{26,18},{3,11},{27,19},{4,12},{... | collective-permute-start | bytes 2359304 | tf_op jit(solution)/shard_map/ppermute | solution.py:701
  623.8 37.5 %collective-permute-start.91 = (bf16[512,1024]{1,0:T(8,128)(2,1)S(1)}, bf16[512,1024]{1,0:T(8,128)(2,1)}, u32[]{:S(2)}, u32[]{:S(2)}) collective-permute-start(bf16[512,1024]{1,0:T(8,128)(2,1)S(1)} %broadcast_select_fusion.3.mine_ref), channel_id=1, source_target_pairs={{0,4},{4,0},{1,5},{5,1},{2,6},{6,2},{3,7},{7,3},{8,12},{12,8},{9,1... | collective-permute-start | bytes 3145736 | tf_op jit(solution)/shard_map/ppermute | solution.py:26
  646.2 38.7 %collective-permute-start.89 = (bf16[512,1024]{1,0:T(8,128)(2,1)}, bf16[512,1024]{1,0:T(8,128)(2,1)}, u32[]{:S(2)}, u32[]{:S(2)}) collective-permute-start(bf16[512,1024]{1,0:T(8,128)(2,1)} %add_convert_fusion), channel_id=1, source_target_pairs={{8,0},{16,24},{9,1},{17,25},{10,2},{18,26},{11,3},{19,27},{12,4},{... | collective-permute-start | bytes 3145736 | tf_op jit(solution)/shard_map/ppermute | solution.py:703
  672.4 42.0 %collective-permute-start.98 = (bf16[512,1024]{1,0:T(8,128)(2,1)}, bf16[512,1024]{1,0:T(8,128)(2,1)}, u32[]{:S(2)}, u32[]{:S(2)}) collective-permute-start(bf16[512,1024]{1,0:T(8,128)(2,1)} %broadcast_select_fusion.1.mine_ref), channel_id=1, source_target_pairs={{0,4},{4,0},{1,5},{5,1},{2,6},{6,2},{3,7},{7,3},{8,12},{12,8},{9,1... | collective-permute-start | bytes 3145736 | tf_op jit(solution)/shard_map/ppermute | solution.py:26
  707.3 50.1 %collective-permute-start.105 = (bf16[512,768]{1,0:T(8,128)(2,1)}, bf16[512,768]{1,0:T(8,128)(2,1)}, u32[]{:S(2)}, u32[]{:S(2)}) collective-permute-start(bf16[512,768]{1,0:T(8,128)(2,1)} %add_convert_fusion.13), channel_id=1, source_target_pairs={{0,8},{8,0},{16,24},{24,16},{1,9},{9,1},{17,25},{25,17},{2,10},{10... | collective-permute-start | bytes 2359304 | tf_op jit(solution)/shard_map/ppermute | solution.py:703
  714.4 39.3 %collective-permute-start.106 = (bf16[512,1024]{1,0:T(8,128)(2,1)S(1)}, bf16[512,1024]{1,0:T(8,128)(2,1)}, u32[]{:S(2)}, u32[]{:S(2)}) collective-permute-start(bf16[512,1024]{1,0:T(8,128)(2,1)S(1)} %broadcast_select_fusion.mine_ref), channel_id=1, source_target_pairs={{0,4},{4,0},{1,5},{5,1},{2,6},{6,2},{3,7},{7,3},{8,12},{12,8},{9,1... | collective-permute-start | bytes 3145736 | tf_op jit(solution)/shard_map/ppermute | solution.py:26
  722.2 36.8 %collective-permute-start.102 = (bf16[512,768]{1,0:T(8,128)(2,1)}, bf16[512,768]{1,0:T(8,128)(2,1)}, u32[]{:S(2)}, u32[]{:S(2)}) collective-permute-start(bf16[512,768]{1,0:T(8,128)(2,1)} %add_convert_fusion.12), channel_id=1, source_target_pairs={{0,8},{8,0},{16,24},{24,16},{1,9},{9,1},{17,25},{25,17},{2,10},{10... | collective-permute-start | bytes 2359304 | tf_op jit(solution)/shard_map/ppermute | solution.py:703
  734.4 36.2 %collective-permute-start.108 = (bf16[512,768]{1,0:T(8,128)(2,1)S(1)}, bf16[512,768]{1,0:T(8,128)(2,1)}, u32[]{:S(2)}, u32[]{:S(2)}) collective-permute-start(bf16[512,768]{1,0:T(8,128)(2,1)S(1)} %broadcast_select_fusion.8.mine_ref), channel_id=1, source_target_pairs={{0,4},{4,0},{1,5},{5,1},{2,6},{6,2},{3,7},{7,3},{8,12},{12,8},{9,1... | collective-permute-start | bytes 2359304 | tf_op jit(solution)/shard_map/ppermute | solution.py:26
  760.3 38.3 %collective-permute-start.104 = (bf16[512,768]{1,0:T(8,128)(2,1)S(1)}, bf16[512,768]{1,0:T(8,128)(2,1)}, u32[]{:S(2)}, u32[]{:S(2)}) collective-permute-start(bf16[512,768]{1,0:T(8,128)(2,1)S(1)} %broadcast_select_fusion.7.mine_ref), channel_id=1, source_target_pairs={{0,4},{4,0},{1,5},{5,1},{2,6},{6,2},{3,7},{7,3},{8,12},{12,8},{9,1... | collective-permute-start | bytes 2359304 | tf_op jit(solution)/shard_map/ppermute | solution.py:26
  (187 other events, 2614.0 us)

commit v8 on v7

--- a/solution.py
+++ b/solution.py
@@ -530,9 +530,11 @@
     swish = gate_proj * gate_sig
     inner_low = (swish * up_proj).astype(jnp.bfloat16)
     inner_low, hidden_rest = lax.optimization_barrier((inner_low, hidden_rest))
-    inner_halves = both_halves(inner_low)
+    inner_given = row_blocks(half_columns(inner_low, 1 - ctx_place), 2)
+    inner_first = flip(inner_given[0], "ctx", 1)
+    inner_second = flip(inner_given[1], "ctx", 1)
     ffn = to_owners(jnp.dot(inner_low, w_down, preferred_element_type=jnp.float32))
-    ffn, inner_halves = lax.optimization_barrier((ffn, inner_halves))
+    ffn, inner_first = lax.optimization_barrier((ffn, inner_first))
     inv_ffn = lax.rsqrt(jnp.mean(ffn * ffn, axis=1, keepdims=True) + EPS)
     ffn_unit = ffn * inv_ffn
     out_tokens = (hidden + ffn_unit * gain_ffn).astype(jnp.bfloat16)
@@ -544,7 +546,8 @@
     grad_out = cotangent.astype(jnp.float32) * picked
     gain_ffn_part = jnp.sum(grad_out * ffn_unit, axis=0)
     grad_ffn_low = norm_back(ffn_unit, inv_ffn, grad_out * gain_ffn).astype(jnp.bfloat16)
-    grad_ffn_own, grad_ffn_other, _ = gather_both(grad_ffn_low, "seq")
+    grad_ffn_own, grad_ffn_other, inner_second = gather_both(grad_ffn_low, "seq", inner_second)
+    inner_both = stacked([half_columns(inner_low, ctx_place), inner_first, inner_second])
     grad_ffn_both = stacked(grad_ffn_own + grad_ffn_other)
 
     grads = {
@@ -554,7 +557,7 @@
         "out": Gradients([w_out.shape], 1, 1, False),
         "in": Gradients([w_query.shape, w_key.shape, w_value.shape], 4, 1, False),
     }
-    sides = {"down": (stacked(inner_halves), grad_ffn_both)}
+    sides = {"down": (inner_both, grad_ffn_both)}
     results = {}
 
     def stages():

time: 809 us -> 804 us (level)
    ppermute x62 -> x63, waiting for transfers between devices: 193 us -> 187 us  [flip(): lax.ppermute(value, axis, [(place, place ^ distance) for place in range(c...]
    ppermute x62 -> x63, starting transfers between devices: 37.1 us -> 38.5 us  [flip(): lax.ppermute(value, axis, [(place, place ^ distance) for place in range(c...]
  transfers between devices with their start and end apart: 109 -> 110, of which waited for: 43 -> 44; matrix products, arithmetic and copies ran while one was open for 23% -> 23% of each run, Pallas kernels for 13% -> 13%
where the time goes in v8:
time: 804 us; the launch traced here: 797 us
  waiting for transfers between devices  280 us (35%)
  starting transfers between devices  141 us (18%)
  Pallas kernels  123 us (15%)
  matrix products  109 us (14%)
  other arithmetic  88.2 us (11%)
  local copies, waits for them, and re-layouts  33.5 us (4%)
  blocking collectives  18.6 us (2%)
    ppermute x63, waiting for transfers between devices, flip(): lax.ppermute(value, axis, [(place, place ^ distance) for place in range(c...  187 us
    pallas_call x17, Pallas kernels, store_chunk(): pl.pallas_call(functools.partial(store_kernel, outs=outs), grid_spec=pltp...  60.7 us
    dot_general x17, matrix products, contract_rows(): lax.dot_general(left, right, (((0,), (0,)), ((), ())), preferred_element_...  47.9 us
    ppermute x8, waiting for transfers between devices, body(): lax.ppermute(entering, 'dp', PAIRS if leaving is None else INWARD)  44.9 us
    ppermute x63, starting transfers between devices, flip(): lax.ppermute(value, axis, [(place, place ^ distance) for place in range(c...  38.5 us
    dot_general x7, matrix products, times_transpose(): lax.dot_general(left, right, (((1,), (1,)), ((), ())), preferred_element_...  38.3 us
    ppermute x9, starting transfers between devices, body(): got_in[tick] = got_out[tick - 2 * STEP] = lax.ppermute(leaving, 'dp', PAIRS)  37.5 us
    convert_element_type x18, other arithmetic, added(): (left.astype(jnp.float32) + right.astype(jnp.float32)).astype(left.dtype)  33.8 us
  transfers between devices with their start and end apart: 110, of which 44 were waited for; matrix products, arithmetic and copies ran while one was open for 23% of the time, Pallas kernels for 13%

profile of v8, /device:TPU:0, one launch (start us, length us, event | category | flops | bytes accessed | tf_op | source)
XLA Modules:
  0.0 797.1 jit_solution(6321986354634465878)
XLA Ops:
  5.3 10.5 %collective-permute-done.3.refs_0_ = bf16[128,2048]{1,0:T(8,128)(2,1)S(1)} collective-permute-done((bf16[128,2048]{1,0:T(8,128)(2,1)}, bf16[128,2048]{1,0:T(8,128)(2,1)S(1)}, u32[]{:S(2)}, u32[]{:S(2)}) %collective-permute-start.3) | collective-permute-done | bytes 524320 | tf_op jit(solution)/shard_map/ppermute | solution.py:26
  27.8 8.4 %project.2 = (bf16[512,2048]{1,0:T(8,128)(2,1)}, f32[512,512]{1,0:T(8,128)}, f32[512,512]{1,0:T(8,128)}, bf16[512,512]{1,0:T(8,128)(2,1)}, f32[512,1]{1,0:T(8,128)}, /*index=5*/f32[512,1]{1,0:T(8,128)}) custom-call(bf16[128,2048]{1,0:T(8,128)(2,1)} %refs_0_.1, bf16[128,2048]{1,0:T(8,128)(2,1)} %collective-permute-done.refs_1_, bf16[128,2048]{1,0:T(8,128)(2,1)} %copy-done.58, ...), custom_call_target="tpu_custom_call" | custom-call | tf_op jit(solution)/shard_map/project/pallas_call | solution.py:156
  56.2 11.8 %attend.1 = (bf16[512,512]{1,0:T(8,128)(2,1)}, bf16[1024,512]{1,0:T(8,128)(2,1)}, bf16[1024,512]{1,0:T(8,128)(2,1)}, bf16[512,512]{1,0:T(8,128)(2,1)}, f32[4,512,1]{2,1,0:T(8,128)}) custom-call(f32[512,512]{1,0:T(8,128)} %get-tuple-element.346.query_ref, f32[512,512]{1,0:T(8,128)} %get-tuple-element.347.key_ref, ...), custom_call_target="tpu_custom_call" | custom-call | tf_op jit(solution)/shard_map/attend/pallas_call | solution.py:264
  73.5 13.1 %collective-permute-done.10 = bf16[128,2048]{1,0:T(8,128)(2,1)S(1)} collective-permute-done((bf16[128,2048]{1,0:T(8,128)(2,1)S(1)}, bf16[128,2048]{1,0:T(8,128)(2,1)S(1)}, u32[]{:S(2)}, u32[]{:S(2)}) %collective-permute-start.10) | collective-permute-done | bytes 524320 | tf_op jit(solution)/shard_map/ppermute | solution.py:26
  89.3 11.1 %collective-permute-done.13 = bf16[128,2048]{1,0:T(8,128)(2,1)S(1)} collective-permute-done((bf16[128,2048]{1,0:T(8,128)(2,1)S(1)}, bf16[128,2048]{1,0:T(8,128)(2,1)S(1)}, u32[]{:S(2)}, u32[]{:S(2)}) %collective-permute-start.13) | collective-permute-done | bytes 524320 | tf_op jit(solution)/shard_map/ppermute | solution.py:26
  138.5 10.7 %collective-permute-done.21 = bf16[128,2048]{1,0:T(8,128)(2,1)S(1)} collective-permute-done((bf16[128,2048]{1,0:T(8,128)(2,1)S(1)}, bf16[128,2048]{1,0:T(8,128)(2,1)S(1)}, u32[]{:S(2)}, u32[]{:S(2)}) %collective-permute-start.21) | collective-permute-done | bytes 524320 | tf_op jit(solution)/shard_map/ppermute | solution.py:26
  187.3 11.4 %multiply_convert_fusion = (bf16[512,2048]{1,0:T(8,128)(2,1)S(1)}, bf16[512,2048]{1,0:T(8,128)(2,1)}) fusion(f32[512,2048]{1,0:T(8,128)} %copy-done.96, f32[512,2048]{1,0:T(8,128)} %get-tuple-element.727, bf16[512,2048]{1,0:T(8,128)(2,1)S(1)} %pad_maximum_fusion.2, bf16[2048,2048]{1,0:T(8,128)(2,1)} %param.29), kind=kOutput, calls=%fused_computation.5 | convolution fusion | flops 4308598784 | bytes 23068672 | tf_op jit(solution)/shard_map/dot_general | solution.py:108
  198.7 8.4 %fusion.65 = f32[512,2048]{1,0:T(8,128)S(1)} fusion(bf16[512,2048]{1,0:T(8,128)(2,1)} %get-tuple-element.381, bf16[2048,2048]{1,0:T(8,128)(2,1)} %param.27), kind=kOutput, calls=%fused_computation.216 | convolution fusion | flops 4294967296 | bytes 14680064 | tf_op jit(solution)/shard_map/dot_general | solution.py:108
  221.2 13.3 %collective-permute-done.32 = bf16[512,1024]{1,0:T(8,128)(2,1)} collective-permute-done((bf16[512,1024]{1,0:T(8,128)(2,1)S(1)}, bf16[512,1024]{1,0:T(8,128)(2,1)}, u32[]{:S(2)}, u32[]{:S(2)}) %collective-permute-start.32) | collective-permute-done | bytes 1048608 | tf_op jit(solution)/shard_map/ppermute | solution.py:704
  241.5 15.3 %collective-permute-done.36 = bf16[512,1024]{1,0:T(8,128)(2,1)S(1)} collective-permute-done((bf16[512,1024]{1,0:T(8,128)(2,1)S(1)}, bf16[512,1024]{1,0:T(8,128)(2,1)S(1)}, u32[]{:S(2)}, u32[]{:S(2)}) %collective-permute-start.36) | collective-permute-done | bytes 1048608 | tf_op jit(solution)/shard_map/ppermute | solution.py:704
  264.7 14.6 %collective-permute-done.33 = bf16[512,1024]{1,0:T(8,128)(2,1)S(1)} collective-permute-done((bf16[512,1024]{1,0:T(8,128)(2,1)S(1)}, bf16[512,1024]{1,0:T(8,128)(2,1)S(1)}, u32[]{:S(2)}, u32[]{:S(2)}) %collective-permute-start.33) | collective-permute-done | bytes 1048608 | tf_op jit(solution)/shard_map/ppermute | solution.py:704
  282.0 10.4 %collective-permute-done.39 = bf16[128,2048]{1,0:T(8,128)(2,1)S(1)} collective-permute-done((bf16[128,2048]{1,0:T(8,128)(2,1)S(1)}, bf16[128,2048]{1,0:T(8,128)(2,1)S(1)}, u32[]{:S(2)}, u32[]{:S(2)}) %collective-permute-start.39) | collective-permute-done | bytes 524320 | tf_op jit(solution)/shard_map/ppermute | solution.py:26
  316.5 8.8 %collective-permute-done.41.got_ref = bf16[512,1024]{1,0:T(8,128)(2,1)S(1)} collective-permute-done((bf16[512,1024]{1,0:T(8,128)(2,1)S(1)}, bf16[512,1024]{1,0:T(8,128)(2,1)S(1)}, u32[]{:S(2)}, u32[]{:S(2)}) %collective-permute-start.41) | collective-permute-done | bytes 1048608 | tf_op jit(solution)/shard_map/ppermute | solution.py:701
  335.3 11.0 %attend_back.1 = (f32[512,512]{1,0:T(8,128)}, f32[512,512]{1,0:T(8,128)}, f32[512,512]{1,0:T(8,128)}, bf16[512,512]{1,0:T(8,128)(2,1)}, bf16[512,512]{1,0:T(8,128)(2,1)}) custom-call(bf16[512,512]{1,0:T(8,128)(2,1)} %get-tuple-element.427.query_low_ref, bf16[1024,512]{1,0:T(8,128)(2,1)} %get-tuple-element.428.key_low_ref, ...), custom_call_target="tpu_custom_call" | custom-call | tf_op jit(solution)/shard_map/attend_back/pallas_call | solution.py:291
  371.5 11.1 %collective-permute-done.53 = bf16[512,512]{1,0:T(8,128)(2,1)S(1)} collective-permute-done((bf16[512,512]{1,0:T(8,128)(2,1)}, bf16[512,512]{1,0:T(8,128)(2,1)S(1)}, u32[]{:S(2)}, u32[]{:S(2)}) %collective-permute-start.53) | collective-permute-done | bytes 524320 | tf_op jit(solution)/shard_map/ppermute | solution.py:591
  390.8 11.1 %all-reduce = (f32[2,4,128]{2,0,1:T(2,128)S(1)}, f32[4096]{0:T(1024)S(1)}) all-reduce(f32[2,4,128]{2,0,1:T(2,128)S(1)} %select_bitcast_fusion.3, f32[4096]{0:T(1024)S(1)} %pad_maximum_fusion.9), channel_id=1, replica_groups=mesh['dp'=4,'ctx'=2,'seq'=4] {'seq'}, use_global_device_ids=true, to_apply=%region_8.11 | all-reduce | flops 5120 | bytes 40960 | tf_op jit(solution)/shard_map/psum | solution.py:604
  462.7 9.4 %collective-permute-done.66 = bf16[512,768]{1,0:T(8,128)(2,1)} collective-permute-done((bf16[512,768]{1,0:T(8,128)(2,1)S(1)}, bf16[512,768]{1,0:T(8,128)(2,1)}, u32[]{:S(2)}, u32[]{:S(2)}) %collective-permute-start.66) | collective-permute-done | bytes 786464 | tf_op jit(solution)/shard_map/ppermute | solution.py:26
  489.4 8.5 %collective-permute-done.65 = f32[40,128]{1,0:T(8,128)S(1)} collective-permute-done((f32[40,128]{1,0:T(8,128)S(1)}, f32[40,128]{1,0:T(8,128)S(1)}, u32[]{:S(2)}, u32[]{:S(2)}) %collective-permute-start.65) | collective-permute-done | bytes 20512 | tf_op jit(solution)/shard_map/ppermute | solution.py:639
  515.9 12.9 %collective-permute-start.77 = (bf16[512,1024]{1,0:T(8,128)(2,1)}, bf16[512,1024]{1,0:T(8,128)(2,1)S(1)}, u32[]{:S(2)}, u32[]{:S(2)}) collective-permute-start(bf16[512,1024]{1,0:T(8,128)(2,1)} %get-tuple-element.557), channel_id=1, source_target_pairs={{0,8},{8,0},{16,24},{24,16},{1,9},{9,1},{17,25},{25,17},{2,10},{10... | collective-permute-start | bytes 3145736 | tf_op jit(solution)/shard_map/ppermute | solution.py:701
  646.2 10.1 %collective-permute-done.92.theirs_ref = bf16[512,1024]{1,0:T(8,128)(2,1)} collective-permute-done((bf16[512,1024]{1,0:T(8,128)(2,1)S(1)}, bf16[512,1024]{1,0:T(8,128)(2,1)}, u32[]{:S(2)}, u32[]{:S(2)}) %collective-permute-start.92) | collective-permute-done | bytes 1048608 | tf_op jit(solution)/shard_map/ppermute | solution.py:26
  718.1 8.2 %collective-permute-done.104.theirs_ref = bf16[512,768]{1,0:T(8,128)(2,1)} collective-permute-done((bf16[512,768]{1,0:T(8,128)(2,1)S(1)}, bf16[512,768]{1,0:T(8,128)(2,1)}, u32[]{:S(2)}, u32[]{:S(2)}) %collective-permute-start.104) | collective-permute-done | bytes 786464 | tf_op jit(solution)/shard_map/ppermute | solution.py:26
  729.7 19.0 %collective-permute-done.107.theirs_ref = bf16[512,1024]{1,0:T(8,128)(2,1)} collective-permute-done((bf16[512,1024]{1,0:T(8,128)(2,1)S(1)}, bf16[512,1024]{1,0:T(8,128)(2,1)}, u32[]{:S(2)}, u32[]{:S(2)}) %collective-permute-start.107) | collective-permute-done | bytes 1048608 | tf_op jit(solution)/shard_map/ppermute | solution.py:26
  768.8 13.7 %collective-permute-done.108.theirs_ref = bf16[512,768]{1,0:T(8,128)(2,1)} collective-permute-done((bf16[512,768]{1,0:T(8,128)(2,1)S(1)}, bf16[512,768]{1,0:T(8,128)(2,1)}, u32[]{:S(2)}, u32[]{:S(2)}) %collective-permute-start.108) | collective-permute-done | bytes 786464 | tf_op jit(solution)/shard_map/ppermute | solution.py:26
  785.6 8.0 %collective-permute-done.105.theirs_ref = bf16[512,768]{1,0:T(8,128)(2,1)} collective-permute-done((bf16[512,768]{1,0:T(8,128)(2,1)S(1)}, bf16[512,768]{1,0:T(8,128)(2,1)}, u32[]{:S(2)}, u32[]{:S(2)}) %collective-permute-start.105) | collective-permute-done | bytes 786464 | tf_op jit(solution)/shard_map/ppermute | solution.py:26
  (599 shorter events, 522.9 us)
Async XLA Ops:
  210.4 46.4 %collective-permute-start.36 = (bf16[512,1024]{1,0:T(8,128)(2,1)S(1)}, bf16[512,1024]{1,0:T(8,128)(2,1)S(1)}, u32[]{:S(2)}, u32[]{:S(2)}) collective-permute-start(bf16[512,1024]{1,0:T(8,128)(2,1)S(1)} %copy-done.63), channel_id=1, source_target_pairs={{0,8},{8,0},{16,24},{24,16},{1,9},{9,1},{17,25},{25,17},{2,10},{10... | collective-permute-start | bytes 3145736 | tf_op jit(solution)/shard_map/ppermute | solution.py:704
  234.5 44.8 %collective-permute-start.33 = (bf16[512,1024]{1,0:T(8,128)(2,1)S(1)}, bf16[512,1024]{1,0:T(8,128)(2,1)S(1)}, u32[]{:S(2)}, u32[]{:S(2)}) collective-permute-start(bf16[512,1024]{1,0:T(8,128)(2,1)S(1)} %fusion.12), channel_id=1, source_target_pairs={{0,8},{8,0},{16,24},{24,16},{1,9},{9,1},{17,25},{25,17},{2,10},{10... | collective-permute-start | bytes 3145736 | tf_op jit(solution)/shard_map/ppermute | solution.py:704
  237.7 42.3 %collective-permute-start.35 = (bf16[512,1024]{1,0:T(8,128)(2,1)S(1)}, bf16[512,1024]{1,0:T(8,128)(2,1)S(1)}, u32[]{:S(2)}, u32[]{:S(2)}) collective-permute-start(bf16[512,1024]{1,0:T(8,128)(2,1)S(1)} %add_convert_fusion.11), channel_id=1, source_target_pairs={{8,16},{16,8},{9,17},{17,9},{10,18},{18,10},{11,19},{19,11},{12,20... | collective-permute-start | bytes 3145736 | tf_op jit(solution)/shard_map/ppermute | solution.py:697
  262.9 38.5 %collective-permute-start.43 = (bf16[512,1024]{1,0:T(8,128)(2,1)S(1)}, bf16[512,1024]{1,0:T(8,128)(2,1)S(1)}, u32[]{:S(2)}, u32[]{:S(2)}) collective-permute-start(bf16[512,1024]{1,0:T(8,128)(2,1)S(1)} %fusion.15), channel_id=1, source_target_pairs={{0,8},{8,0},{16,24},{24,16},{1,9},{9,1},{17,25},{25,17},{2,10},{10... | collective-permute-start | bytes 3145736 | tf_op jit(solution)/shard_map/ppermute | solution.py:704
  308.8 45.7 %collective-permute-start.50 = (bf16[512,1024]{1,0:T(8,128)(2,1)}, bf16[512,1024]{1,0:T(8,128)(2,1)}, u32[]{:S(2)}, u32[]{:S(2)}) collective-permute-start(bf16[512,1024]{1,0:T(8,128)(2,1)} %fusion.22.sent_ref), channel_id=1, source_target_pairs={{0,8},{8,0},{16,24},{24,16},{1,9},{9,1},{17,25},{25,17},{2,10},{10... | collective-permute-start | bytes 3145736 | tf_op jit(solution)/shard_map/ppermute | solution.py:701
  312.7 43.1 %collective-permute-start.51 = (bf16[512,1024]{1,0:T(8,128)(2,1)S(1)}, bf16[512,1024]{1,0:T(8,128)(2,1)}, u32[]{:S(2)}, u32[]{:S(2)}) collective-permute-start(bf16[512,1024]{1,0:T(8,128)(2,1)S(1)} %add_convert_fusion.7.pair_ref), channel_id=1, source_target_pairs={{8,16},{16,8},{9,17},{17,9},{10,18},{18,10},{11,19},{19,11},{12,20... | collective-permute-start | bytes 3145736 | tf_op jit(solution)/shard_map/ppermute | solution.py:697
  327.5 55.1 %collective-permute-start.54 = (bf16[512,1024]{1,0:T(8,128)(2,1)}, bf16[512,1024]{1,0:T(8,128)(2,1)}, u32[]{:S(2)}, u32[]{:S(2)}) collective-permute-start(bf16[512,1024]{1,0:T(8,128)(2,1)} %get-tuple-element.691), channel_id=1, source_target_pairs={{0,4},{4,0},{1,5},{5,1},{2,6},{6,2},{3,7},{7,3},{8,12},{12,8},{9,1... | collective-permute-start | bytes 3145736 | tf_op jit(solution)/shard_map/ppermute | solution.py:26
  346.3 40.8 %collective-permute-start.48 = (bf16[512,1024]{1,0:T(8,128)(2,1)}, bf16[512,1024]{1,0:T(8,128)(2,1)}, u32[]{:S(2)}, u32[]{:S(2)}) collective-permute-start(bf16[512,1024]{1,0:T(8,128)(2,1)} %get-tuple-element.438.sent_ref), channel_id=1, source_target_pairs={{0,8},{8,0},{16,24},{24,16},{1,9},{9,1},{17,25},{25,17},{2,10},{10... | collective-permute-start | bytes 3145736 | tf_op jit(solution)/shard_map/ppermute | solution.py:701
  371.5 57.8 %collective-permute-start.59 = (bf16[512,1024]{1,0:T(8,128)(2,1)}, bf16[512,1024]{1,0:T(8,128)(2,1)}, u32[]{:S(2)}, u32[]{:S(2)}) collective-permute-start(bf16[512,1024]{1,0:T(8,128)(2,1)} %get-tuple-element.480.mine_ref), channel_id=1, source_target_pairs={{0,4},{4,0},{1,5},{5,1},{2,6},{6,2},{3,7},{7,3},{8,12},{12,8},{9,1... | collective-permute-start | bytes 3145736 | tf_op jit(solution)/shard_map/ppermute | solution.py:26
  416.0 39.1 %collective-permute-start.60 = (bf16[512,1024]{1,0:T(8,128)(2,1)}, bf16[512,1024]{1,0:T(8,128)(2,1)}, u32[]{:S(2)}, u32[]{:S(2)}) collective-permute-start(bf16[512,1024]{1,0:T(8,128)(2,1)} %get-tuple-element.486.mine_ref), channel_id=1, source_target_pairs={{0,4},{4,0},{1,5},{5,1},{2,6},{6,2},{3,7},{7,3},{8,12},{12,8},{9,1... | collective-permute-start | bytes 3145736 | tf_op jit(solution)/shard_map/ppermute | solution.py:26
  486.3 42.6 %collective-permute-start.72 = (bf16[512,1024]{1,0:T(8,128)(2,1)}, bf16[512,1024]{1,0:T(8,128)(2,1)}, u32[]{:S(2)}, u32[]{:S(2)}) collective-permute-start(bf16[512,1024]{1,0:T(8,128)(2,1)} %get-tuple-element.532.mine_ref), channel_id=1, source_target_pairs={{0,4},{4,0},{1,5},{5,1},{2,6},{6,2},{3,7},{7,3},{8,12},{12,8},{9,1... | collective-permute-start | bytes 3145736 | tf_op jit(solution)/shard_map/ppermute | solution.py:26
  497.8 38.7 %collective-permute-start.67 = (bf16[512,1024]{1,0:T(8,128)(2,1)}, bf16[512,1024]{1,0:T(8,128)(2,1)}, u32[]{:S(2)}, u32[]{:S(2)}) collective-permute-start(bf16[512,1024]{1,0:T(8,128)(2,1)} %get-tuple-element.513.sent_ref), channel_id=1, source_target_pairs={{0,8},{8,0},{16,24},{24,16},{1,9},{9,1},{17,25},{25,17},{2,10},{10... | collective-permute-start | bytes 3145736 | tf_op jit(solution)/shard_map/ppermute | solution.py:701
  502.0 41.7 %collective-permute-start.68 = (bf16[512,1024]{1,0:T(8,128)(2,1)}, bf16[512,1024]{1,0:T(8,128)(2,1)}, u32[]{:S(2)}, u32[]{:S(2)}) collective-permute-start(bf16[512,1024]{1,0:T(8,128)(2,1)} %get-tuple-element.514.pair_ref), channel_id=1, source_target_pairs={{8,16},{16,8},{9,17},{17,9},{10,18},{18,10},{11,19},{19,11},{12,20... | collective-permute-start | bytes 3145736 | tf_op jit(solution)/shard_map/ppermute | solution.py:697
  504.3 48.2 %collective-permute-start.79 = (bf16[512,1024]{1,0:T(8,128)(2,1)}, bf16[512,1024]{1,0:T(8,128)(2,1)}, u32[]{:S(2)}, u32[]{:S(2)}) collective-permute-start(bf16[512,1024]{1,0:T(8,128)(2,1)} %get-tuple-element.561.mine_ref), channel_id=1, source_target_pairs={{0,4},{4,0},{1,5},{5,1},{2,6},{6,2},{3,7},{7,3},{8,12},{12,8},{9,1... | collective-permute-start | bytes 3145736 | tf_op jit(solution)/shard_map/ppermute | solution.py:26
  515.9 45.7 %collective-permute-start.77 = (bf16[512,1024]{1,0:T(8,128)(2,1)}, bf16[512,1024]{1,0:T(8,128)(2,1)S(1)}, u32[]{:S(2)}, u32[]{:S(2)}) collective-permute-start(bf16[512,1024]{1,0:T(8,128)(2,1)} %get-tuple-element.557), channel_id=1, source_target_pairs={{0,8},{8,0},{16,24},{24,16},{1,9},{9,1},{17,25},{25,17},{2,10},{10... | collective-permute-start | bytes 3145736 | tf_op jit(solution)/shard_map/ppermute | solution.py:701
  562.6 42.7 %collective-permute-start.84 = (bf16[512,768]{1,0:T(8,128)(2,1)}, bf16[512,768]{1,0:T(8,128)(2,1)}, u32[]{:S(2)}, u32[]{:S(2)}) collective-permute-start(bf16[512,768]{1,0:T(8,128)(2,1)} %convolution_convert_fusion.12), channel_id=1, source_target_pairs={{0,8},{24,16},{1,9},{25,17},{2,10},{26,18},{3,11},{27,19},{4,12},{... | collective-permute-start | bytes 2359304 | tf_op jit(solution)/shard_map/ppermute | solution.py:704
  618.8 37.5 %collective-permute-start.92 = (bf16[512,1024]{1,0:T(8,128)(2,1)S(1)}, bf16[512,1024]{1,0:T(8,128)(2,1)}, u32[]{:S(2)}, u32[]{:S(2)}) collective-permute-start(bf16[512,1024]{1,0:T(8,128)(2,1)S(1)} %broadcast_select_fusion.3.mine_ref), channel_id=1, source_target_pairs={{0,4},{4,0},{1,5},{5,1},{2,6},{6,2},{3,7},{7,3},{8,12},{12,8},{9,1... | collective-permute-start | bytes 3145736 | tf_op jit(solution)/shard_map/ppermute | solution.py:26
  641.2 38.6 %collective-permute-start.90 = (bf16[512,1024]{1,0:T(8,128)(2,1)}, bf16[512,1024]{1,0:T(8,128)(2,1)}, u32[]{:S(2)}, u32[]{:S(2)}) collective-permute-start(bf16[512,1024]{1,0:T(8,128)(2,1)} %add_convert_fusion), channel_id=1, source_target_pairs={{8,0},{16,24},{9,1},{17,25},{10,2},{18,26},{11,3},{19,27},{12,4},{... | collective-permute-start | bytes 3145736 | tf_op jit(solution)/shard_map/ppermute | solution.py:706
  667.4 42.0 %collective-permute-start.99 = (bf16[512,1024]{1,0:T(8,128)(2,1)}, bf16[512,1024]{1,0:T(8,128)(2,1)}, u32[]{:S(2)}, u32[]{:S(2)}) collective-permute-start(bf16[512,1024]{1,0:T(8,128)(2,1)} %broadcast_select_fusion.1.mine_ref), channel_id=1, source_target_pairs={{0,4},{4,0},{1,5},{5,1},{2,6},{6,2},{3,7},{7,3},{8,12},{12,8},{9,1... | collective-permute-start | bytes 3145736 | tf_op jit(solution)/shard_map/ppermute | solution.py:26
  702.3 50.2 %collective-permute-start.106 = (bf16[512,768]{1,0:T(8,128)(2,1)}, bf16[512,768]{1,0:T(8,128)(2,1)}, u32[]{:S(2)}, u32[]{:S(2)}) collective-permute-start(bf16[512,768]{1,0:T(8,128)(2,1)} %add_convert_fusion.13), channel_id=1, source_target_pairs={{0,8},{8,0},{16,24},{24,16},{1,9},{9,1},{17,25},{25,17},{2,10},{10... | collective-permute-start | bytes 2359304 | tf_op jit(solution)/shard_map/ppermute | solution.py:706
  709.5 39.3 %collective-permute-start.107 = (bf16[512,1024]{1,0:T(8,128)(2,1)S(1)}, bf16[512,1024]{1,0:T(8,128)(2,1)}, u32[]{:S(2)}, u32[]{:S(2)}) collective-permute-start(bf16[512,1024]{1,0:T(8,128)(2,1)S(1)} %broadcast_select_fusion.mine_ref), channel_id=1, source_target_pairs={{0,4},{4,0},{1,5},{5,1},{2,6},{6,2},{3,7},{7,3},{8,12},{12,8},{9,1... | collective-permute-start | bytes 3145736 | tf_op jit(solution)/shard_map/ppermute | solution.py:26
  717.2 36.9 %collective-permute-start.103 = (bf16[512,768]{1,0:T(8,128)(2,1)}, bf16[512,768]{1,0:T(8,128)(2,1)}, u32[]{:S(2)}, u32[]{:S(2)}) collective-permute-start(bf16[512,768]{1,0:T(8,128)(2,1)} %add_convert_fusion.12), channel_id=1, source_target_pairs={{0,8},{8,0},{16,24},{24,16},{1,9},{9,1},{17,25},{25,17},{2,10},{10... | collective-permute-start | bytes 2359304 | tf_op jit(solution)/shard_map/ppermute | solution.py:706
  729.4 36.2 %collective-permute-start.109 = (bf16[512,768]{1,0:T(8,128)(2,1)S(1)}, bf16[512,768]{1,0:T(8,128)(2,1)}, u32[]{:S(2)}, u32[]{:S(2)}) collective-permute-start(bf16[512,768]{1,0:T(8,128)(2,1)S(1)} %broadcast_select_fusion.8.mine_ref), channel_id=1, source_target_pairs={{0,4},{4,0},{1,5},{5,1},{2,6},{6,2},{3,7},{7,3},{8,12},{12,8},{9,1... | collective-permute-start | bytes 2359304 | tf_op jit(solution)/shard_map/ppermute | solution.py:26
  755.3 38.3 %collective-permute-start.105 = (bf16[512,768]{1,0:T(8,128)(2,1)S(1)}, bf16[512,768]{1,0:T(8,128)(2,1)}, u32[]{:S(2)}, u32[]{:S(2)}) collective-permute-start(bf16[512,768]{1,0:T(8,128)(2,1)S(1)} %broadcast_select_fusion.7.mine_ref), channel_id=1, source_target_pairs={{0,4},{4,0},{1,5},{5,1},{2,6},{6,2},{3,7},{7,3},{8,12},{12,8},{9,1... | collective-permute-start | bytes 2359304 | tf_op jit(solution)/shard_map/ppermute | solution.py:26
  (187 other events, 2600.7 us)
